TPU v7x, 256 devices: a whole 4x4x8 slice. The times are simulated.
256 devices in a mesh: prog: 32 (over z, x), clus: 8 (over y, core).
Axes of the slice: x: 4, y: 4, z: 8, core: 2. Of those that a mesh axis runs over, the one named last changes fastest.
Arguments:
- embeddings: bfloat16 [32768, 2048], P('prog', 'clus'), may hold values from -64 to 64, as said below
- centroids: bfloat16 [4096, 2048], P('clus'), may hold values from -6 to 6, as said below
- plan_grad: bfloat16 [32768, 4096], P('prog', 'clus'), may hold values from -24 to 24
Outputs:
- embed_grad: bfloat16 [32768, 2048], P('prog', 'clus')
- centroid_grad: bfloat16 [4096, 2048], P(('clus', 'prog'))
Inputs may be any that keep to these rules, and one draw needn't show every extreme that they name: embeddings are real-valued with full-rank spread. centroids are real-valued with full-rank spread.
All inputs are finite; a program needn't handle non-finite values.
Results may differ from a plain program's by a relative error of at most 0.006.
Values may be sent and summed in bfloat16 or wider, within the bound.
No kernel may reach another device: no remote copies, remote signals or barrier semaphores. Data moves between devices by JAX's collectives and lax.ppermute only.
A program may use at most 64 MiB of HBM per device.

v0:
```python
import jax
import jax.numpy as jnp
from jax import lax
from jax.sharding import PartitionSpec as P

D = 2048
CENTROIDS = 4096
ITERS = 4


def row_lse(values):
    top = lax.pmax(jnp.max(values, axis=1), "clus")
    total = lax.psum(jnp.sum(jnp.exp(values - top[:, None]), axis=1), "clus")
    return top + jnp.log(total)


def col_lse(values):
    top = lax.pmax(jnp.max(values, axis=0), "prog")
    total = lax.psum(jnp.sum(jnp.exp(values - top[None, :]), axis=0), "prog")
    return top + jnp.log(total)


def shards(embeddings, centroids, plan_grad):
    scale = 1.0 / (0.25 * jnp.sqrt(jnp.float32(D)))
    whole_rows = lax.all_gather(embeddings, "clus", axis=1, tiled=True)
    logits = scale * lax.dot_general(
        whole_rows, centroids, (((1,), (1,)), ((), ())), preferred_element_type=jnp.float32
    )
    total_rows = embeddings.shape[0] * lax.axis_size("prog")
    log_b = jnp.log(jnp.float32(total_rows) / jnp.float32(CENTROIDS))
    col_pot = jnp.zeros((centroids.shape[0],), jnp.float32)
    row_list = []
    col_list = []
    for step in range(ITERS):
        row_pot = -row_lse(logits + col_pot[None, :])
        col_pot = log_b - col_lse(logits + row_pot[:, None])
        row_list.append(row_pot)
        col_list.append(col_pot)
    plan = jnp.exp(logits + row_list[-1][:, None] + col_list[-1][None, :])
    pbar = plan_grad.astype(jnp.float32) * plan
    adjoint = pbar
    col_adj = lax.psum(jnp.sum(pbar, axis=0), "prog")
    direct = jnp.sum(pbar, axis=1)
    for step in range(ITERS - 1, -1, -1):
        weights_a = jnp.exp(logits + row_list[step][:, None] + col_list[step][None, :] - log_b)
        term_a = weights_a * col_adj[None, :]
        adjoint = adjoint - term_a
        row_adj = lax.psum(direct - jnp.sum(term_a, axis=1), "clus")
        direct = jnp.zeros_like(direct)
        if step > 0:
            prev_col = col_list[step - 1]
        else:
            prev_col = jnp.zeros_like(col_pot)
        term_b = jnp.exp(logits + prev_col[None, :] + row_list[step][:, None]) * row_adj[:, None]
        adjoint = adjoint - term_b
        if step > 0:
            col_adj = -lax.psum(jnp.sum(term_b, axis=0), "prog")
    adjoint_b = adjoint.astype(jnp.bfloat16)
    partial_rows = scale * jnp.dot(adjoint_b, centroids, preferred_element_type=jnp.float32)
    embed_grad = lax.psum_scatter(partial_rows, "clus", scatter_dimension=1, tiled=True).astype(
        jnp.bfloat16
    )
    centroid_grad = lax.psum_scatter(
        scale
        * lax.dot_general(
            adjoint_b, whole_rows, (((0,), (0,)), ((), ())), preferred_element_type=jnp.float32
        ),
        "prog",
        scatter_dimension=0,
        tiled=True,
    ).astype(jnp.bfloat16)
    return (embed_grad, centroid_grad)


def solution(mesh):
    placed = (P("prog", "clus"), P("clus", None), P("prog", "clus"))
    return jax.shard_map(
        shards,
        mesh=mesh,
        in_specs=placed,
        out_specs=(P("prog", "clus"), P(("clus", "prog"), None)),
        check_vma=False,
    )
```

profile of v0, /device:TPU:1, one launch (start us, length us, event | category | flops | bytes accessed | tf_op | source)
XLA Modules:
  0.0 1400.4 jit_solution(5728778426446037416)
XLA Ops:
  9.5 42.7 %all-gather.2.cloned.1.call-done = bf16[1024,2048]{1,0:T(8,128)(2,1)} async-done(((bf16[1024,256]{1,0:T(8,128)(2,1)}), bf16[1024,2048]{1,0:T(8,128)(2,1)}) %all-gather.2.cloned.1.call-update) | async-done | bytes 4194320 | tf_op jit(solution)/shard_map/all_gather | solution.py:25
  52.1 5.9 fusion.9
  58.0 12.0 pmax.56
  70.0 1.9 exponential_reduce_fusion.7
  71.9 14.3 %psum.112 = f32[1024]{0:T(1024)S(1)} all-reduce(f32[1024]{0:T(1024)S(1)} %exponential_reduce_fusion.7), channel_id=1, replica_groups=mesh['prog'=32,'clus'=8] {'clus'}, use_global_device_ids=true, to_apply=%region_3.0 | all-reduce | flops 1024 | bytes 8192 | tf_op jit(solution)/shard_map/psum | solution.py:13
  88.1 60.9 %pmax.57 = f32[512]{0:T(512)S(1)} all-reduce(f32[512]{0:T(512)S(1)} %add_reduce_fusion.6), channel_id=1, replica_groups=mesh['prog'=32,'clus'=8] {'prog'}, use_global_device_ids=true, to_apply=%region_5.0 | all-reduce | flops 512 | bytes 4096 | tf_op jit(solution)/shard_map/pmax | solution.py:18
  148.9 2.1 exponential_reduce_fusion.6
  151.0 56.1 %psum.113 = f32[512]{0:T(512)S(1)} all-reduce(f32[512]{0:T(512)S(1)} %exponential_reduce_fusion.6), channel_id=1, replica_groups=mesh['prog'=32,'clus'=8] {'prog'}, use_global_device_ids=true, to_apply=%region_7.0 | all-reduce | flops 512 | bytes 4096 | tf_op jit(solution)/shard_map/psum | solution.py:19
  208.9 40.2 %pmax.58 = f32[1024]{0:T(1024)S(1)} all-reduce(f32[1024]{0:T(1024)S(1)} %add_reduce_fusion.4), channel_id=1, replica_groups=mesh['prog'=32,'clus'=8] {'clus'}, use_global_device_ids=true, to_apply=%region_9.0 | all-reduce | flops 1024 | bytes 8192 | tf_op jit(solution)/shard_map/pmax | solution.py:12
  249.1 2.0 exponential_reduce_fusion.5
  251.1 12.4 psum.114
  265.4 57.4 %pmax.59 = f32[512]{0:T(512)S(1)} all-reduce(f32[512]{0:T(512)S(1)} %add_reduce_fusion.3), channel_id=1, replica_groups=mesh['prog'=32,'clus'=8] {'prog'}, use_global_device_ids=true, to_apply=%region_13.0 | all-reduce | flops 512 | bytes 4096 | tf_op jit(solution)/shard_map/pmax | solution.py:18
  322.8 2.1 exponential_reduce_fusion.4
  324.9 56.1 %psum.115 = f32[512]{0:T(512)S(1)} all-reduce(f32[512]{0:T(512)S(1)} %exponential_reduce_fusion.4), channel_id=1, replica_groups=mesh['prog'=32,'clus'=8] {'prog'}, use_global_device_ids=true, to_apply=%region_15.0 | all-reduce | flops 512 | bytes 4096 | tf_op jit(solution)/shard_map/psum | solution.py:19
  382.9 40.1 %pmax.60 = f32[1024]{0:T(1024)S(1)} all-reduce(f32[1024]{0:T(1024)S(1)} %add_reduce_fusion.2), channel_id=1, replica_groups=mesh['prog'=32,'clus'=8] {'clus'}, use_global_device_ids=true, to_apply=%region_17.0 | all-reduce | flops 1024 | bytes 8192 | tf_op jit(solution)/shard_map/pmax | solution.py:12
  423.0 2.0 exponential_reduce_fusion.3
  425.0 12.4 psum.116
  439.2 57.4 %pmax.61 = f32[512]{0:T(512)S(1)} all-reduce(f32[512]{0:T(512)S(1)} %add_reduce_fusion.1), channel_id=1, replica_groups=mesh['prog'=32,'clus'=8] {'prog'}, use_global_device_ids=true, to_apply=%region_21.0 | all-reduce | flops 512 | bytes 4096 | tf_op jit(solution)/shard_map/pmax | solution.py:18
  496.7 2.1 exponential_reduce_fusion.2
  498.8 56.1 %psum.117 = f32[512]{0:T(512)S(1)} all-reduce(f32[512]{0:T(512)S(1)} %exponential_reduce_fusion.2), channel_id=1, replica_groups=mesh['prog'=32,'clus'=8] {'prog'}, use_global_device_ids=true, to_apply=%region_23.0 | all-reduce | flops 512 | bytes 4096 | tf_op jit(solution)/shard_map/psum | solution.py:19
  556.7 40.1 %pmax.62 = f32[1024]{0:T(1024)S(1)} all-reduce(f32[1024]{0:T(1024)S(1)} %add_reduce_fusion), channel_id=1, replica_groups=mesh['prog'=32,'clus'=8] {'clus'}, use_global_device_ids=true, to_apply=%region_25.0 | all-reduce | flops 1024 | bytes 8192 | tf_op jit(solution)/shard_map/pmax | solution.py:12
  596.8 2.0 exponential_reduce_fusion.1
  598.9 12.4 psum.118
  613.1 57.4 %pmax.63 = f32[512]{0:T(512)S(1)} all-reduce(f32[512]{0:T(512)S(1)} %add_reduce_fusion.5), channel_id=1, replica_groups=mesh['prog'=32,'clus'=8] {'prog'}, use_global_device_ids=true, to_apply=%region_29.0 | all-reduce | flops 512 | bytes 4096 | tf_op jit(solution)/shard_map/pmax | solution.py:18
  670.5 2.1 exponential_reduce_fusion
  672.6 56.2 %psum.119 = f32[512]{0:T(512)S(1)} all-reduce(f32[512]{0:T(512)S(1)} %exponential_reduce_fusion), channel_id=1, replica_groups=mesh['prog'=32,'clus'=8] {'prog'}, use_global_device_ids=true, to_apply=%region_31.0 | all-reduce | flops 512 | bytes 4096 | tf_op jit(solution)/shard_map/psum | solution.py:19
  728.8 2.3 fusion.8
  731.1 57.0 %psum.120 = f32[512]{0:T(512)S(1)} all-reduce(f32[512]{0:T(512)S(1)} %get-tuple-element.2), channel_id=1, replica_groups=mesh['prog'=32,'clus'=8] {'prog'}, use_global_device_ids=true, to_apply=%region_33.0 | all-reduce | flops 512 | bytes 4096 | tf_op jit(solution)/shard_map/psum | solution.py:42
  788.1 2.1 fusion.4
  790.3 54.7 %psum.121 = f32[1024]{0:T(1024)S(1)} all-reduce(f32[1024]{0:T(1024)S(1)} %sub.146), channel_id=1, replica_groups=mesh['prog'=32,'clus'=8] {'clus'}, use_global_device_ids=true, to_apply=%region_36.0 | all-reduce | flops 1024 | bytes 8192 | tf_op jit(solution)/shard_map/psum | solution.py:48
  845.0 2.2 fusion.1
  847.1 55.9 %psum.122 = f32[512]{0:T(512)S(1)} all-reduce(f32[512]{0:T(512)S(1)} %fusion.1), channel_id=1, replica_groups=mesh['prog'=32,'clus'=8] {'prog'}, use_global_device_ids=true, to_apply=%region_38.0 | all-reduce | flops 512 | bytes 4096 | tf_op jit(solution)/shard_map/psum | solution.py:57
  903.0 2.1 fusion.5
  905.2 26.4 %psum.123 = f32[1024]{0:T(1024)S(1)} all-reduce(f32[1024]{0:T(1024)S(1)} %broadcast_subtract_fusion.2), channel_id=1, replica_groups=mesh['prog'=32,'clus'=8] {'clus'}, use_global_device_ids=true, to_apply=%region_40.0 | all-reduce | flops 1024 | bytes 8192 | tf_op jit(solution)/shard_map/psum | solution.py:48
  931.6 2.2 fusion.2
  933.7 57.4 %psum.124 = f32[512]{0:T(512)S(1)} all-reduce(f32[512]{0:T(512)S(1)} %fusion.2), channel_id=1, replica_groups=mesh['prog'=32,'clus'=8] {'prog'}, use_global_device_ids=true, to_apply=%region_42.0 | all-reduce | flops 512 | bytes 4096 | tf_op jit(solution)/shard_map/psum | solution.py:57
  991.2 2.1 fusion.6
  993.3 26.6 %psum.125 = f32[1024]{0:T(1024)S(1)} all-reduce(f32[1024]{0:T(1024)S(1)} %broadcast_subtract_fusion.1), channel_id=1, replica_groups=mesh['prog'=32,'clus'=8] {'clus'}, use_global_device_ids=true, to_apply=%region_44.0 | all-reduce | flops 1024 | bytes 8192 | tf_op jit(solution)/shard_map/psum | solution.py:48
  1019.9 2.2 fusion.3
  1022.1 55.7 %psum.126 = f32[512]{0:T(512)S(1)} all-reduce(f32[512]{0:T(512)S(1)} %fusion.3), channel_id=1, replica_groups=mesh['prog'=32,'clus'=8] {'prog'}, use_global_device_ids=true, to_apply=%region_46.0 | all-reduce | flops 512 | bytes 4096 | tf_op jit(solution)/shard_map/psum | solution.py:57
  1077.8 2.1 fusion
  1080.0 26.4 %psum.127 = f32[1024]{0:T(1024)S(1)} all-reduce(f32[1024]{0:T(1024)S(1)} %broadcast_subtract_fusion), channel_id=1, replica_groups=mesh['prog'=32,'clus'=8] {'clus'}, use_global_device_ids=true, to_apply=%region_48.0 | all-reduce | flops 1024 | bytes 8192 | tf_op jit(solution)/shard_map/psum | solution.py:48
  1106.4 6.2 subtract_convert_fusion
  1113.6 4.3 convolution_multiply_fusion.1
  1119.2 5.6 convolution_multiply_fusion
  1124.8 206.5 %reduce-scatter.5.cloned.1.call-done = f32[16,2048]{1,0:T(8,128)} async-done(((f32[512,2048]{1,0:T(8,128)}), f32[16,2048]{1,0:T(8,128)}) %reduce-scatter.5.cloned.1.call-update) | async-done | bytes 131088 | tf_op jit(solution)/shard_map/reduce_scatter | solution.py:63
  1332.8 59.0 %reduce-scatter.3.cloned.1.call-done = f32[1024,256]{1,0:T(8,128)} async-done(((f32[1024,2048]{1,0:T(8,128)}), f32[1024,256]{1,0:T(8,128)}) %reduce-scatter.3.cloned.1.call-update) | async-done | bytes 1048592 | tf_op jit(solution)/shard_map/reduce_scatter | solution.py:60
  1391.8 2.1 convert_element_type.14
  (38 shorter events, 18.8 us)
Async XLA Ops:
  7.2 45.0 %copy-start = (bf16[512,2048]{1,0:T(8,128)(2,1)S(1)}, bf16[512,2048]{1,0:T(8,128)(2,1)}, u32[]{:S(2)}) copy-start(bf16[512,2048]{1,0:T(8,128)(2,1)} %param.4) | copy-start | bytes 6291460
  7.2 45.0 %all-gather.2.cloned.1.call-start = ((), (), s32[]{:S(2)}) async-start(), calls=%async_computation.2 | async-start | bytes 4718592 | tf_op jit(solution)/shard_map/all_gather | solution.py:25
  7.9 1323.4 %reduce-scatter.5.cloned.1.call-start = ((), (), s32[]{:S(2)}) async-start(), calls=%async_computation.4 | async-start | bytes 4325376 | tf_op jit(solution)/shard_map/reduce_scatter | solution.py:63
  1106.4 7.2 copy-start.1
  1112.6 1.0 copy-start.2
  1117.9 1.2 copy-start.3
  1118.0 273.8 %reduce-scatter.3.cloned.1.call-start = ((), (), s32[]{:S(2)}) async-start(), calls=%async_computation.3 | async-start | bytes 9437184 | tf_op jit(solution)/shard_map/reduce_scatter | solution.py:60
Sparse Core Ops, SparseCore 0:
  9.8 42.2 all-gather.1
  1118.1 213.1 reduce-scatter.4
  1333.8 57.9 reduce-scatter.2
where the time goes:
time: 1400 us
  blocking collectives  1000 us (71%)
  waiting for transfers between devices  309 us (22%)
  other arithmetic  56.3 us (4%)
  matrix products  15.8 us (1%)
    pmax x4, blocking collectives, col_lse(): top = lax.pmax(jnp.max(values, axis=0), 'prog')  233 us
    psum x4, blocking collectives, col_lse(): total = lax.psum(jnp.sum(jnp.exp(values - top[None, :]), axis=0), 'prog')  225 us
    reduce_scatter x1, waiting for transfers between devices, shards(): lax.psum_scatter(scale * lax.dot_general(adjoint_b, whole_rows, (((0,), (...  206 us
    psum x3, blocking collectives, shards(): col_adj = -lax.psum(jnp.sum(term_b, axis=0), 'prog')  169 us
    psum x4, blocking collectives, shards(): row_adj = lax.psum(direct - jnp.sum(term_a, axis=1), 'clus')  134 us
    pmax x4, blocking collectives, row_lse(): top = lax.pmax(jnp.max(values, axis=1), 'clus')  132 us
    reduce_scatter x1, waiting for transfers between devices, shards(): lax.psum_scatter(partial_rows, 'clus', scatter_dimension=1, tiled=True)  59 us
    psum x1, blocking collectives, shards(): col_adj = lax.psum(jnp.sum(pbar, axis=0), 'prog')  57 us
  transfers between devices with their start and end apart: 3, of which 3 were waited for; matrix products, arithmetic and copies ran while one was open for 1% of the time, Pallas kernels for 0%

commit v1 on v0

v1 whole, which is shorter than its diff:
```python
import functools
import math

import jax
import jax.numpy as jnp
from jax import lax
from jax.experimental import pallas as pl
from jax.experimental.pallas import tpu as pltpu
from jax.sharding import Mesh
from jax.sharding import PartitionSpec as P

ITERS = 4
L = 128
F32 = jnp.float32
BF16 = jnp.bfloat16
NT = (((1,), (1,)), ((), ()))
NN = (((1,), (0,)), ((), ()))
TN = (((0,), (0,)), ((), ()))
SMALL = 12 << 20
LARGE = 40 << 20


def spread(vec):
    parts = [jnp.broadcast_to(vec[q : q + 1, :], (L, L)).T for q in range(vec.shape[0])]
    return jnp.concatenate(parts, axis=0)


def put_rows(out, parts):
    whole = jnp.concatenate(parts, axis=0)
    out[...] = jnp.broadcast_to(whole[None], out.shape)


def row_sums(values):
    return [jnp.sum(v, axis=0, keepdims=True) for v in values]


def gather_cols(part):
    return jnp.concatenate(
        [
            jnp.sum(part[q * L : (q + 1) * L, :].T, axis=0, keepdims=True)
            for q in range(part.shape[0] // L)
        ],
        axis=0,
    )


def first_lane(part):
    return jnp.concatenate(
        [part[q * L : (q + 1) * L, :].T[0:1, :] for q in range(part.shape[0] // L)], axis=0
    )


def lanes(ref, r):
    return ref[:, r * L : (r + 1) * L]


def total(recv):
    return jnp.sum(recv[...], axis=0)


def merge(recv):
    tops = recv[:, 0]
    top = jnp.max(tops, axis=0)
    return top + jnp.log(jnp.sum(recv[:, 1] * jnp.exp(tops - top[None]), axis=0))


def k_logits(scale, where, cent, *refs):
    n = len(refs) - 3
    pieces, (whole, logits, send) = refs[:n], refs[n:]
    width = pieces[0].shape[1]
    for k in range(n):
        whole[:, pl.ds(pl.multiple_of(where[k] * width, L), width)] = pieces[k][...]
    logits[...] = scale * lax.dot_general(cent[...], whole[...], NT, preferred_element_type=F32)
    count = logits.shape[1] // L
    tops, sums = [], []
    for r in range(count):
        tile = lanes(logits, r)
        top = jnp.max(tile, axis=0, keepdims=True)
        tops.append(top)
        sums.append(jnp.sum(jnp.exp(tile - top), axis=0, keepdims=True))
    send[:, 0] = jnp.broadcast_to(jnp.concatenate(tops, axis=0)[None], send[:, 0].shape)
    send[:, 1] = jnp.broadcast_to(jnp.concatenate(sums, axis=0)[None], send[:, 1].shape)


def k_first_col(logits, recv, row_pot, send):
    u = -merge(recv)
    row_pot[...] = u
    count = u.shape[0]
    top = lanes(logits, 0) + u[0:1, :]
    for r in range(1, count):
        top = jnp.maximum(top, lanes(logits, r) + u[r : r + 1, :])
    top = jnp.broadcast_to(jnp.max(top, axis=1, keepdims=True), top.shape)
    part = jnp.exp(lanes(logits, 0) + u[0:1, :] - top)
    for r in range(1, count):
        part = part + jnp.exp(lanes(logits, r) + u[r : r + 1, :] - top)
    send[:, 0] = jnp.broadcast_to(first_lane(top)[None], send[:, 0].shape)
    send[:, 1] = jnp.broadcast_to(gather_cols(part)[None], send[:, 1].shape)


def k_weights(log_b, logits, row_pot, recv, col_pot, weights, send):
    v = log_b - merge(recv)
    col_pot[...] = v
    vv = spread(v)
    u = row_pot[...]
    out = []
    for r in range(u.shape[0]):
        tile = jnp.exp(lanes(logits, r) + u[r : r + 1, :] + vv)
        weights[:, r * L : (r + 1) * L] = tile
        out.append(jnp.sum(tile, axis=0, keepdims=True))
    put_rows(send, out)


def weighted(weights, vec):
    part = lanes(weights, 0) * vec[0:1, :]
    for r in range(1, vec.shape[0]):
        part = part + lanes(weights, r) * vec[r : r + 1, :]
    return part


def k_col(weights, recv, row_mul, send):
    a = 1.0 / total(recv)
    row_mul[...] = a
    send[...] = jnp.broadcast_to(gather_cols(weighted(weights, a))[None], send.shape)


def k_row(ratio, weights, recv, col_mul, send):
    b = ratio / total(recv)
    col_mul[...] = b
    bb = spread(b)
    count = weights.shape[1] // L
    put_rows(send, row_sums([lanes(weights, r) * bb for r in range(count)]))


def k_last_col(weights, grad, recv, row_mul, send):
    a = 1.0 / total(recv)
    row_mul[...] = a
    part = lanes(weights, 0) * a[0:1, :]
    bar = part * lanes(grad, 0).astype(F32)
    for r in range(1, a.shape[0]):
        step = lanes(weights, r) * a[r : r + 1, :]
        part = part + step
        bar = bar + step * lanes(grad, r).astype(F32)
    send[:, 0] = jnp.broadcast_to(gather_cols(part)[None], send[:, 0].shape)
    send[:, 1] = jnp.broadcast_to(gather_cols(bar)[None], send[:, 1].shape)


def k_adj_row(ratio, weights, grad, recv, col_mul, col_adj, send):
    sums = total(recv)
    b = ratio / sums[0]
    x = b * (b * sums[1]) / ratio
    col_mul[...] = b
    col_adj[...] = x
    bb, xx = spread(b), spread(x)
    count = weights.shape[1] // L
    put_rows(
        send,
        row_sums(
            [lanes(weights, r) * (bb * lanes(grad, r).astype(F32) - xx) for r in range(count)]
        ),
    )


def k_back_col(sign, weights, row_mul, recv, row_adj, send):
    a = row_mul[...]
    y = sign * a * a * total(recv)
    row_adj[...] = y
    send[...] = jnp.broadcast_to(gather_cols(weighted(weights, y))[None], send.shape)


def k_back_row(ratio, weights, col_mul, recv, col_adj, send):
    b = col_mul[...]
    x = -b * b * total(recv) / ratio
    col_adj[...] = x
    xx = spread(x)
    count = weights.shape[1] // L
    put_rows(send, row_sums([lanes(weights, r) * xx for r in range(count)]))


def k_adjoint(scale, where, weights, grad, cent, col_pot, *refs):
    n = ITERS - 1
    row_mul = [None] + [r[...] for r in refs[:n]]
    col_mul = [jnp.exp(-col_pot[...]), None] + [r[...] for r in refs[n : 2 * n]]
    x = [r[...] for r in refs[2 * n : 3 * n + 1]]
    y = [None] + [r[...] for r in refs[3 * n + 1 : 4 * n + 1]]
    recv, adjoint, keep, cross = refs[4 * n + 1 :]
    y[0] = -total(recv)
    b4 = spread(col_mul[ITERS])
    xs = [spread(v) for v in x]
    bs = [spread(col_mul[0]), None] + [spread(v) for v in col_mul[2:ITERS]]
    count = y[0].shape[0]
    for r in range(count):
        row = slice(r, r + 1)
        inner = (b4 * row_mul[n][row, :]) * lanes(grad, r).astype(F32) - xs[0] - y[1][row, :]
        inner = inner - bs[0] * y[0][row, :]
        for t in range(1, ITERS):
            inner = inner - xs[t] * row_mul[t][row, :]
        for t in range(2, ITERS):
            inner = inner - bs[t] * y[t][row, :]
        adjoint[:, r * L : (r + 1) * L] = (lanes(weights, r) * inner).astype(BF16)
    width = keep.shape[2]
    for k in range(keep.shape[0]):
        for out, at in ((cross, where[1, k]), (keep, where[0, k])):
            block = cent[:, pl.ds(pl.multiple_of(at * width, L), width)]
            out[k] = (
                scale * lax.dot_general(adjoint[...], block, TN, preferred_element_type=F32)
            ).astype(out.dtype)


def k_cent(scale, groups, adjoint, whole, out):
    xs, zs, rows, _ = out.shape
    half = whole.shape[1] // 2
    for h in range(2):
        cols = slice(h * half, (h + 1) * half)
        part = scale * lax.dot_general(
            adjoint[...], whole[:, cols], NN, preferred_element_type=F32
        )
        part = part.astype(BF16)
        for iz in range(zs):
            for ix in range(xs):
                at = (iz * xs + ix) * rows
                out[ix, iz, :, cols] = part[at : at + rows, :]


def call(body, outs, *args, limit=SMALL, scalars=0, flops=0):
    spec = pl.BlockSpec(memory_space=pltpu.VMEM)
    ins = [pl.BlockSpec(memory_space=pltpu.SMEM)] * scalars + [spec] * (len(args) - scalars)
    size = sum(a.size * a.dtype.itemsize for a in args)
    return pl.pallas_call(
        body,
        out_shape=[jax.ShapeDtypeStruct(s, d) for s, d in outs],
        in_specs=ins,
        out_specs=[spec] * len(outs),
        compiler_params=pltpu.CompilerParams(vmem_limit_bytes=limit),
        cost_estimate=pl.CostEstimate(flops=flops, bytes_accessed=size, transcendentals=0),
        name=getattr(body, "func", body).__name__,
    )(*args)


def shift(value, axis, step):
    n = lax.axis_size(axis)
    return lax.ppermute(value, axis, [(i, (i + step) % n) for i in range(n)])


def shards(embeddings, centroids, plan_grad):
    rows, width = embeddings.shape
    cols, depth = centroids.shape
    ny, nx, nz = lax.axis_size("y"), lax.axis_size("x"), lax.axis_size("z")
    nclus, nprog = ny * 2, nz * nx
    scale = 1.0 / (0.25 * float(depth) ** 0.5)
    ratio = (rows * nprog) / (cols * nclus)
    log_b = math.log(ratio)
    rv, cv = (rows // L, L), (cols // L, L)
    iy, ic = lax.axis_index("y"), lax.axis_index("core")

    mine = [embeddings] + [shift(embeddings, "y", k) for k in range(1, ny)]
    theirs = [shift(m, "core", 1) for m in mine]
    source = [lax.rem(iy - k + ny, ny) * 2 for k in range(ny)]
    where = jnp.stack([s + ic for s in source] + [s + 1 - ic for s in source]).astype(jnp.int32)
    grad = plan_grad.T

    def over_clus(send):
        return lax.all_to_all(send, ("y", "core"), 0, 0, tiled=True)

    def over_prog(send):
        return lax.all_to_all(send, ("z", "x"), 0, 0, tiled=True)

    block = ((cols, rows), F32)
    row_send, col_send = ((nclus, *rv), F32), ((nprog, *cv), F32)
    row_pair, col_pair = ((nclus, 2, *rv), F32), ((nprog, 2, *cv), F32)
    a_row, a_col = (rv, F32), (cv, F32)

    whole, logits, send = call(
        functools.partial(k_logits, scale),
        [((rows, depth), BF16), block, row_pair],
        where, centroids, *mine, *theirs,
        limit=LARGE, scalars=1, flops=2 * rows * cols * depth,
    )
    row_pot, send = call(k_first_col, [a_row, col_pair], logits, over_clus(send))
    col_pot, weights, send = call(
        functools.partial(k_weights, log_b), [a_col, block, row_send], logits, row_pot, over_prog(send)
    )
    row_mul, col_mul = [], []
    for step in range(1, ITERS):
        recv = over_clus(send)
        if step < ITERS - 1:
            a, send = call(k_col, [a_row, col_send], weights, recv)
            b, send = call(
                functools.partial(k_row, ratio), [a_col, row_send], weights, over_prog(send)
            )
            col_mul.append(b)
        else:
            a, send = call(k_last_col, [a_row, col_pair], weights, grad, recv)
        row_mul.append(a)
    b, x, send = call(
        functools.partial(k_adj_row, ratio),
        [a_col, a_col, row_send],
        weights, grad, over_prog(send),
    )
    col_mul.append(b)
    col_adj, row_adj = [x], []
    for step in range(ITERS - 1, 0, -1):
        y, send = call(
            functools.partial(k_back_col, 1.0 if step == ITERS - 1 else -1.0),
            [a_row, col_send],
            weights, row_mul[step - 1], over_clus(send),
        )
        row_adj.insert(0, y)
        b = col_mul[step - 2] if step > 1 else jnp.ones(cv, F32)
        x, send = call(
            functools.partial(k_back_row, ratio), [a_col, row_send], weights, b, over_prog(send)
        )
        col_adj.insert(0, x)

    target = [lax.rem(iy + k, ny) * 2 for k in range(ny)]
    slots = jnp.stack(
        [jnp.stack([s + ic for s in target]), jnp.stack([s + 1 - ic for s in target])]
    ).astype(jnp.int32)
    adjoint, keep, cross = call(
        functools.partial(k_adjoint, scale),
        [((cols, rows), BF16), ((ny, rows, width), F32), ((ny, rows, width), BF16)],
        slots, weights, grad, centroids, col_pot, *row_mul, *col_mul, *col_adj, *row_adj, over_clus(send),
        limit=LARGE, scalars=1, flops=2 * rows * cols * depth,
    )
    cross = shift(cross, "core", 1)
    (parts,) = call(
        functools.partial(k_cent, scale, nx),
        [((nx, nz, cols // nprog, depth), BF16)],
        adjoint, whole,
        limit=LARGE, flops=2 * rows * cols * depth,
    )
    both = [keep[k] + cross[k].astype(F32) for k in range(ny)]
    moved = [shift(both[k].astype(BF16), "y", k) for k in range(1, ny)]
    parts = lax.all_to_all(parts, "x", 0, 0, tiled=True)
    parts = jnp.sum(parts.astype(F32), axis=0).astype(BF16)
    parts = lax.all_to_all(parts, "z", 0, 0, tiled=True)
    centroid_grad = jnp.sum(parts.astype(F32), axis=0).astype(BF16)
    embed_grad = both[0]
    for m in moved:
        embed_grad = embed_grad + m.astype(F32)
    return embed_grad.astype(BF16), centroid_grad


def solution(mesh):
    shape = dict(mesh.shape)
    nx = 4 if shape["prog"] % 4 == 0 and shape["prog"] > 4 else 2
    grid = (shape["prog"] // nx, nx, shape["clus"] // 2, 2)
    fine = Mesh(mesh.devices.reshape(grid), ("z", "x", "y", "core"))
    prog, clus = ("z", "x"), ("y", "core")
    return jax.shard_map(
        shards,
        mesh=fine,
        in_specs=(P(prog, clus), P(clus, None), P(prog, clus)),
        out_specs=(P(prog, clus), P(clus + prog, None)),
        check_vma=False,
    )
```

time: 1400 us -> 293 us (0.21)
  blocking collectives: 1000 us -> 162 us
  waiting for transfers between devices: 309 us -> 62 us
  other arithmetic: 56.3 us -> 8 us
  starting transfers between devices: 0.12 us -> 29.4 us
  Pallas kernels: 0 us -> 19.2 us
  matrix products: 15.8 us -> 0 us
    psum x16 -> x0, blocking collectives: 636 us -> none  [the longest x4 225 us: col_lse(): total = lax.psum(jnp.sum(jnp.exp(values - top[None, :]), axis=0), 'prog')]
    pmax x8 -> x0, blocking collectives: 366 us -> none  [the longest x4 233 us: col_lse(): top = lax.pmax(jnp.max(values, axis=0), 'prog')]
    reduce_scatter x2 -> x0, waiting for transfers between devices: 265 us -> none  [the longest x1 206 us: shards(): lax.psum_scatter(scale * lax.dot_general(adjoint_b, whole_rows, (((0,), (...]
    all_to_all x0 -> x13, blocking collectives: none -> 162 us  [the longest x6 80 us: over_prog(): return lax.all_to_all(send, ('z', 'x'), 0, 0, tiled=True)]
    all_gather x1 -> x0, waiting for transfers between devices: 42.7 us -> none  [shards(): whole_rows = lax.all_gather(embeddings, 'clus', axis=1, tiled=True)]
    ppermute x0 -> x11, waiting for transfers between devices: none -> 33.5 us  [shift(): return lax.ppermute(value, axis, [(i, (i + step) % n) for i in range(n)])]
    reduce_sum x16 -> x2, other arithmetic: 33.7 us -> 2.01 us  [the longest x1 1.31 us: shards(): parts = jnp.sum(parts.astype(F32), axis=0).astype(BF16)]
    all_to_all x0 -> x4, waiting for transfers between devices: none -> 28.4 us  [the longest x1 11.6 us: shards(): parts = lax.all_to_all(parts, 'z', 0, 0, tiled=True)]
  transfers between devices with their start and end apart: 3 -> 15, of which waited for: 3 -> 8; matrix products, arithmetic and copies ran while one was open for 1% -> 2% of each run, Pallas kernels for 0% -> 1%
where the time goes in v1:
time: 293 us; the launch traced here: 291 us
  blocking collectives  162 us (55%)
  waiting for transfers between devices  62 us (21%)
  starting transfers between devices  29.4 us (10%)
  Pallas kernels  19.2 us (7%)
  local copies, waits for them, and re-layouts  9.79 us (3%)
  other arithmetic  8 us (3%)
    all_to_all x6, blocking collectives, over_prog(): return lax.all_to_all(send, ('z', 'x'), 0, 0, tiled=True)  80 us
    all_to_all x6, blocking collectives, over_clus(): return lax.all_to_all(send, ('y', 'core'), 0, 0, tiled=True)  53.6 us
    ppermute x11, waiting for transfers between devices, shift(): return lax.ppermute(value, axis, [(i, (i + step) % n) for i in range(n)])  33.5 us
    all_to_all x1, blocking collectives, shards(): parts = lax.all_to_all(parts, 'x', 0, 0, tiled=True)  28.6 us
    pallas_call x17, Pallas kernels, call(): pl.pallas_call(body, out_shape=[jax.ShapeDtypeStruct(s, d) for s, d in ou...  19.2 us
    ppermute x11, starting transfers between devices, shift(): return lax.ppermute(value, axis, [(i, (i + step) % n) for i in range(n)])  11.7 us
    all_to_all x1, waiting for transfers between devices, shards(): parts = lax.all_to_all(parts, 'z', 0, 0, tiled=True)  11.6 us
    all_to_all x2, starting transfers between devices, over_clus(): return lax.all_to_all(send, ('y', 'core'), 0, 0, tiled=True)  10.3 us
  transfers between devices with their start and end apart: 15, of which 8 were waited for; matrix products, arithmetic and copies ran while one was open for 2% of the time, Pallas kernels for 1%

profile of v1, /device:TPU:1, one launch (start us, length us, event | category | flops | bytes accessed | tf_op | source)
XLA Modules:
  0.0 291.3 jit_solution(11706449628843849669)
XLA Ops:
  0.6 3.6 %collective-permute-start.2 = (bf16[1024,256]{1,0:T(8,128)(2,1)}, bf16[1024,256]{1,0:T(8,128)(2,1)S(1)}, u32[]{:S(2)}, u32[]{:S(2)}) collective-permute-start(bf16[1024,256]{1,0:T(8,128)(2,1)} %refs_0_.1), channel_id=1, source_target_pairs={{0,6},{2,0},{4,2},{6,4},{1,7},{3,1},{5,3},{7,5},{8,14},{10,8},{12,... | collective-permute-start | bytes 1572872 | tf_op jit(solution)/shard_map/ppermute | solution.py:241
  4.6 0.7 collective-permute-start
  5.3 1.5 collective-permute-start.3
  6.8 19.5 %collective-permute-done.2.refs_3_ = bf16[1024,256]{1,0:T(8,128)(2,1)S(1)} collective-permute-done((bf16[1024,256]{1,0:T(8,128)(2,1)}, bf16[1024,256]{1,0:T(8,128)(2,1)S(1)}, u32[]{:S(2)}, u32[]{:S(2)}) %collective-permute-start.2) | collective-permute-done | bytes 524320 | tf_op jit(solution)/shard_map/ppermute | solution.py:241
  26.3 1.7 collective-permute-start.6
  28.0 3.1 %collective-permute-done.refs_1_ = bf16[1024,256]{1,0:T(8,128)(2,1)S(1)} collective-permute-done((bf16[1024,256]{1,0:T(8,128)(2,1)}, bf16[1024,256]{1,0:T(8,128)(2,1)S(1)}, u32[]{:S(2)}, u32[]{:S(2)}) %collective-permute-start) | collective-permute-done | bytes 524320 | tf_op jit(solution)/shard_map/ppermute | solution.py:241
  31.7 1.6 collective-permute-done.4.refs_5_
  33.2 1.6 copy-done.1
  34.8 1.0 copy-done.3
  35.9 4.3 %k_logits.1 = (bf16[1024,2048]{1,0:T(8,128)(2,1)S(1)}, f32[512,1024]{1,0:T(8,128)S(1)}, f32[8,2,8,128]{3,2,1,0:T(8,128)S(1)}) custom-call(s32[8]{0:T(128)S(1)} %stack.69.where, bf16[512,2048]{1,0:T(8,128)(2,1)S(1)} %copy-done.1, bf16[1024,256]{1,0:T(8,128)(2,1)S(1)} %copy-done.3, bf16[1024,256]{1,0:T(8,128)(2,1)S(1)} %collective-permute-done.refs_1_, ...), custom_call_target="tpu_custom_call" | custom-call | flops 2147483648 | bytes 6291488 | tf_op jit(solution)/shard_map/k_logits/pallas_call | solution.py:228
  40.2 2.0 copy-done.4
  42.2 7.8 %all_to_all.85.recv = f32[8,2,8,128]{3,2,1,0:T(8,128)S(1)} all-to-all(f32[8,2,8,128]{3,2,1,0:T(8,128)S(1)} %get-tuple-element.39), channel_id=1, replica_groups=mesh['z'=8,'x'=4,'y'=4,'core'=2] {'y','core'}, dimensions={0} | all-to-all | bytes 131072 | tf_op jit(solution)/shard_map/all_to_all | solution.py:262
  49.9 0.6 k_first_col.1
  50.5 20.2 %all_to_all.86.recv = f32[32,2,4,128]{3,2,1,0:T(4,128)S(1)} all-to-all(f32[32,2,4,128]{3,2,1,0:T(4,128)S(1)} %get-tuple-element.41), channel_id=1, replica_groups=mesh['z'=8,'x'=4,'y'=4,'core'=2] {'z','x'}, dimensions={0} | all-to-all | bytes 262144 | tf_op jit(solution)/shard_map/all_to_all | solution.py:265
  71.2 9.3 %all_to_all.87.recv = f32[8,8,128]{2,1,0:T(8,128)S(1)} all-to-all(f32[8,8,128]{2,1,0:T(8,128)S(1)} %get-tuple-element.44), channel_id=1, replica_groups=mesh['z'=8,'x'=4,'y'=4,'core'=2] {'y','core'}, dimensions={0} | all-to-all | bytes 65536 | tf_op jit(solution)/shard_map/all_to_all | solution.py:262
  80.7 11.8 %all_to_all.88.recv = f32[32,4,128]{2,1,0:T(4,128)S(1)} all-to-all(f32[32,4,128]{2,1,0:T(4,128)S(1)} %get-tuple-element.46), channel_id=1, replica_groups=mesh['z'=8,'x'=4,'y'=4,'core'=2] {'z','x'}, dimensions={0} | all-to-all | bytes 131072 | tf_op jit(solution)/shard_map/all_to_all | solution.py:265
  92.8 9.2 %all_to_all.89.recv = f32[8,8,128]{2,1,0:T(8,128)S(1)} all-to-all(f32[8,8,128]{2,1,0:T(8,128)S(1)} %get-tuple-element.47), channel_id=1, replica_groups=mesh['z'=8,'x'=4,'y'=4,'core'=2] {'y','core'}, dimensions={0} | all-to-all | bytes 65536 | tf_op jit(solution)/shard_map/all_to_all | solution.py:262
  102.2 11.8 %all_to_all.90.recv = f32[32,4,128]{2,1,0:T(4,128)S(1)} all-to-all(f32[32,4,128]{2,1,0:T(4,128)S(1)} %get-tuple-element.49), channel_id=1, replica_groups=mesh['z'=8,'x'=4,'y'=4,'core'=2] {'z','x'}, dimensions={0} | all-to-all | bytes 131072 | tf_op jit(solution)/shard_map/all_to_all | solution.py:265
  114.1 0.9 k_row.3
  115.0 5.2 %all-to-all-start.6 = ((f32[8,8,128]{2,1,0:T(8,128)}), f32[8,8,128]{2,1,0:T(8,128)S(1)}, u32[]{:S(2)}, u32[]{:S(2)}) async-start(f32[8,8,128]{2,1,0:T(8,128)} %get-tuple-element.50), calls=%async_computation.6 | async-start | bytes 65536 | tf_op jit(solution)/shard_map/all_to_all | solution.py:262
  120.2 1.5 copy.6
  121.7 3.2 %all-to-all-done.6.recv = f32[8,8,128]{2,1,0:T(8,128)S(1)} async-done(((f32[8,8,128]{2,1,0:T(8,128)}), f32[8,8,128]{2,1,0:T(8,128)S(1)}, u32[]{:S(2)}, u32[]{:S(2)}) %all-to-all-start.6) | async-done | bytes 32800 | tf_op jit(solution)/shard_map/all_to_all | solution.py:262
  125.4 12.4 %all_to_all.91.recv = f32[32,2,4,128]{3,2,1,0:T(4,128)S(1)} all-to-all(f32[32,2,4,128]{3,2,1,0:T(4,128)S(1)} %get-tuple-element.54), channel_id=1, replica_groups=mesh['z'=8,'x'=4,'y'=4,'core'=2] {'z','x'}, dimensions={0} | all-to-all | bytes 262144 | tf_op jit(solution)/shard_map/all_to_all | solution.py:265
  138.3 9.2 %all_to_all.92.recv = f32[8,8,128]{2,1,0:T(8,128)S(1)} all-to-all(f32[8,8,128]{2,1,0:T(8,128)S(1)} %get-tuple-element.56), channel_id=1, replica_groups=mesh['z'=8,'x'=4,'y'=4,'core'=2] {'y','core'}, dimensions={0} | all-to-all | bytes 65536 | tf_op jit(solution)/shard_map/all_to_all | solution.py:262
  147.7 11.9 %all_to_all.93.recv = f32[32,4,128]{2,1,0:T(4,128)S(1)} all-to-all(f32[32,4,128]{2,1,0:T(4,128)S(1)} %get-tuple-element.57), channel_id=1, replica_groups=mesh['z'=8,'x'=4,'y'=4,'core'=2] {'z','x'}, dimensions={0} | all-to-all | bytes 131072 | tf_op jit(solution)/shard_map/all_to_all | solution.py:265
  159.9 9.0 %all_to_all.94.recv = f32[8,8,128]{2,1,0:T(8,128)S(1)} all-to-all(f32[8,8,128]{2,1,0:T(8,128)S(1)} %get-tuple-element.58), channel_id=1, replica_groups=mesh['z'=8,'x'=4,'y'=4,'core'=2] {'y','core'}, dimensions={0} | all-to-all | bytes 65536 | tf_op jit(solution)/shard_map/all_to_all | solution.py:262
  169.1 11.8 %all_to_all.95.recv = f32[32,4,128]{2,1,0:T(4,128)S(1)} all-to-all(f32[32,4,128]{2,1,0:T(4,128)S(1)} %get-tuple-element.59), channel_id=1, replica_groups=mesh['z'=8,'x'=4,'y'=4,'core'=2] {'z','x'}, dimensions={0} | all-to-all | bytes 131072 | tf_op jit(solution)/shard_map/all_to_all | solution.py:265
  181.3 9.1 %all_to_all.96.recv = f32[8,8,128]{2,1,0:T(8,128)S(1)} all-to-all(f32[8,8,128]{2,1,0:T(8,128)S(1)} %get-tuple-element.60), channel_id=1, replica_groups=mesh['z'=8,'x'=4,'y'=4,'core'=2] {'y','core'}, dimensions={0} | all-to-all | bytes 65536 | tf_op jit(solution)/shard_map/all_to_all | solution.py:262
  190.3 0.9 k_back_col.5
  191.2 3.9 %all-to-all-start.13 = ((f32[32,4,128]{2,1,0:T(4,128)}), f32[32,4,128]{2,1,0:T(4,128)S(1)}, u32[]{:S(2)}, u32[]{:S(2)}) async-start(f32[32,4,128]{2,1,0:T(4,128)} %get-tuple-element.61), calls=%async_computation.13 | async-start | bytes 131072 | tf_op jit(solution)/shard_map/all_to_all | solution.py:265
  195.1 8.8 %all-to-all-done.13.recv = f32[32,4,128]{2,1,0:T(4,128)S(1)} async-done(((f32[32,4,128]{2,1,0:T(4,128)}), f32[32,4,128]{2,1,0:T(4,128)S(1)}, u32[]{:S(2)}, u32[]{:S(2)}) %all-to-all-start.13) | async-done | bytes 65568 | tf_op jit(solution)/shard_map/all_to_all | solution.py:265
  203.9 0.9 k_back_row.5
  204.8 5.1 %all-to-all-start.14 = ((f32[8,8,128]{2,1,0:T(8,128)}), f32[8,8,128]{2,1,0:T(8,128)S(1)}, u32[]{:S(2)}, u32[]{:S(2)}) async-start(f32[8,8,128]{2,1,0:T(8,128)} %get-tuple-element.69), calls=%async_computation.14 | async-start | bytes 65536 | tf_op jit(solution)/shard_map/all_to_all | solution.py:262
  209.9 4.7 %all-to-all-done.14.refs_13_ = f32[8,8,128]{2,1,0:T(8,128)S(1)} async-done(((f32[8,8,128]{2,1,0:T(8,128)}), f32[8,8,128]{2,1,0:T(8,128)S(1)}, u32[]{:S(2)}, u32[]{:S(2)}) %all-to-all-start.14) | async-done | bytes 32800 | tf_op jit(solution)/shard_map/all_to_all | solution.py:262
  214.6 1.6 copy-done.2
  216.2 6.3 %k_adjoint.1 = (bf16[512,1024]{1,0:T(8,128)(2,1)S(1)}, f32[4,1024,256]{2,1,0:T(8,128)S(1)}, bf16[4,1024,256]{2,1,0:T(8,128)(2,1)}) custom-call(s32[2,4]{1,0:T(2,128)S(1)} %pad_add_fusion.where, f32[512,1024]{1,0:T(8,128)S(1)} %get-tuple-element.42.weights, bf16[512,1024]{1,0:T(8,128)(2,1)S(1)} %bitcast.31, bf16[512,2048]{1,0:T(8,128)(2,1)S(1)} %copy-done.2, ...), custom_call_target="tpu_custom_call" | custom-call | flops 2147483648 | bytes 5316640 | tf_op jit(solution)/shard_map/k_adjoint/pallas_call | solution.py:228
  222.5 2.0 copy-done
  224.5 0.7 collective-permute-start.7
  225.2 2.3 k_cent.1
  227.6 28.6 %all_to_all.97 = bf16[4,8,16,2048]{3,2,1,0:T(8,128)(2,1)S(1)} all-to-all(bf16[4,8,16,2048]{3,2,1,0:T(8,128)(2,1)S(1)} %k_cent.1), channel_id=1, replica_groups=mesh['z'=8,'x'=4,'y'=4,'core'=2] {'x'}, dimensions={0} | all-to-all | bytes 4194304 | tf_op jit(solution)/shard_map/all_to_all | solution.py:333
  256.2 1.3 reduce_sum.24
  257.5 3.5 %all-to-all-start.16 = ((bf16[8,16,2048]{2,1,0:T(8,128)(2,1)}), bf16[8,16,2048]{2,1,0:T(8,128)(2,1)S(1)}, u32[]{:S(2)}, u32[]{:S(2)}) async-start(bf16[8,16,2048]{2,1,0:T(8,128)(2,1)} %reduce_sum.24), calls=%async_computation.16 | async-start | bytes 1048576 | tf_op jit(solution)/shard_map/all_to_all | solution.py:335
  261.0 3.5 %fusion.3 = (bf16[1024,256]{1,0:T(8,128)(2,1)}, bf16[1024,256]{1,0:T(8,128)(2,1)S(1)}, bf16[1024,256]{1,0:T(8,128)(2,1)S(1)}) fusion(f32[4,1024,256]{2,1,0:T(8,128)} %copy-done, bf16[4,1024,256]{2,1,0:T(8,128)(2,1)} %collective-permute-done.7), kind=kLoop, calls=%fused_computation.7 | loop fusion | flops 2359296 | bytes 6291456 | tf_op jit(solution)/shard_map/convert_element_type | solution.py:332
  264.8 2.4 collective-permute-start.10
  267.1 11.6 %all-to-all-done.16 = bf16[8,16,2048]{2,1,0:T(8,128)(2,1)S(1)} async-done(((bf16[8,16,2048]{2,1,0:T(8,128)(2,1)}), bf16[8,16,2048]{2,1,0:T(8,128)(2,1)S(1)}, u32[]{:S(2)}, u32[]{:S(2)}) %all-to-all-start.16) | async-done | bytes 524320 | tf_op jit(solution)/shard_map/all_to_all | solution.py:335
  278.8 0.7 reduce_sum.25
  279.5 9.4 %collective-permute-done.9 = bf16[1024,256]{1,0:T(8,128)(2,1)S(1)} collective-permute-done((bf16[1024,256]{1,0:T(8,128)(2,1)S(1)}, bf16[1024,256]{1,0:T(8,128)(2,1)S(1)}, u32[]{:S(2)}, u32[]{:S(2)}) %collective-permute-start.9) | collective-permute-done | bytes 524320 | tf_op jit(solution)/shard_map/ppermute | solution.py:241
  288.9 2.4 fusion.2
  (33 shorter events, 4.5 us)
Async XLA Ops:
  0.6 25.6 %collective-permute-start.2 = (bf16[1024,256]{1,0:T(8,128)(2,1)}, bf16[1024,256]{1,0:T(8,128)(2,1)S(1)}, u32[]{:S(2)}, u32[]{:S(2)}) collective-permute-start(bf16[1024,256]{1,0:T(8,128)(2,1)} %refs_0_.1), channel_id=1, source_target_pairs={{0,6},{2,0},{4,2},{6,4},{1,7},{3,1},{5,3},{7,5},{8,14},{10,8},{12,... | collective-permute-start | bytes 1572872 | tf_op jit(solution)/shard_map/ppermute | solution.py:241
  4.3 23.7 %collective-permute-start.1 = (bf16[1024,256]{1,0:T(8,128)(2,1)}, bf16[1024,256]{1,0:T(8,128)(2,1)S(1)}, u32[]{:S(2)}, u32[]{:S(2)}) collective-permute-start(bf16[1024,256]{1,0:T(8,128)(2,1)} %refs_0_.1), channel_id=1, source_target_pairs={{0,4},{2,6},{4,0},{6,2},{1,5},{3,7},{5,1},{7,3},{8,12},{10,14},{12... | collective-permute-start | bytes 1572872 | tf_op jit(solution)/shard_map/ppermute | solution.py:241
  4.6 26.4 %collective-permute-start = (bf16[1024,256]{1,0:T(8,128)(2,1)}, bf16[1024,256]{1,0:T(8,128)(2,1)S(1)}, u32[]{:S(2)}, u32[]{:S(2)}) collective-permute-start(bf16[1024,256]{1,0:T(8,128)(2,1)} %refs_0_.1), channel_id=1, source_target_pairs={{0,2},{2,4},{4,6},{6,0},{1,3},{3,5},{5,7},{7,1},{8,10},{10,12},{12... | collective-permute-start | bytes 1572872 | tf_op jit(solution)/shard_map/ppermute | solution.py:241
  5.3 26.3 %collective-permute-start.3 = (bf16[1024,256]{1,0:T(8,128)(2,1)}, bf16[1024,256]{1,0:T(8,128)(2,1)S(1)}, u32[]{:S(2)}, u32[]{:S(2)}) collective-permute-start(bf16[1024,256]{1,0:T(8,128)(2,1)} %refs_0_.1), channel_id=1, source_target_pairs={{0,1},{1,0},{2,3},{3,2},{4,5},{5,4},{6,7},{7,6},{8,9},{9,8},{10,11... | collective-permute-start | bytes 1572872 | tf_op jit(solution)/shard_map/ppermute | solution.py:241
  26.3 5.4 %collective-permute-start.6 = (bf16[1024,256]{1,0:T(8,128)(2,1)S(1)}, bf16[1024,256]{1,0:T(8,128)(2,1)S(1)}, u32[]{:S(2)}, u32[]{:S(2)}) collective-permute-start(bf16[1024,256]{1,0:T(8,128)(2,1)S(1)} %collective-permute-done.2.refs_3_), channel_id=1, source_target_pairs={{0,1},{1,0},{2,3},{3,2},{4,5},{5,4},{6,7},{7,6},{8,9},{9,8},{10,11... | collective-permute-start | bytes 1572872 | tf_op jit(solution)/shard_map/ppermute | solution.py:241
  28.0 3.7 %collective-permute-start.5 = (bf16[1024,256]{1,0:T(8,128)(2,1)S(1)}, bf16[1024,256]{1,0:T(8,128)(2,1)S(1)}, u32[]{:S(2)}, u32[]{:S(2)}) collective-permute-start(bf16[1024,256]{1,0:T(8,128)(2,1)S(1)} %collective-permute-done.1.refs_2_), channel_id=1, source_target_pairs={{0,1},{1,0},{2,3},{3,2},{4,5},{5,4},{6,7},{7,6},{8,9},{9,8},{10,11... | collective-permute-start | bytes 1572872 | tf_op jit(solution)/shard_map/ppermute | solution.py:241
  31.1 2.2 collective-permute-start.4
  33.2 1.6 copy-start.1
  34.8 1.0 copy-start.3
  40.2 2.0 copy-start.4
  115.0 9.9 %all-to-all-start.6 = ((f32[8,8,128]{2,1,0:T(8,128)}), f32[8,8,128]{2,1,0:T(8,128)S(1)}, u32[]{:S(2)}, u32[]{:S(2)}) async-start(f32[8,8,128]{2,1,0:T(8,128)} %get-tuple-element.50), calls=%async_computation.6 | async-start | bytes 65536 | tf_op jit(solution)/shard_map/all_to_all | solution.py:262
  191.2 12.8 %all-to-all-start.13 = ((f32[32,4,128]{2,1,0:T(4,128)}), f32[32,4,128]{2,1,0:T(4,128)S(1)}, u32[]{:S(2)}, u32[]{:S(2)}) async-start(f32[32,4,128]{2,1,0:T(4,128)} %get-tuple-element.61), calls=%async_computation.13 | async-start | bytes 131072 | tf_op jit(solution)/shard_map/all_to_all | solution.py:265
  204.8 9.8 %all-to-all-start.14 = ((f32[8,8,128]{2,1,0:T(8,128)}), f32[8,8,128]{2,1,0:T(8,128)S(1)}, u32[]{:S(2)}, u32[]{:S(2)}) async-start(f32[8,8,128]{2,1,0:T(8,128)} %get-tuple-element.69), calls=%async_computation.14 | async-start | bytes 65536 | tf_op jit(solution)/shard_map/all_to_all | solution.py:262
  214.6 1.6 copy-start.2
  216.2 9.0 %copy-start.5 = (bf16[1024,2048]{1,0:T(8,128)(2,1)S(1)}, bf16[1024,2048]{1,0:T(8,128)(2,1)}, u32[]{:S(2)}) copy-start(bf16[1024,2048]{1,0:T(8,128)(2,1)} %copy-done.4) | copy-start | bytes 12582916
  222.5 2.0 copy-start
  224.5 36.5 %collective-permute-start.7 = (bf16[4,1024,256]{2,1,0:T(8,128)(2,1)}, bf16[4,1024,256]{2,1,0:T(8,128)(2,1)}, u32[]{:S(2)}, u32[]{:S(2)}) collective-permute-start(bf16[4,1024,256]{2,1,0:T(8,128)(2,1)} %get-tuple-element.71), channel_id=1, source_target_pairs={{0,1},{1,0},{2,3},{3,2},{4,5},{5,4},{6,7},{7,6},{8,9},{9,8},{10,11... | collective-permute-start | bytes 6291464 | tf_op jit(solution)/shard_map/ppermute | solution.py:241
  257.5 21.3 %all-to-all-start.16 = ((bf16[8,16,2048]{2,1,0:T(8,128)(2,1)}), bf16[8,16,2048]{2,1,0:T(8,128)(2,1)S(1)}, u32[]{:S(2)}, u32[]{:S(2)}) async-start(bf16[8,16,2048]{2,1,0:T(8,128)(2,1)} %reduce_sum.24), calls=%async_computation.16 | async-start | bytes 1048576 | tf_op jit(solution)/shard_map/all_to_all | solution.py:335
  264.5 15.0 %collective-permute-start.8 = (bf16[1024,256]{1,0:T(8,128)(2,1)}, bf16[1024,256]{1,0:T(8,128)(2,1)S(1)}, u32[]{:S(2)}, u32[]{:S(2)}) collective-permute-start(bf16[1024,256]{1,0:T(8,128)(2,1)} %get-tuple-element.74), channel_id=1, source_target_pairs={{0,2},{2,4},{4,6},{6,0},{1,3},{3,5},{5,7},{7,1},{8,10},{10,12},{12... | collective-permute-start | bytes 1572872 | tf_op jit(solution)/shard_map/ppermute | solution.py:241
  264.8 14.7 %collective-permute-start.10 = (bf16[1024,256]{1,0:T(8,128)(2,1)S(1)}, bf16[1024,256]{1,0:T(8,128)(2,1)S(1)}, u32[]{:S(2)}, u32[]{:S(2)}) collective-permute-start(bf16[1024,256]{1,0:T(8,128)(2,1)S(1)} %get-tuple-element.75), channel_id=1, source_target_pairs={{0,6},{2,0},{4,2},{6,4},{1,7},{3,1},{5,3},{7,5},{8,14},{10,8},{12,... | collective-permute-start | bytes 1572872 | tf_op jit(solution)/shard_map/ppermute | solution.py:241
  267.1 21.7 %collective-permute-start.9 = (bf16[1024,256]{1,0:T(8,128)(2,1)S(1)}, bf16[1024,256]{1,0:T(8,128)(2,1)S(1)}, u32[]{:S(2)}, u32[]{:S(2)}) collective-permute-start(bf16[1024,256]{1,0:T(8,128)(2,1)S(1)} %get-tuple-element.76), channel_id=1, source_target_pairs={{0,4},{2,6},{4,0},{6,2},{1,5},{3,7},{5,1},{7,3},{8,12},{10,14},{12... | collective-permute-start | bytes 1572872 | tf_op jit(solution)/shard_map/ppermute | solution.py:241

commit v2 on v1

--- a/solution.py
+++ b/solution.py
@@ -9,13 +9,13 @@
 from jax.sharding import Mesh
 from jax.sharding import PartitionSpec as P
 
+
 ITERS = 4
 L = 128
 F32 = jnp.float32
 BF16 = jnp.bfloat16
 NT = (((1,), (1,)), ((), ()))
 NN = (((1,), (0,)), ((), ()))
-TN = (((0,), (0,)), ((), ()))
 SMALL = 12 << 20
 LARGE = 40 << 20
 
@@ -64,13 +64,25 @@
     return top + jnp.log(jnp.sum(recv[:, 1] * jnp.exp(tops - top[None]), axis=0))
 
 
+def k_prepare(plan_grad, grad):
+    grad[...] = plan_grad[...].T
+
+
 def k_logits(scale, where, cent, *refs):
-    n = len(refs) - 3
-    pieces, (whole, logits, send) = refs[:n], refs[n:]
+    n = len(refs) - 4
+    pieces, (logits, send, held, sems) = refs[:n], refs[n:]
     width = pieces[0].shape[1]
-    for k in range(n):
-        whole[:, pl.ds(pl.multiple_of(where[k] * width, L), width)] = pieces[k][...]
-    logits[...] = scale * lax.dot_general(cent[...], whole[...], NT, preferred_element_type=F32)
+    copies = [
+        pltpu.make_async_copy(
+            piece, held.at[:, pl.ds(pl.multiple_of(where[k] * width, L), width)], sems.at[k]
+        )
+        for k, piece in enumerate(pieces)
+    ]
+    for c in copies:
+        c.start()
+    for c in copies:
+        c.wait()
+    logits[...] = scale * lax.dot_general(cent[...], held[...], NT, preferred_element_type=F32)
     count = logits.shape[1] // L
     tops, sums = [], []
     for r in range(count):
@@ -176,63 +188,117 @@
     put_rows(send, row_sums([lanes(weights, r) * xx for r in range(count)]))
 
 
-def k_adjoint(scale, where, weights, grad, cent, col_pot, *refs):
+def k_known(weights, grad, col_pot, *refs):
     n = ITERS - 1
+    base, first = refs[4 * n + 1 :]
     row_mul = [None] + [r[...] for r in refs[:n]]
-    col_mul = [jnp.exp(-col_pot[...]), None] + [r[...] for r in refs[n : 2 * n]]
+    col_mul = [None, None] + [r[...] for r in refs[n : 2 * n]]
     x = [r[...] for r in refs[2 * n : 3 * n + 1]]
     y = [None] + [r[...] for r in refs[3 * n + 1 : 4 * n + 1]]
-    recv, adjoint, keep, cross = refs[4 * n + 1 :]
-    y[0] = -total(recv)
+    b0 = spread(jnp.exp(-col_pot[...]))
     b4 = spread(col_mul[ITERS])
     xs = [spread(v) for v in x]
-    bs = [spread(col_mul[0]), None] + [spread(v) for v in col_mul[2:ITERS]]
-    count = y[0].shape[0]
-    for r in range(count):
+    bs = [None, None] + [spread(v) for v in col_mul[2:ITERS]]
+    for r in range(base.shape[1] // L):
         row = slice(r, r + 1)
+        tile = lanes(weights, r)
         inner = (b4 * row_mul[n][row, :]) * lanes(grad, r).astype(F32) - xs[0] - y[1][row, :]
-        inner = inner - bs[0] * y[0][row, :]
         for t in range(1, ITERS):
             inner = inner - xs[t] * row_mul[t][row, :]
         for t in range(2, ITERS):
             inner = inner - bs[t] * y[t][row, :]
-        adjoint[:, r * L : (r + 1) * L] = (lanes(weights, r) * inner).astype(BF16)
-    width = keep.shape[2]
-    for k in range(keep.shape[0]):
-        for out, at in ((cross, where[1, k]), (keep, where[0, k])):
-            block = cent[:, pl.ds(pl.multiple_of(at * width, L), width)]
-            out[k] = (
-                scale * lax.dot_general(adjoint[...], block, TN, preferred_element_type=F32)
-            ).astype(out.dtype)
-
-
-def k_cent(scale, groups, adjoint, whole, out):
-    xs, zs, rows, _ = out.shape
-    half = whole.shape[1] // 2
-    for h in range(2):
-        cols = slice(h * half, (h + 1) * half)
-        part = scale * lax.dot_general(
-            adjoint[...], whole[:, cols], NN, preferred_element_type=F32
-        )
-        part = part.astype(BF16)
-        for iz in range(zs):
-            for ix in range(xs):
-                at = (iz * xs + ix) * rows
-                out[ix, iz, :, cols] = part[at : at + rows, :]
-
-
-def call(body, outs, *args, limit=SMALL, scalars=0, flops=0):
-    spec = pl.BlockSpec(memory_space=pltpu.VMEM)
-    ins = [pl.BlockSpec(memory_space=pltpu.SMEM)] * scalars + [spec] * (len(args) - scalars)
+        first[:, r * L : (r + 1) * L] = (tile * b0).astype(BF16)
+        base[:, r * L : (r + 1) * L] = tile * inner
+
+
+def k_adjoint(scale, where, order, base, first, recv, *refs):
+    n = where.shape[0]
+    nx = order.shape[0]
+    pieces, adjoint, keep = refs[:n], refs[n], refs[n + 1]
+    sends, (held, turned, sems) = refs[n + 2 : n + 1 + nx], refs[n + 1 + nx :]
+    copies = [
+        pltpu.make_async_copy(piece, held.at[k], sems.at[k]) for k, piece in enumerate(pieces)
+    ]
+    for c in copies:
+        c.start()
+    y = -total(recv)
+    for r in range(y.shape[0]):
+        adjoint[:, r * L : (r + 1) * L] = (
+            lanes(base, r) - lanes(first, r).astype(F32) * y[r : r + 1, :]
+        ).astype(BF16)
+    per = keep.shape[0]
+    group = 16
+    for k in range(nx):
+        for iz in range(per // group):
+            at = pl.multiple_of((iz * nx + order[k]) * group, group)
+            turned[k * per + iz * group : k * per + (iz + 1) * group, :] = adjoint[pl.ds(at, group), :]
+    width = held.shape[2]
+    for p in range(n):
+        copies[p].wait()
+        part = scale * lax.dot_general(turned[...], held[p], NN, preferred_element_type=F32)
+        cols = pl.ds(pl.multiple_of(where[p] * width, L), width)
+        keep[:, cols] = part[:per, :]
+        for k in range(1, nx):
+            sends[k - 1][:, cols] = part[k * per : (k + 1) * per, :].astype(BF16)
+
+
+def k_cross(scale, where, adjoint, cent_hbm, cross, turned, cent, sem):
+    copy = pltpu.make_async_copy(cent_hbm, cent, sem)
+    copy.start()
+    turned[...] = adjoint[...].T
+    copy.wait()
+    width = cross.shape[2]
+    for k in range(cross.shape[0]):
+        block = cent[:, pl.ds(pl.multiple_of(where[k] * width, L), width)]
+        part = scale * lax.dot_general(turned[...], block, NN, preferred_element_type=F32)
+        cross[k] = part.astype(cross.dtype)
+
+
+def k_pair(scale, where, turned, cent_hbm, cross_hbm, first, *refs):
+    rest, (cent, cross, sems) = refs[:-3], refs[-3:]
+    copies = [
+        pltpu.make_async_copy(cent_hbm, cent, sems.at[0]),
+        pltpu.make_async_copy(cross_hbm, cross, sems.at[1]),
+    ]
+    for c in copies:
+        c.start()
+    for c in copies:
+        c.wait()
+    width = first.shape[1]
+    for k, out in enumerate((first, *rest)):
+        block = cent[:, pl.ds(pl.multiple_of(where[k] * width, L), width)]
+        part = scale * lax.dot_general(turned[...], block, NN, preferred_element_type=F32)
+        out[...] = (part + cross[k].astype(F32)).astype(out.dtype)
+
+
+def k_add(first, *refs):
+    value = first[...]
+    for r in refs[:-1]:
+        value = value + r[...].astype(F32)
+    refs[-1][...] = value.astype(BF16).reshape(refs[-1].shape)
+
+
+def k_sum(recv, out):
+    value = recv[0].astype(F32)
+    for k in range(1, recv.shape[0]):
+        value = value + recv[k].astype(F32)
+    out[...] = value.astype(BF16)
+
+
+def call(body, outs, *args, limit=SMALL, scalars=0, flops=0, hbm_in=(), alias=None, scratch=()):
+    spec, far = pl.BlockSpec(memory_space=pltpu.VMEM), pl.BlockSpec(memory_space=pltpu.HBM)
+    smem = pl.BlockSpec(memory_space=pltpu.SMEM)
+    ins = [smem if i < scalars else far if i in hbm_in else spec for i in range(len(args))]
     size = sum(a.size * a.dtype.itemsize for a in args)
     return pl.pallas_call(
         body,
         out_shape=[jax.ShapeDtypeStruct(s, d) for s, d in outs],
         in_specs=ins,
         out_specs=[spec] * len(outs),
+        input_output_aliases=alias or {},
+        scratch_shapes=list(scratch),
         compiler_params=pltpu.CompilerParams(vmem_limit_bytes=limit),
         cost_estimate=pl.CostEstimate(flops=flops, bytes_accessed=size, transcendentals=0),
-        name=getattr(body, "func", body).__name__,
     )(*args)
 
 
@@ -250,13 +316,14 @@
     ratio = (rows * nprog) / (cols * nclus)
     log_b = math.log(ratio)
     rv, cv = (rows // L, L), (cols // L, L)
-    iy, ic = lax.axis_index("y"), lax.axis_index("core")
+    ix, iy, ic = lax.axis_index("x"), lax.axis_index("y"), lax.axis_index("core")
 
     mine = [embeddings] + [shift(embeddings, "y", k) for k in range(1, ny)]
     theirs = [shift(m, "core", 1) for m in mine]
     source = [lax.rem(iy - k + ny, ny) * 2 for k in range(ny)]
     where = jnp.stack([s + ic for s in source] + [s + 1 - ic for s in source]).astype(jnp.int32)
-    grad = plan_grad.T
+    (grad,) = call(k_prepare, [((cols, rows), BF16)], plan_grad)
+    mine[0], grad = lax.optimization_barrier((mine[0], grad))
 
     def over_clus(send):
         return lax.all_to_all(send, ("y", "core"), 0, 0, tiled=True)
@@ -269,11 +336,14 @@
     row_pair, col_pair = ((nclus, 2, *rv), F32), ((nprog, 2, *cv), F32)
     a_row, a_col = (rv, F32), (cv, F32)
 
-    whole, logits, send = call(
+    pieces = [*mine, *theirs]
+    logits, send = call(
         functools.partial(k_logits, scale),
-        [((rows, depth), BF16), block, row_pair],
-        where, centroids, *mine, *theirs,
+        [block, row_pair],
+        where, centroids, *pieces,
         limit=LARGE, scalars=1, flops=2 * rows * cols * depth,
+        hbm_in=range(2, 2 + len(pieces)),
+        scratch=[pltpu.VMEM((rows, depth), BF16), pltpu.SemaphoreType.DMA((len(pieces),))],
     )
     row_pot, send = call(k_first_col, [a_row, col_pair], logits, over_clus(send))
     col_pot, weights, send = call(
@@ -312,32 +382,56 @@
         col_adj.insert(0, x)
 
     target = [lax.rem(iy + k, ny) * 2 for k in range(ny)]
-    slots = jnp.stack(
-        [jnp.stack([s + ic for s in target]), jnp.stack([s + 1 - ic for s in target])]
-    ).astype(jnp.int32)
-    adjoint, keep, cross = call(
+    here = jnp.stack([s + ic for s in target]).astype(jnp.int32)
+    there = jnp.stack([s + 1 - ic for s in target]).astype(jnp.int32)
+    order = jnp.stack([lax.rem(ix + k, nx) for k in range(nx)]).astype(jnp.int32)
+    work = 2 * rows * cols * depth
+    recv = over_clus(send)
+    base, first = call(
+        k_known,
+        [block, ((cols, rows), BF16)],
+        weights, grad, col_pot, *row_mul, *col_mul, *col_adj, *row_adj,
+        flops=work, alias={0: 0, 1: 1},
+    )
+    per, n = cols // nx, len(pieces)
+    adjoint, near, *parts = call(
         functools.partial(k_adjoint, scale),
-        [((cols, rows), BF16), ((ny, rows, width), F32), ((ny, rows, width), BF16)],
-        slots, weights, grad, centroids, col_pot, *row_mul, *col_mul, *col_adj, *row_adj, over_clus(send),
-        limit=LARGE, scalars=1, flops=2 * rows * cols * depth,
+        [((cols, rows), BF16), ((per, depth), F32)] + [((per, depth), BF16)] * (nx - 1),
+        where, order, base, first, recv, *pieces,
+        limit=LARGE, scalars=2, flops=work, hbm_in=range(5, 5 + n),
+        scratch=[
+            pltpu.VMEM((n, rows, width), BF16),
+            pltpu.VMEM((cols, rows), BF16),
+            pltpu.SemaphoreType.DMA((n,)),
+        ],
+    )
+    parts = [shift(p, "x", k + 1) for k, p in enumerate(parts)]
+    cross, turned = call(
+        functools.partial(k_cross, scale),
+        [((ny, rows, width), BF16), ((rows, cols), BF16)],
+        there, adjoint, centroids,
+        limit=LARGE, scalars=1, flops=work // 2, hbm_in=(2,),
+        scratch=[pltpu.VMEM((cols, depth), BF16), pltpu.SemaphoreType.DMA],
     )
     cross = shift(cross, "core", 1)
-    (parts,) = call(
-        functools.partial(k_cent, scale, nx),
-        [((nx, nz, cols // nprog, depth), BF16)],
-        adjoint, whole,
-        limit=LARGE, flops=2 * rows * cols * depth,
-    )
-    both = [keep[k] + cross[k].astype(F32) for k in range(ny)]
-    moved = [shift(both[k].astype(BF16), "y", k) for k in range(1, ny)]
-    parts = lax.all_to_all(parts, "x", 0, 0, tiled=True)
-    parts = jnp.sum(parts.astype(F32), axis=0).astype(BF16)
+    own, *moved = call(
+        functools.partial(k_pair, scale),
+        [((rows, width), F32)] + [((rows, width), BF16)] * (ny - 1),
+        here, turned, centroids, cross,
+        limit=LARGE, scalars=1, flops=work // 2, hbm_in=(2, 3),
+        scratch=[
+            pltpu.VMEM((cols, depth), BF16),
+            pltpu.VMEM((ny, rows, width), BF16),
+            pltpu.SemaphoreType.DMA((2,)),
+        ],
+    )
+    near, own = lax.optimization_barrier((near, own))
+    moved = [shift(m, "y", k + 1) for k, m in enumerate(moved)]
+    (parts,) = call(k_add, [((nz, per // nz, depth), BF16)], near, *parts, limit=LARGE)
     parts = lax.all_to_all(parts, "z", 0, 0, tiled=True)
-    centroid_grad = jnp.sum(parts.astype(F32), axis=0).astype(BF16)
-    embed_grad = both[0]
-    for m in moved:
-        embed_grad = embed_grad + m.astype(F32)
-    return embed_grad.astype(BF16), centroid_grad
+    (centroid_grad,) = call(k_sum, [((per // nz, depth), BF16)], parts, limit=LARGE)
+    (embed_grad,) = call(k_add, [((rows, width), BF16)], own, *moved, limit=LARGE)
+    return embed_grad, centroid_grad
 
 
 def solution(mesh):

time: 293 us -> 288 us (0.983)
  blocking collectives: 162 us -> 135 us
  Pallas kernels: 19.2 us -> 33.5 us
  starting transfers between devices: 29.4 us -> 38.5 us
  waiting for transfers between devices: 62 us -> 70.2 us
  other arithmetic: 8 us -> 0.23 us
    all_to_all x1 -> x0, blocking collectives: 28.6 us -> none  [shards(): parts = lax.all_to_all(parts, 'x', 0, 0, tiled=True)]
    ppermute x11 -> x14, waiting for transfers between devices: 33.5 us -> 54.1 us  [shift(): return lax.ppermute(value, axis, [(i, (i + step) % n) for i in range(n)])]
    pallas_call x17 -> x23, Pallas kernels: 19.2 us -> 33.5 us  [call(): pl.pallas_call(body, out_shape=[jax.ShapeDtypeStruct(s, d) for s, d in ou...]
    all_to_all x1, waiting for transfers between devices: 11.6 us -> 0.01 us  [shards(): parts = lax.all_to_all(parts, 'z', 0, 0, tiled=True)]
    ppermute x11 -> x14, starting transfers between devices: 11.7 us -> 20.8 us  [shift(): return lax.ppermute(value, axis, [(i, (i + step) % n) for i in range(n)])]
    convert_element_type x2 -> x0, other arithmetic: 5.9 us -> none  [the longest x1 3.45 us: shards(): moved = [shift(both[k].astype(BF16), 'y', k) for k in range(1, ny)]]
    unnamed x13 -> x32, local copies, waits for them, and re-layouts: 9.7 us -> 7.96 us
  transfers between devices with their start and end apart: 15 -> 18, of which waited for: 8 -> 13; matrix products, arithmetic and copies ran while one was open for 2% -> 0% of each run, Pallas kernels for 1% -> 2%
where the time goes in v2:
time: 288 us; the launch traced here: 286 us
  blocking collectives  135 us (47%)
  waiting for transfers between devices  70.2 us (24%)
  starting transfers between devices  38.5 us (13%)
  Pallas kernels  33.5 us (12%)
  local copies, waits for them, and re-layouts  8.05 us (3%)
    all_to_all x6, blocking collectives, over_prog(): return lax.all_to_all(send, ('z', 'x'), 0, 0, tiled=True)  80 us
    all_to_all x6, blocking collectives, over_clus(): return lax.all_to_all(send, ('y', 'core'), 0, 0, tiled=True)  54.8 us
    ppermute x14, waiting for transfers between devices, shift(): return lax.ppermute(value, axis, [(i, (i + step) % n) for i in range(n)])  54.1 us
    pallas_call x23, Pallas kernels, call(): pl.pallas_call(body, out_shape=[jax.ShapeDtypeStruct(s, d) for s, d in ou...  33.5 us
    ppermute x14, starting transfers between devices, shift(): return lax.ppermute(value, axis, [(i, (i + step) % n) for i in range(n)])  20.8 us
    all_to_all x2, starting transfers between devices, over_clus(): return lax.all_to_all(send, ('y', 'core'), 0, 0, tiled=True)  10.3 us
    all_to_all x1, waiting for transfers between devices, over_prog(): return lax.all_to_all(send, ('z', 'x'), 0, 0, tiled=True)  8.75 us
    unnamed x32, local copies, waits for them, and re-layouts  7.96 us
  transfers between devices with their start and end apart: 18, of which 13 were waited for; matrix products, arithmetic and copies ran while one was open for 0% of the time, Pallas kernels for 2%

profile of v2, /device:TPU:1, one launch (start us, length us, event | category | flops | bytes accessed | tf_op | source)
XLA Modules:
  0.0 286.1 jit_solution(3549692552787288857)
XLA Ops:
  0.6 3.8 %collective-permute-start.1 = (bf16[1024,256]{1,0:T(8,128)(2,1)}, bf16[1024,256]{1,0:T(8,128)(2,1)}, u32[]{:S(2)}, u32[]{:S(2)}) collective-permute-start(bf16[1024,256]{1,0:T(8,128)(2,1)} %refs_0_.1), channel_id=1, source_target_pairs={{0,4},{2,6},{4,0},{6,2},{1,5},{3,7},{5,1},{7,3},{8,12},{10,14},{12... | collective-permute-start | bytes 1572872 | tf_op jit(solution)/shard_map/ppermute | solution.py:307
  4.9 2.3 collective-permute-start.2
  7.1 1.5 collective-permute-start.3
  8.7 6.8 %collective-permute-done.1.refs_2_ = bf16[1024,256]{1,0:T(8,128)(2,1)} collective-permute-done((bf16[1024,256]{1,0:T(8,128)(2,1)}, bf16[1024,256]{1,0:T(8,128)(2,1)}, u32[]{:S(2)}, u32[]{:S(2)}) %collective-permute-start.1) | collective-permute-done | bytes 524320 | tf_op jit(solution)/shard_map/ppermute | solution.py:307
  15.5 5.1 %collective-permute-start.5 = (bf16[1024,256]{1,0:T(8,128)(2,1)}, bf16[1024,256]{1,0:T(8,128)(2,1)}, u32[]{:S(2)}, u32[]{:S(2)}) collective-permute-start(bf16[1024,256]{1,0:T(8,128)(2,1)} %collective-permute-done.1.refs_2_), channel_id=1, source_target_pairs={{0,1},{1,0},{2,3},{3,2},{4,5},{5,4},{6,7},{7,6},{8,9},{9,8},{10,11... | collective-permute-start | bytes 1572872 | tf_op jit(solution)/shard_map/ppermute | solution.py:307
  20.6 7.8 %collective-permute-done.refs_1_ = bf16[1024,256]{1,0:T(8,128)(2,1)} collective-permute-done((bf16[1024,256]{1,0:T(8,128)(2,1)}, bf16[1024,256]{1,0:T(8,128)(2,1)}, u32[]{:S(2)}, u32[]{:S(2)}) %collective-permute-start) | collective-permute-done | bytes 524320 | tf_op jit(solution)/shard_map/ppermute | solution.py:307
  29.3 1.2 copy-done.5
  31.5 1.0 copy-done.8
  32.6 5.4 %shard_map.51 = (f32[512,1024]{1,0:T(8,128)S(1)}, f32[8,2,8,128]{3,2,1,0:T(8,128)S(1)}) custom-call(s32[8]{0:T(128)S(1)} %stack.68.where, bf16[512,2048]{1,0:T(8,128)(2,1)S(1)} %copy-done, bf16[1024,256]{1,0:T(8,128)(2,1)S(1)} %copy-done.8, bf16[1024,256]{1,0:T(8,128)(2,1)} %collective-permute-done.refs_1_, ...), custom_call_target="tpu_custom_call" | custom-call | flops 2147483648 | bytes 6291488 | tf_op jit(solution)/shard_map/pallas_call | solution.py:293
  38.0 8.8 %all_to_all.80.recv = f32[8,2,8,128]{3,2,1,0:T(8,128)S(1)} all-to-all(f32[8,2,8,128]{3,2,1,0:T(8,128)S(1)} %get-tuple-element.53), channel_id=1, replica_groups=mesh['z'=8,'x'=4,'y'=4,'core'=2] {'y','core'}, dimensions={0} | all-to-all | bytes 131072 | tf_op jit(solution)/shard_map/all_to_all | solution.py:329
  47.3 20.2 %all_to_all.81.recv = f32[32,2,4,128]{3,2,1,0:T(4,128)S(1)} all-to-all(f32[32,2,4,128]{3,2,1,0:T(4,128)S(1)} %get-tuple-element.55), channel_id=1, replica_groups=mesh['z'=8,'x'=4,'y'=4,'core'=2] {'z','x'}, dimensions={0} | all-to-all | bytes 262144 | tf_op jit(solution)/shard_map/all_to_all | solution.py:332
  68.0 9.3 %all_to_all.82.recv = f32[8,8,128]{2,1,0:T(8,128)S(1)} all-to-all(f32[8,8,128]{2,1,0:T(8,128)S(1)} %get-tuple-element.59), channel_id=1, replica_groups=mesh['z'=8,'x'=4,'y'=4,'core'=2] {'y','core'}, dimensions={0} | all-to-all | bytes 65536 | tf_op jit(solution)/shard_map/all_to_all | solution.py:329
  77.5 11.8 %all_to_all.83.recv = f32[32,4,128]{2,1,0:T(4,128)S(1)} all-to-all(f32[32,4,128]{2,1,0:T(4,128)S(1)} %get-tuple-element.61), channel_id=1, replica_groups=mesh['z'=8,'x'=4,'y'=4,'core'=2] {'z','x'}, dimensions={0} | all-to-all | bytes 131072 | tf_op jit(solution)/shard_map/all_to_all | solution.py:332
  89.6 9.2 %all_to_all.84.recv = f32[8,8,128]{2,1,0:T(8,128)S(1)} all-to-all(f32[8,8,128]{2,1,0:T(8,128)S(1)} %get-tuple-element.62), channel_id=1, replica_groups=mesh['z'=8,'x'=4,'y'=4,'core'=2] {'y','core'}, dimensions={0} | all-to-all | bytes 65536 | tf_op jit(solution)/shard_map/all_to_all | solution.py:329
  99.1 11.8 %all_to_all.85.recv = f32[32,4,128]{2,1,0:T(4,128)S(1)} all-to-all(f32[32,4,128]{2,1,0:T(4,128)S(1)} %get-tuple-element.64), channel_id=1, replica_groups=mesh['z'=8,'x'=4,'y'=4,'core'=2] {'z','x'}, dimensions={0} | all-to-all | bytes 131072 | tf_op jit(solution)/shard_map/all_to_all | solution.py:332
  111.2 9.1 %all_to_all.86.recv = f32[8,8,128]{2,1,0:T(8,128)S(1)} all-to-all(f32[8,8,128]{2,1,0:T(8,128)S(1)} %get-tuple-element.65), channel_id=1, replica_groups=mesh['z'=8,'x'=4,'y'=4,'core'=2] {'y','core'}, dimensions={0} | all-to-all | bytes 65536 | tf_op jit(solution)/shard_map/all_to_all | solution.py:329
  120.7 12.4 %all_to_all.87.recv = f32[32,2,4,128]{3,2,1,0:T(4,128)S(1)} all-to-all(f32[32,2,4,128]{3,2,1,0:T(4,128)S(1)} %get-tuple-element.69), channel_id=1, replica_groups=mesh['z'=8,'x'=4,'y'=4,'core'=2] {'z','x'}, dimensions={0} | all-to-all | bytes 262144 | tf_op jit(solution)/shard_map/all_to_all | solution.py:332
  133.6 9.4 %all_to_all.88.recv = f32[8,8,128]{2,1,0:T(8,128)S(1)} all-to-all(f32[8,8,128]{2,1,0:T(8,128)S(1)} %get-tuple-element.71), channel_id=1, replica_groups=mesh['z'=8,'x'=4,'y'=4,'core'=2] {'y','core'}, dimensions={0} | all-to-all | bytes 65536 | tf_op jit(solution)/shard_map/all_to_all | solution.py:329
  143.2 11.9 %all_to_all.89.recv = f32[32,4,128]{2,1,0:T(4,128)S(1)} all-to-all(f32[32,4,128]{2,1,0:T(4,128)S(1)} %get-tuple-element.72), channel_id=1, replica_groups=mesh['z'=8,'x'=4,'y'=4,'core'=2] {'z','x'}, dimensions={0} | all-to-all | bytes 131072 | tf_op jit(solution)/shard_map/all_to_all | solution.py:332
  155.4 9.0 %all_to_all.90.recv = f32[8,8,128]{2,1,0:T(8,128)S(1)} all-to-all(f32[8,8,128]{2,1,0:T(8,128)S(1)} %get-tuple-element.73), channel_id=1, replica_groups=mesh['z'=8,'x'=4,'y'=4,'core'=2] {'y','core'}, dimensions={0} | all-to-all | bytes 65536 | tf_op jit(solution)/shard_map/all_to_all | solution.py:329
  164.6 11.8 %all_to_all.91.recv = f32[32,4,128]{2,1,0:T(4,128)S(1)} all-to-all(f32[32,4,128]{2,1,0:T(4,128)S(1)} %get-tuple-element.74), channel_id=1, replica_groups=mesh['z'=8,'x'=4,'y'=4,'core'=2] {'z','x'}, dimensions={0} | all-to-all | bytes 131072 | tf_op jit(solution)/shard_map/all_to_all | solution.py:332
  176.4 0.9 shard_map.63
  177.3 5.2 %all-to-all-start.12 = ((f32[8,8,128]{2,1,0:T(8,128)}), f32[8,8,128]{2,1,0:T(8,128)S(1)}, u32[]{:S(2)}, u32[]{:S(2)}) async-start(f32[8,8,128]{2,1,0:T(8,128)} %get-tuple-element.75), calls=%async_computation.12 | async-start | bytes 65536 | tf_op jit(solution)/shard_map/all_to_all | solution.py:329
  182.5 4.7 %all-to-all-done.12.recv = f32[8,8,128]{2,1,0:T(8,128)S(1)} async-done(((f32[8,8,128]{2,1,0:T(8,128)}), f32[8,8,128]{2,1,0:T(8,128)S(1)}, u32[]{:S(2)}, u32[]{:S(2)}) %all-to-all-start.12) | async-done | bytes 32800 | tf_op jit(solution)/shard_map/all_to_all | solution.py:329
  187.3 0.9 shard_map.64
  188.1 3.9 %all-to-all-start.13 = ((f32[32,4,128]{2,1,0:T(4,128)}), f32[32,4,128]{2,1,0:T(4,128)S(1)}, u32[]{:S(2)}, u32[]{:S(2)}) async-start(f32[32,4,128]{2,1,0:T(4,128)} %get-tuple-element.76), calls=%async_computation.13 | async-start | bytes 131072 | tf_op jit(solution)/shard_map/all_to_all | solution.py:332
  192.1 8.7 %all-to-all-done.13.recv = f32[32,4,128]{2,1,0:T(4,128)S(1)} async-done(((f32[32,4,128]{2,1,0:T(4,128)}), f32[32,4,128]{2,1,0:T(4,128)S(1)}, u32[]{:S(2)}, u32[]{:S(2)}) %all-to-all-start.13) | async-done | bytes 65568 | tf_op jit(solution)/shard_map/all_to_all | solution.py:332
  200.9 0.9 shard_map.65
  201.8 5.1 %all-to-all-start.14 = ((f32[8,8,128]{2,1,0:T(8,128)}), f32[8,8,128]{2,1,0:T(8,128)S(1)}, u32[]{:S(2)}, u32[]{:S(2)}) async-start(f32[8,8,128]{2,1,0:T(8,128)} %get-tuple-element.86), calls=%async_computation.14 | async-start | bytes 65536 | tf_op jit(solution)/shard_map/all_to_all | solution.py:329
  206.8 2.2 shard_map.66
  209.0 2.5 all-to-all-done.14.recv
  211.6 1.0 copy-done.9
  212.6 8.1 %shard_map.67 = (bf16[512,1024]{1,0:T(8,128)(2,1)S(1)}, f32[128,2048]{1,0:T(8,128)S(1)}, bf16[128,2048]{1,0:T(8,128)(2,1)}, bf16[128,2048]{1,0:T(8,128)(2,1)}, bf16[128,2048]{1,0:T(8,128)(2,1)}) custom-call(s32[8]{0:T(128)S(1)} %stack.68.where, s32[4]{0:T(128)S(1)} %pad_add_fusion.order, f32[512,1024]{1,0:T(8,128)S(1)} %get-tuple-element.84.base, ...), custom_call_target="tpu_custom_call" | custom-call | flops 2147483648 | bytes 7372848 | tf_op jit(solution)/shard_map/pallas_call | solution.py:293
  220.8 3.6 %shard_map.68 = (bf16[4,1024,256]{2,1,0:T(8,128)(2,1)}, bf16[1024,512]{1,0:T(8,128)(2,1)S(1)}) custom-call(s32[4]{0:T(128)S(1)} %pad_add_fusion.2.where, bf16[512,1024]{1,0:T(8,128)(2,1)S(1)} %get-tuple-element.88.adjoint, bf16[512,2048]{1,0:T(8,128)(2,1)S(1)} %copy-done.1), custom_call_target="tpu_custom_call" | custom-call | flops 1073741824 | bytes 3145744 | tf_op jit(solution)/shard_map/pallas_call | solution.py:293
  224.4 1.0 copy-done.6
  226.3 2.1 collective-permute-start.12
  229.3 1.0 collective-permute-done.7.cross_hbm
  230.3 1.2 copy-done.7
  231.5 3.6 %shard_map.69 = (f32[1024,256]{1,0:T(8,128)S(1)}, bf16[1024,256]{1,0:T(8,128)(2,1)S(1)}, bf16[1024,256]{1,0:T(8,128)(2,1)S(1)}, bf16[1024,256]{1,0:T(8,128)(2,1)S(1)}) custom-call(s32[4]{0:T(128)S(1)} %pad_add_fusion.1.where, bf16[1024,512]{1,0:T(8,128)(2,1)S(1)} %copy-done.7, bf16[512,2048]{1,0:T(8,128)(2,1)S(1)} %copy-done.2, ...), custom_call_target="tpu_custom_call" | custom-call | flops 1073741824 | bytes 5242896 | tf_op jit(solution)/shard_map/pallas_call | solution.py:293
  237.5 4.0 %collective-permute-done.11.refs_0_ = bf16[128,2048]{1,0:T(8,128)(2,1)} collective-permute-done((bf16[128,2048]{1,0:T(8,128)(2,1)}, bf16[128,2048]{1,0:T(8,128)(2,1)}, u32[]{:S(2)}, u32[]{:S(2)}) %collective-permute-start.11) | collective-permute-done | bytes 524320 | tf_op jit(solution)/shard_map/ppermute | solution.py:307
  241.6 10.4 %collective-permute-done.12.refs_1_ = bf16[128,2048]{1,0:T(8,128)(2,1)} collective-permute-done((bf16[128,2048]{1,0:T(8,128)(2,1)}, bf16[128,2048]{1,0:T(8,128)(2,1)}, u32[]{:S(2)}, u32[]{:S(2)}) %collective-permute-start.12) | collective-permute-done | bytes 524320 | tf_op jit(solution)/shard_map/ppermute | solution.py:307
  252.7 2.4 shard_map.71
  255.1 3.5 %all-to-all-start.15 = ((bf16[8,16,2048]{2,1,0:T(8,128)(2,1)}), bf16[8,16,2048]{2,1,0:T(8,128)(2,1)S(1)}, u32[]{:S(2)}, u32[]{:S(2)}) async-start(bf16[8,16,2048]{2,1,0:T(8,128)(2,1)} %shard_map.71), calls=%async_computation.15 | async-start | bytes 1048576 | tf_op jit(solution)/shard_map/all_to_all | solution.py:431
  259.0 1.8 collective-permute-start.9
  261.6 11.3 %collective-permute-done.8.refs_0_ = bf16[1024,256]{1,0:T(8,128)(2,1)S(1)} collective-permute-done((bf16[1024,256]{1,0:T(8,128)(2,1)S(1)}, bf16[1024,256]{1,0:T(8,128)(2,1)S(1)}, u32[]{:S(2)}, u32[]{:S(2)}) %collective-permute-start.8) | collective-permute-done | bytes 524320 | tf_op jit(solution)/shard_map/ppermute | solution.py:307
  272.8 10.1 %collective-permute-done.9.refs_1_ = bf16[1024,256]{1,0:T(8,128)(2,1)S(1)} collective-permute-done((bf16[1024,256]{1,0:T(8,128)(2,1)S(1)}, bf16[1024,256]{1,0:T(8,128)(2,1)S(1)}, u32[]{:S(2)}, u32[]{:S(2)}) %collective-permute-start.9) | collective-permute-done | bytes 524320 | tf_op jit(solution)/shard_map/ppermute | solution.py:307
  282.9 1.5 collective-permute-done.10.refs_2_
  284.4 1.0 shard_map.70
  (60 shorter events, 12.9 us)
Async XLA Ops:
  0.6 30.9 %copy-start = (bf16[512,2048]{1,0:T(8,128)(2,1)S(1)}, bf16[512,2048]{1,0:T(8,128)(2,1)}, u32[]{:S(2)}) copy-start(bf16[512,2048]{1,0:T(8,128)(2,1)} %cent_hbm.3) | copy-start | bytes 6291460
  0.6 14.8 %collective-permute-start.1 = (bf16[1024,256]{1,0:T(8,128)(2,1)}, bf16[1024,256]{1,0:T(8,128)(2,1)}, u32[]{:S(2)}, u32[]{:S(2)}) collective-permute-start(bf16[1024,256]{1,0:T(8,128)(2,1)} %refs_0_.1), channel_id=1, source_target_pairs={{0,4},{2,6},{4,0},{6,2},{1,5},{3,7},{5,1},{7,3},{8,12},{10,14},{12... | collective-permute-start | bytes 1572872 | tf_op jit(solution)/shard_map/ppermute | solution.py:307
  4.5 23.9 %collective-permute-start = (bf16[1024,256]{1,0:T(8,128)(2,1)}, bf16[1024,256]{1,0:T(8,128)(2,1)}, u32[]{:S(2)}, u32[]{:S(2)}) collective-permute-start(bf16[1024,256]{1,0:T(8,128)(2,1)} %refs_0_.1), channel_id=1, source_target_pairs={{0,2},{2,4},{4,6},{6,0},{1,3},{3,5},{5,7},{7,1},{8,10},{10,12},{12... | collective-permute-start | bytes 1572872 | tf_op jit(solution)/shard_map/ppermute | solution.py:307
  4.9 24.0 %collective-permute-start.2 = (bf16[1024,256]{1,0:T(8,128)(2,1)}, bf16[1024,256]{1,0:T(8,128)(2,1)}, u32[]{:S(2)}, u32[]{:S(2)}) collective-permute-start(bf16[1024,256]{1,0:T(8,128)(2,1)} %refs_0_.1), channel_id=1, source_target_pairs={{0,6},{2,0},{4,2},{6,4},{1,7},{3,1},{5,3},{7,5},{8,14},{10,8},{12,... | collective-permute-start | bytes 1572872 | tf_op jit(solution)/shard_map/ppermute | solution.py:307
  7.1 23.9 %collective-permute-start.3 = (bf16[1024,256]{1,0:T(8,128)(2,1)}, bf16[1024,256]{1,0:T(8,128)(2,1)}, u32[]{:S(2)}, u32[]{:S(2)}) collective-permute-start(bf16[1024,256]{1,0:T(8,128)(2,1)} %refs_0_.1), channel_id=1, source_target_pairs={{0,1},{1,0},{2,3},{3,2},{4,5},{5,4},{6,7},{7,6},{8,9},{9,8},{10,11... | collective-permute-start | bytes 1572872 | tf_op jit(solution)/shard_map/ppermute | solution.py:307
  15.5 15.5 %collective-permute-start.5 = (bf16[1024,256]{1,0:T(8,128)(2,1)}, bf16[1024,256]{1,0:T(8,128)(2,1)}, u32[]{:S(2)}, u32[]{:S(2)}) collective-permute-start(bf16[1024,256]{1,0:T(8,128)(2,1)} %collective-permute-done.1.refs_2_), channel_id=1, source_target_pairs={{0,1},{1,0},{2,3},{3,2},{4,5},{5,4},{6,7},{7,6},{8,9},{9,8},{10,11... | collective-permute-start | bytes 1572872 | tf_op jit(solution)/shard_map/ppermute | solution.py:307
  28.4 2.6 collective-permute-start.4
  28.9 2.6 collective-permute-start.6
  29.3 1.2 copy-start.5
  31.5 1.0 copy-start.8
  177.3 9.9 %all-to-all-start.12 = ((f32[8,8,128]{2,1,0:T(8,128)}), f32[8,8,128]{2,1,0:T(8,128)S(1)}, u32[]{:S(2)}, u32[]{:S(2)}) async-start(f32[8,8,128]{2,1,0:T(8,128)} %get-tuple-element.75), calls=%async_computation.12 | async-start | bytes 65536 | tf_op jit(solution)/shard_map/all_to_all | solution.py:329
  188.1 12.8 %all-to-all-start.13 = ((f32[32,4,128]{2,1,0:T(4,128)}), f32[32,4,128]{2,1,0:T(4,128)S(1)}, u32[]{:S(2)}, u32[]{:S(2)}) async-start(f32[32,4,128]{2,1,0:T(4,128)} %get-tuple-element.76), calls=%async_computation.13 | async-start | bytes 131072 | tf_op jit(solution)/shard_map/all_to_all | solution.py:332
  201.8 9.8 %all-to-all-start.14 = ((f32[8,8,128]{2,1,0:T(8,128)}), f32[8,8,128]{2,1,0:T(8,128)S(1)}, u32[]{:S(2)}, u32[]{:S(2)}) async-start(f32[8,8,128]{2,1,0:T(8,128)} %get-tuple-element.86), calls=%async_computation.14 | async-start | bytes 65536 | tf_op jit(solution)/shard_map/all_to_all | solution.py:329
  211.6 1.0 copy-start.9
  212.6 8.1 %copy-start.1 = (bf16[512,2048]{1,0:T(8,128)(2,1)S(1)}, bf16[512,2048]{1,0:T(8,128)(2,1)}, u32[]{:S(2)}) copy-start(bf16[512,2048]{1,0:T(8,128)(2,1)} %cent_hbm.3) | copy-start | bytes 6291460
  220.7 3.7 %copy-start.3 = (f32[128,2048]{1,0:T(8,128)}, f32[128,2048]{1,0:T(8,128)S(1)}, u32[]{:S(2)}) copy-start(f32[128,2048]{1,0:T(8,128)S(1)} %get-tuple-element.96.first) | copy-start | bytes 3145732
  220.8 9.5 %copy-start.2 = (bf16[512,2048]{1,0:T(8,128)(2,1)S(1)}, bf16[512,2048]{1,0:T(8,128)(2,1)}, u32[]{:S(2)}) copy-start(bf16[512,2048]{1,0:T(8,128)(2,1)} %cent_hbm.3) | copy-start | bytes 6291460
  224.4 1.0 copy-start.6
  225.4 4.9 %collective-permute-start.7 = (bf16[4,1024,256]{2,1,0:T(8,128)(2,1)}, bf16[4,1024,256]{2,1,0:T(8,128)(2,1)}, u32[]{:S(2)}, u32[]{:S(2)}) collective-permute-start(bf16[4,1024,256]{2,1,0:T(8,128)(2,1)} %get-tuple-element.90), channel_id=1, source_target_pairs={{0,1},{1,0},{2,3},{3,2},{4,5},{5,4},{6,7},{7,6},{8,9},{9,8},{10,11... | collective-permute-start | bytes 6291464 | tf_op jit(solution)/shard_map/ppermute | solution.py:307
  226.1 15.4 %collective-permute-start.11 = (bf16[128,2048]{1,0:T(8,128)(2,1)}, bf16[128,2048]{1,0:T(8,128)(2,1)}, u32[]{:S(2)}, u32[]{:S(2)}) collective-permute-start(bf16[128,2048]{1,0:T(8,128)(2,1)} %get-tuple-element.97), channel_id=1, source_target_pairs={{0,8},{8,16},{16,24},{24,0},{1,9},{9,17},{17,25},{25,1},{2,10},{10... | collective-permute-start | bytes 1572872 | tf_op jit(solution)/shard_map/ppermute | solution.py:307
  226.3 25.7 %collective-permute-start.12 = (bf16[128,2048]{1,0:T(8,128)(2,1)}, bf16[128,2048]{1,0:T(8,128)(2,1)}, u32[]{:S(2)}, u32[]{:S(2)}) collective-permute-start(bf16[128,2048]{1,0:T(8,128)(2,1)} %get-tuple-element.98), channel_id=1, source_target_pairs={{0,16},{8,24},{16,0},{24,8},{1,17},{9,25},{17,1},{25,9},{2,18},{10... | collective-permute-start | bytes 1572872 | tf_op jit(solution)/shard_map/ppermute | solution.py:307
  228.4 24.3 %collective-permute-start.13 = (bf16[128,2048]{1,0:T(8,128)(2,1)}, bf16[128,2048]{1,0:T(8,128)(2,1)}, u32[]{:S(2)}, u32[]{:S(2)}) collective-permute-start(bf16[128,2048]{1,0:T(8,128)(2,1)} %get-tuple-element.99), channel_id=1, source_target_pairs={{0,24},{8,0},{16,8},{24,16},{1,25},{9,1},{17,9},{25,17},{2,26},{10... | collective-permute-start | bytes 1572872 | tf_op jit(solution)/shard_map/ppermute | solution.py:307
  230.3 1.2 copy-start.7
  231.5 21.2 %copy-start.4 = (f32[128,2048]{1,0:T(8,128)S(1)}, f32[128,2048]{1,0:T(8,128)}, u32[]{:S(2)}) copy-start(f32[128,2048]{1,0:T(8,128)} %copy-done.3) | copy-start | bytes 3145732
  235.1 0.8 copy-start.10
  235.9 0.8 copy-start.12
  236.7 0.8 copy-start.14
  237.5 21.1 %copy-start.15 = (bf16[1024,256]{1,0:T(8,128)(2,1)S(1)}, bf16[1024,256]{1,0:T(8,128)(2,1)}, u32[]{:S(2)}) copy-start(bf16[1024,256]{1,0:T(8,128)(2,1)} %copy-done.14) | copy-start | bytes 1572868
  237.5 21.4 %copy-start.13 = (bf16[1024,256]{1,0:T(8,128)(2,1)S(1)}, bf16[1024,256]{1,0:T(8,128)(2,1)}, u32[]{:S(2)}) copy-start(bf16[1024,256]{1,0:T(8,128)(2,1)} %copy-done.12) | copy-start | bytes 1572868
  237.5 23.2 %copy-start.11 = (bf16[1024,256]{1,0:T(8,128)(2,1)S(1)}, bf16[1024,256]{1,0:T(8,128)(2,1)}, u32[]{:S(2)}) copy-start(bf16[1024,256]{1,0:T(8,128)(2,1)} %copy-done.10) | copy-start | bytes 1572868
  255.1 30.3 %all-to-all-start.15 = ((bf16[8,16,2048]{2,1,0:T(8,128)(2,1)}), bf16[8,16,2048]{2,1,0:T(8,128)(2,1)S(1)}, u32[]{:S(2)}, u32[]{:S(2)}) async-start(bf16[8,16,2048]{2,1,0:T(8,128)(2,1)} %shard_map.71), calls=%async_computation.15 | async-start | bytes 1048576 | tf_op jit(solution)/shard_map/all_to_all | solution.py:431
  258.6 14.2 %collective-permute-start.8 = (bf16[1024,256]{1,0:T(8,128)(2,1)S(1)}, bf16[1024,256]{1,0:T(8,128)(2,1)S(1)}, u32[]{:S(2)}, u32[]{:S(2)}) collective-permute-start(bf16[1024,256]{1,0:T(8,128)(2,1)S(1)} %copy-done.15), channel_id=1, source_target_pairs={{0,2},{2,4},{4,6},{6,0},{1,3},{3,5},{5,7},{7,1},{8,10},{10,12},{12... | collective-permute-start | bytes 1572872 | tf_op jit(solution)/shard_map/ppermute | solution.py:307
  259.0 23.9 %collective-permute-start.9 = (bf16[1024,256]{1,0:T(8,128)(2,1)S(1)}, bf16[1024,256]{1,0:T(8,128)(2,1)S(1)}, u32[]{:S(2)}, u32[]{:S(2)}) collective-permute-start(bf16[1024,256]{1,0:T(8,128)(2,1)S(1)} %copy-done.13), channel_id=1, source_target_pairs={{0,4},{2,6},{4,0},{6,2},{1,5},{3,7},{5,1},{7,3},{8,12},{10,14},{12... | collective-permute-start | bytes 1572872 | tf_op jit(solution)/shard_map/ppermute | solution.py:307
  260.7 23.6 %collective-permute-start.10 = (bf16[1024,256]{1,0:T(8,128)(2,1)S(1)}, bf16[1024,256]{1,0:T(8,128)(2,1)S(1)}, u32[]{:S(2)}, u32[]{:S(2)}) collective-permute-start(bf16[1024,256]{1,0:T(8,128)(2,1)S(1)} %copy-done.11), channel_id=1, source_target_pairs={{0,6},{2,0},{4,2},{6,4},{1,7},{3,1},{5,3},{7,5},{8,14},{10,8},{12,... | collective-permute-start | bytes 1572872 | tf_op jit(solution)/shard_map/ppermute | solution.py:307

commit v3 on v2

--- a/solution.py
+++ b/solution.py
@@ -68,20 +68,25 @@
     grad[...] = plan_grad[...].T
 
 
-def k_logits(scale, where, cent, *refs):
-    n = len(refs) - 4
-    pieces, (logits, send, held, sems) = refs[:n], refs[n:]
-    width = pieces[0].shape[1]
-    copies = [
-        pltpu.make_async_copy(
-            piece, held.at[:, pl.ds(pl.multiple_of(where[k] * width, L), width)], sems.at[k]
-        )
-        for k, piece in enumerate(pieces)
-    ]
-    for c in copies:
-        c.start()
-    for c in copies:
-        c.wait()
+def source(ny, k):
+    core = lax.axis_index("core") if k < ny else 1 - lax.axis_index("core")
+    return lax.rem(lax.axis_index("y") + (ny - k % ny), ny) * 2 + core
+
+
+def target(ny, k, cross):
+    core = 1 - lax.axis_index("core") if cross else lax.axis_index("core")
+    return lax.rem(lax.axis_index("y") + k, ny) * 2 + core
+
+
+def span(at, width):
+    return pl.ds(pl.multiple_of(at * width, L), width)
+
+
+def k_logits(scale, cent, *refs):
+    n = len(refs) - 3
+    pieces, (logits, send, held) = refs[:n], refs[n:]
+    for k, piece in enumerate(pieces):
+        held[:, span(source(n // 2, k), piece.shape[1])] = piece[...]
     logits[...] = scale * lax.dot_general(cent[...], held[...], NT, preferred_element_type=F32)
     count = logits.shape[1] // L
     tops, sums = [], []
@@ -179,9 +184,11 @@
     send[...] = jnp.broadcast_to(gather_cols(weighted(weights, y))[None], send.shape)
 
 
-def k_back_row(ratio, weights, col_mul, recv, col_adj, send):
-    b = col_mul[...]
-    x = -b * b * total(recv) / ratio
+def k_back_row(ratio, weights, *refs):
+    *col_mul, recv, col_adj, send = refs
+    x = total(recv) / -ratio
+    for b in col_mul:
+        x = x * b[...] * b[...]
     col_adj[...] = x
     xx = spread(x)
     count = weights.shape[1] // L
@@ -211,11 +218,9 @@
         base[:, r * L : (r + 1) * L] = tile * inner
 
 
-def k_adjoint(scale, where, order, base, first, recv, *refs):
-    n = where.shape[0]
-    nx = order.shape[0]
+def k_adjoint(scale, n, nx, base, first, recv, *refs):
     pieces, adjoint, keep = refs[:n], refs[n], refs[n + 1]
-    sends, (held, turned, sems) = refs[n + 2 : n + 1 + nx], refs[n + 1 + nx :]
+    sends, (held, turned, stage, sems, out_sems) = refs[n + 2 : n + 1 + nx], refs[n + 1 + nx :]
     copies = [
         pltpu.make_async_copy(piece, held.at[k], sems.at[k]) for k, piece in enumerate(pieces)
     ]
@@ -229,46 +234,59 @@
     per = keep.shape[0]
     group = 16
     for k in range(nx):
+        to = lax.rem(lax.axis_index("x") + k, nx)
         for iz in range(per // group):
-            at = pl.multiple_of((iz * nx + order[k]) * group, group)
+            at = pl.multiple_of((iz * nx + to) * group, group)
             turned[k * per + iz * group : k * per + (iz + 1) * group, :] = adjoint[pl.ds(at, group), :]
     width = held.shape[2]
+    outs = []
     for p in range(n):
         copies[p].wait()
         part = scale * lax.dot_general(turned[...], held[p], NN, preferred_element_type=F32)
-        cols = pl.ds(pl.multiple_of(where[p] * width, L), width)
+        cols = span(source(n // 2, p), width)
         keep[:, cols] = part[:per, :]
         for k in range(1, nx):
-            sends[k - 1][:, cols] = part[k * per : (k + 1) * per, :].astype(BF16)
-
-
-def k_cross(scale, where, adjoint, cent_hbm, cross, turned, cent, sem):
-    copy = pltpu.make_async_copy(cent_hbm, cent, sem)
-    copy.start()
+            stage[p, k - 1] = part[k * per : (k + 1) * per, :].astype(BF16)
+            outs.append(
+                pltpu.make_async_copy(
+                    stage.at[p, k - 1], sends[k - 1].at[:, cols], out_sems.at[p, k - 1]
+                )
+            )
+            outs[-1].start()
+    for c in outs:
+        c.wait()
+
+
+def k_cross(scale, adjoint, cent, cross, turned, stage, sems):
     turned[...] = adjoint[...].T
-    copy.wait()
-    width = cross.shape[2]
-    for k in range(cross.shape[0]):
-        block = cent[:, pl.ds(pl.multiple_of(where[k] * width, L), width)]
+    ny, _, width = cross.shape
+    outs = []
+    for k in range(ny):
+        block = cent[:, span(target(ny, k, True), width)]
         part = scale * lax.dot_general(turned[...], block, NN, preferred_element_type=F32)
-        cross[k] = part.astype(cross.dtype)
-
-
-def k_pair(scale, where, turned, cent_hbm, cross_hbm, first, *refs):
-    rest, (cent, cross, sems) = refs[:-3], refs[-3:]
-    copies = [
-        pltpu.make_async_copy(cent_hbm, cent, sems.at[0]),
-        pltpu.make_async_copy(cross_hbm, cross, sems.at[1]),
-    ]
-    for c in copies:
-        c.start()
-    for c in copies:
+        stage[k] = part.astype(cross.dtype)
+        outs.append(pltpu.make_async_copy(stage.at[k], cross.at[k], sems.at[k]))
+        outs[-1].start()
+    for c in outs:
         c.wait()
-    width = first.shape[1]
-    for k, out in enumerate((first, *rest)):
-        block = cent[:, pl.ds(pl.multiple_of(where[k] * width, L), width)]
+
+
+def k_pair(scale, turned, cent, cross, first, *refs):
+    rest, (stage, sems) = refs[:-2], refs[-2:]
+    ny, _, width = cross.shape
+    outs = []
+    for k in range(ny - 1, -1, -1):
+        block = cent[:, span(target(ny, k, False), width)]
         part = scale * lax.dot_general(turned[...], block, NN, preferred_element_type=F32)
-        out[...] = (part + cross[k].astype(F32)).astype(out.dtype)
+        part = part + cross[k].astype(F32)
+        if k:
+            stage[k - 1] = part.astype(BF16)
+            outs.append(pltpu.make_async_copy(stage.at[k - 1], rest[k - 1], sems.at[k - 1]))
+            outs[-1].start()
+        else:
+            first[...] = part
+    for c in outs:
+        c.wait()
 
 
 def k_add(first, *refs):
@@ -285,16 +303,15 @@
     out[...] = value.astype(BF16)
 
 
-def call(body, outs, *args, limit=SMALL, scalars=0, flops=0, hbm_in=(), alias=None, scratch=()):
+def call(body, outs, *args, limit=SMALL, flops=0, hbm_in=(), hbm_out=(), alias=None, scratch=()):
     spec, far = pl.BlockSpec(memory_space=pltpu.VMEM), pl.BlockSpec(memory_space=pltpu.HBM)
-    smem = pl.BlockSpec(memory_space=pltpu.SMEM)
-    ins = [smem if i < scalars else far if i in hbm_in else spec for i in range(len(args))]
+    ins = [far if i in hbm_in else spec for i in range(len(args))]
     size = sum(a.size * a.dtype.itemsize for a in args)
     return pl.pallas_call(
         body,
         out_shape=[jax.ShapeDtypeStruct(s, d) for s, d in outs],
         in_specs=ins,
-        out_specs=[spec] * len(outs),
+        out_specs=[far if i in hbm_out else spec for i in range(len(outs))],
         input_output_aliases=alias or {},
         scratch_shapes=list(scratch),
         compiler_params=pltpu.CompilerParams(vmem_limit_bytes=limit),
@@ -316,14 +333,12 @@
     ratio = (rows * nprog) / (cols * nclus)
     log_b = math.log(ratio)
     rv, cv = (rows // L, L), (cols // L, L)
-    ix, iy, ic = lax.axis_index("x"), lax.axis_index("y"), lax.axis_index("core")
 
     mine = [embeddings] + [shift(embeddings, "y", k) for k in range(1, ny)]
     theirs = [shift(m, "core", 1) for m in mine]
-    source = [lax.rem(iy - k + ny, ny) * 2 for k in range(ny)]
-    where = jnp.stack([s + ic for s in source] + [s + 1 - ic for s in source]).astype(jnp.int32)
     (grad,) = call(k_prepare, [((cols, rows), BF16)], plan_grad)
     mine[0], grad = lax.optimization_barrier((mine[0], grad))
+    pieces = [*mine, *theirs]
 
     def over_clus(send):
         return lax.all_to_all(send, ("y", "core"), 0, 0, tiled=True)
@@ -336,14 +351,13 @@
     row_pair, col_pair = ((nclus, 2, *rv), F32), ((nprog, 2, *cv), F32)
     a_row, a_col = (rv, F32), (cv, F32)
 
-    pieces = [*mine, *theirs]
+    work = 2 * rows * cols * depth
     logits, send = call(
         functools.partial(k_logits, scale),
         [block, row_pair],
-        where, centroids, *pieces,
-        limit=LARGE, scalars=1, flops=2 * rows * cols * depth,
-        hbm_in=range(2, 2 + len(pieces)),
-        scratch=[pltpu.VMEM((rows, depth), BF16), pltpu.SemaphoreType.DMA((len(pieces),))],
+        centroids, *pieces,
+        limit=LARGE, flops=work,
+        scratch=[pltpu.VMEM((rows, depth), BF16)],
     )
     row_pot, send = call(k_first_col, [a_row, col_pair], logits, over_clus(send))
     col_pot, weights, send = call(
@@ -375,17 +389,12 @@
             weights, row_mul[step - 1], over_clus(send),
         )
         row_adj.insert(0, y)
-        b = col_mul[step - 2] if step > 1 else jnp.ones(cv, F32)
+        b = col_mul[step - 2 : step - 1] if step > 1 else []
         x, send = call(
-            functools.partial(k_back_row, ratio), [a_col, row_send], weights, b, over_prog(send)
+            functools.partial(k_back_row, ratio), [a_col, row_send], weights, *b, over_prog(send)
         )
         col_adj.insert(0, x)
 
-    target = [lax.rem(iy + k, ny) * 2 for k in range(ny)]
-    here = jnp.stack([s + ic for s in target]).astype(jnp.int32)
-    there = jnp.stack([s + 1 - ic for s in target]).astype(jnp.int32)
-    order = jnp.stack([lax.rem(ix + k, nx) for k in range(nx)]).astype(jnp.int32)
-    work = 2 * rows * cols * depth
     recv = over_clus(send)
     base, first = call(
         k_known,
@@ -395,35 +404,34 @@
     )
     per, n = cols // nx, len(pieces)
     adjoint, near, *parts = call(
-        functools.partial(k_adjoint, scale),
+        functools.partial(k_adjoint, scale, n, nx),
         [((cols, rows), BF16), ((per, depth), F32)] + [((per, depth), BF16)] * (nx - 1),
-        where, order, base, first, recv, *pieces,
-        limit=LARGE, scalars=2, flops=work, hbm_in=range(5, 5 + n),
+        base, first, recv,
+        *(pltpu.with_memory_space_constraint(p, pltpu.HBM) for p in pieces),
+        limit=LARGE, flops=work, hbm_in=range(3, 3 + n), hbm_out=range(2, 1 + nx),
         scratch=[
             pltpu.VMEM((n, rows, width), BF16),
             pltpu.VMEM((cols, rows), BF16),
+            pltpu.VMEM((n, nx - 1, per, width), BF16),
             pltpu.SemaphoreType.DMA((n,)),
+            pltpu.SemaphoreType.DMA((n, nx - 1)),
         ],
     )
     parts = [shift(p, "x", k + 1) for k, p in enumerate(parts)]
     cross, turned = call(
         functools.partial(k_cross, scale),
         [((ny, rows, width), BF16), ((rows, cols), BF16)],
-        there, adjoint, centroids,
-        limit=LARGE, scalars=1, flops=work // 2, hbm_in=(2,),
-        scratch=[pltpu.VMEM((cols, depth), BF16), pltpu.SemaphoreType.DMA],
+        adjoint, centroids,
+        limit=LARGE, flops=work // 2, hbm_out=(0,),
+        scratch=[pltpu.VMEM((ny, rows, width), BF16), pltpu.SemaphoreType.DMA((ny,))],
     )
     cross = shift(cross, "core", 1)
     own, *moved = call(
         functools.partial(k_pair, scale),
         [((rows, width), F32)] + [((rows, width), BF16)] * (ny - 1),
-        here, turned, centroids, cross,
-        limit=LARGE, scalars=1, flops=work // 2, hbm_in=(2, 3),
-        scratch=[
-            pltpu.VMEM((cols, depth), BF16),
-            pltpu.VMEM((ny, rows, width), BF16),
-            pltpu.SemaphoreType.DMA((2,)),
-        ],
+        turned, centroids, cross,
+        limit=LARGE, flops=work // 2, hbm_out=range(1, ny),
+        scratch=[pltpu.VMEM((ny - 1, rows, width), BF16), pltpu.SemaphoreType.DMA((ny - 1,))],
     )
     near, own = lax.optimization_barrier((near, own))
     moved = [shift(m, "y", k + 1) for k, m in enumerate(moved)]

time: 288 us -> 277 us (0.962)
  blocking collectives: 135 us -> 155 us
  waiting for transfers between devices: 70.2 us -> 60.3 us
  starting transfers between devices: 38.5 us -> 29.8 us
  Pallas kernels: 33.5 us -> 26.9 us
  local copies, waits for them, and re-layouts: 8.05 us -> 2.59 us
    all_to_all x6 -> x7, blocking collectives: 80 us -> 91.8 us  [over_prog(): return lax.all_to_all(send, ('z', 'x'), 0, 0, tiled=True)]
    all_to_all x6 -> x7, blocking collectives: 54.8 us -> 63.6 us  [over_clus(): return lax.all_to_all(send, ('y', 'core'), 0, 0, tiled=True)]
    all_to_all x1 -> x0, waiting for transfers between devices: 8.75 us -> none  [over_prog(): return lax.all_to_all(send, ('z', 'x'), 0, 0, tiled=True)]
    pallas_call x23, Pallas kernels: 33.5 us -> 26.9 us  [call(): pl.pallas_call(body, out_shape=[jax.ShapeDtypeStruct(s, d) for s, d in ou...]
    unnamed x32 -> x22, local copies, waits for them, and re-layouts: 7.96 us -> 2.59 us
    all_to_all x2 -> x1, starting transfers between devices: 10.3 us -> 5.21 us  [over_clus(): return lax.all_to_all(send, ('y', 'core'), 0, 0, tiled=True)]
    all_to_all x2 -> x1, waiting for transfers between devices: 7.28 us -> 2.54 us  [over_clus(): return lax.all_to_all(send, ('y', 'core'), 0, 0, tiled=True)]
    all_to_all x1 -> x0, starting transfers between devices: 3.86 us -> none  [over_prog(): return lax.all_to_all(send, ('z', 'x'), 0, 0, tiled=True)]
  transfers between devices with their start and end apart: 18 -> 16, of which waited for: 13 -> 11; matrix products, arithmetic and copies ran while one was open for 0% -> 0% of each run, Pallas kernels for 2% -> 2%
where the time goes in v3:
time: 277 us; the launch traced here: 276 us
  blocking collectives  155 us (56%)
  waiting for transfers between devices  60.3 us (22%)
  starting transfers between devices  29.8 us (11%)
  Pallas kernels  26.9 us (10%)
    all_to_all x7, blocking collectives, over_prog(): return lax.all_to_all(send, ('z', 'x'), 0, 0, tiled=True)  91.8 us
    all_to_all x7, blocking collectives, over_clus(): return lax.all_to_all(send, ('y', 'core'), 0, 0, tiled=True)  63.6 us
    ppermute x14, waiting for transfers between devices, shift(): return lax.ppermute(value, axis, [(i, (i + step) % n) for i in range(n)])  57.8 us
    pallas_call x23, Pallas kernels, call(): pl.pallas_call(body, out_shape=[jax.ShapeDtypeStruct(s, d) for s, d in ou...  26.9 us
    ppermute x14, starting transfers between devices, shift(): return lax.ppermute(value, axis, [(i, (i + step) % n) for i in range(n)])  21.1 us
  transfers between devices with their start and end apart: 16, of which 11 were waited for; matrix products, arithmetic and copies ran while one was open for 0% of the time, Pallas kernels for 2%

profile of v3, /device:TPU:1, one launch (start us, length us, event | category | flops | bytes accessed | tf_op | source)
XLA Modules:
  0.0 275.8 jit_solution(7757084922523524257)
XLA Ops:
  0.6 3.8 %collective-permute-start.1 = (bf16[1024,256]{1,0:T(8,128)(2,1)}, bf16[1024,256]{1,0:T(8,128)(2,1)S(1)}, u32[]{:S(2)}, u32[]{:S(2)}) collective-permute-start(bf16[1024,256]{1,0:T(8,128)(2,1)} %refs_0_.1), channel_id=1, source_target_pairs={{0,4},{2,6},{4,0},{6,2},{1,5},{3,7},{5,1},{7,3},{8,12},{10,14},{12... | collective-permute-start | bytes 1572872 | tf_op jit(solution)/shard_map/ppermute | solution.py:324
  4.9 2.3 collective-permute-start.2
  7.1 1.5 collective-permute-start.3
  8.7 6.8 %collective-permute-done.1.refs_2_ = bf16[1024,256]{1,0:T(8,128)(2,1)S(1)} collective-permute-done((bf16[1024,256]{1,0:T(8,128)(2,1)}, bf16[1024,256]{1,0:T(8,128)(2,1)S(1)}, u32[]{:S(2)}, u32[]{:S(2)}) %collective-permute-start.1) | collective-permute-done | bytes 524320 | tf_op jit(solution)/shard_map/ppermute | solution.py:324
  15.5 5.0 %collective-permute-start.5 = (bf16[1024,256]{1,0:T(8,128)(2,1)S(1)}, bf16[1024,256]{1,0:T(8,128)(2,1)S(1)}, u32[]{:S(2)}, u32[]{:S(2)}) collective-permute-start(bf16[1024,256]{1,0:T(8,128)(2,1)S(1)} %collective-permute-done.1.refs_2_), channel_id=1, source_target_pairs={{0,1},{1,0},{2,3},{3,2},{4,5},{5,4},{6,7},{7,6},{8,9},{9,8},{10,11... | collective-permute-start | bytes 1572872 | tf_op jit(solution)/shard_map/ppermute | solution.py:324
  20.5 7.8 %collective-permute-done.refs_1_ = bf16[1024,256]{1,0:T(8,128)(2,1)S(1)} collective-permute-done((bf16[1024,256]{1,0:T(8,128)(2,1)}, bf16[1024,256]{1,0:T(8,128)(2,1)S(1)}, u32[]{:S(2)}, u32[]{:S(2)}) %collective-permute-start) | collective-permute-done | bytes 524320 | tf_op jit(solution)/shard_map/ppermute | solution.py:324
  28.3 0.5 collective-permute-start.4
  29.2 1.2 copy-done.2
  31.1 1.3 copy-done.3
  32.4 3.3 %shard_map.51 = (f32[512,1024]{1,0:T(8,128)S(1)}, f32[8,2,8,128]{3,2,1,0:T(8,128)S(1)}) custom-call(bf16[512,2048]{1,0:T(8,128)(2,1)S(1)} %copy-done, bf16[1024,256]{1,0:T(8,128)(2,1)S(1)} %copy-done.3, bf16[1024,256]{1,0:T(8,128)(2,1)S(1)} %collective-permute-done.refs_1_, bf16[1024,256]{1,0:T(8,128)(2,1)S(1)} %collective-permute-done.1.refs_2_, ...), custom_call_target="tpu_custom_call" | custom-call | flops 2147483648 | bytes 6291456 | tf_op jit(solution)/shard_map/pallas_call | solution.py:310
  35.8 8.7 %all_to_all.80.recv = f32[8,2,8,128]{3,2,1,0:T(8,128)S(1)} all-to-all(f32[8,2,8,128]{3,2,1,0:T(8,128)S(1)} %get-tuple-element.53), channel_id=1, replica_groups=mesh['z'=8,'x'=4,'y'=4,'core'=2] {'y','core'}, dimensions={0} | all-to-all | bytes 131072 | tf_op jit(solution)/shard_map/all_to_all | solution.py:344
  44.5 0.6 shard_map.52
  45.0 20.2 %all_to_all.81.recv = f32[32,2,4,128]{3,2,1,0:T(4,128)S(1)} all-to-all(f32[32,2,4,128]{3,2,1,0:T(4,128)S(1)} %get-tuple-element.55), channel_id=1, replica_groups=mesh['z'=8,'x'=4,'y'=4,'core'=2] {'z','x'}, dimensions={0} | all-to-all | bytes 262144 | tf_op jit(solution)/shard_map/all_to_all | solution.py:347
  65.7 9.3 %all_to_all.82.recv = f32[8,8,128]{2,1,0:T(8,128)S(1)} all-to-all(f32[8,8,128]{2,1,0:T(8,128)S(1)} %get-tuple-element.59), channel_id=1, replica_groups=mesh['z'=8,'x'=4,'y'=4,'core'=2] {'y','core'}, dimensions={0} | all-to-all | bytes 65536 | tf_op jit(solution)/shard_map/all_to_all | solution.py:344
  75.3 11.8 %all_to_all.83.recv = f32[32,4,128]{2,1,0:T(4,128)S(1)} all-to-all(f32[32,4,128]{2,1,0:T(4,128)S(1)} %get-tuple-element.61), channel_id=1, replica_groups=mesh['z'=8,'x'=4,'y'=4,'core'=2] {'z','x'}, dimensions={0} | all-to-all | bytes 131072 | tf_op jit(solution)/shard_map/all_to_all | solution.py:347
  87.3 9.2 %all_to_all.84.recv = f32[8,8,128]{2,1,0:T(8,128)S(1)} all-to-all(f32[8,8,128]{2,1,0:T(8,128)S(1)} %get-tuple-element.62), channel_id=1, replica_groups=mesh['z'=8,'x'=4,'y'=4,'core'=2] {'y','core'}, dimensions={0} | all-to-all | bytes 65536 | tf_op jit(solution)/shard_map/all_to_all | solution.py:344
  96.8 11.8 %all_to_all.85.recv = f32[32,4,128]{2,1,0:T(4,128)S(1)} all-to-all(f32[32,4,128]{2,1,0:T(4,128)S(1)} %get-tuple-element.64), channel_id=1, replica_groups=mesh['z'=8,'x'=4,'y'=4,'core'=2] {'z','x'}, dimensions={0} | all-to-all | bytes 131072 | tf_op jit(solution)/shard_map/all_to_all | solution.py:347
  108.9 9.1 %all_to_all.86.recv = f32[8,8,128]{2,1,0:T(8,128)S(1)} all-to-all(f32[8,8,128]{2,1,0:T(8,128)S(1)} %get-tuple-element.65), channel_id=1, replica_groups=mesh['z'=8,'x'=4,'y'=4,'core'=2] {'y','core'}, dimensions={0} | all-to-all | bytes 65536 | tf_op jit(solution)/shard_map/all_to_all | solution.py:344
  118.4 12.4 %all_to_all.87.recv = f32[32,2,4,128]{3,2,1,0:T(4,128)S(1)} all-to-all(f32[32,2,4,128]{3,2,1,0:T(4,128)S(1)} %get-tuple-element.69), channel_id=1, replica_groups=mesh['z'=8,'x'=4,'y'=4,'core'=2] {'z','x'}, dimensions={0} | all-to-all | bytes 262144 | tf_op jit(solution)/shard_map/all_to_all | solution.py:347
  131.3 9.2 %all_to_all.88.recv = f32[8,8,128]{2,1,0:T(8,128)S(1)} all-to-all(f32[8,8,128]{2,1,0:T(8,128)S(1)} %get-tuple-element.71), channel_id=1, replica_groups=mesh['z'=8,'x'=4,'y'=4,'core'=2] {'y','core'}, dimensions={0} | all-to-all | bytes 65536 | tf_op jit(solution)/shard_map/all_to_all | solution.py:344
  140.7 11.9 %all_to_all.89.refs_1_ = f32[32,4,128]{2,1,0:T(4,128)S(1)} all-to-all(f32[32,4,128]{2,1,0:T(4,128)S(1)} %get-tuple-element.72), channel_id=1, replica_groups=mesh['z'=8,'x'=4,'y'=4,'core'=2] {'z','x'}, dimensions={0} | all-to-all | bytes 131072 | tf_op jit(solution)/shard_map/all_to_all | solution.py:347
  152.9 9.0 %all_to_all.90.recv = f32[8,8,128]{2,1,0:T(8,128)S(1)} all-to-all(f32[8,8,128]{2,1,0:T(8,128)S(1)} %get-tuple-element.73), channel_id=1, replica_groups=mesh['z'=8,'x'=4,'y'=4,'core'=2] {'y','core'}, dimensions={0} | all-to-all | bytes 65536 | tf_op jit(solution)/shard_map/all_to_all | solution.py:344
  162.1 11.8 %all_to_all.91.refs_1_ = f32[32,4,128]{2,1,0:T(4,128)S(1)} all-to-all(f32[32,4,128]{2,1,0:T(4,128)S(1)} %get-tuple-element.74), channel_id=1, replica_groups=mesh['z'=8,'x'=4,'y'=4,'core'=2] {'z','x'}, dimensions={0} | all-to-all | bytes 131072 | tf_op jit(solution)/shard_map/all_to_all | solution.py:347
  174.3 9.1 %all_to_all.92.recv = f32[8,8,128]{2,1,0:T(8,128)S(1)} all-to-all(f32[8,8,128]{2,1,0:T(8,128)S(1)} %get-tuple-element.75), channel_id=1, replica_groups=mesh['z'=8,'x'=4,'y'=4,'core'=2] {'y','core'}, dimensions={0} | all-to-all | bytes 65536 | tf_op jit(solution)/shard_map/all_to_all | solution.py:344
  183.5 11.8 %all_to_all.93.refs_0_ = f32[32,4,128]{2,1,0:T(4,128)S(1)} all-to-all(f32[32,4,128]{2,1,0:T(4,128)S(1)} %get-tuple-element.76), channel_id=1, replica_groups=mesh['z'=8,'x'=4,'y'=4,'core'=2] {'z','x'}, dimensions={0} | all-to-all | bytes 131072 | tf_op jit(solution)/shard_map/all_to_all | solution.py:347
  195.4 0.9 shard_map.65
  196.2 5.2 %all-to-all-start.14 = ((f32[8,8,128]{2,1,0:T(8,128)}), f32[8,8,128]{2,1,0:T(8,128)S(1)}, u32[]{:S(2)}, u32[]{:S(2)}) async-start(f32[8,8,128]{2,1,0:T(8,128)} %get-tuple-element.86), calls=%async_computation.14 | async-start | bytes 65536 | tf_op jit(solution)/shard_map/all_to_all | solution.py:344
  201.5 2.2 shard_map.66
  203.7 2.5 all-to-all-done.14.recv
  206.2 7.4 %shard_map.67 = (bf16[512,1024]{1,0:T(8,128)(2,1)S(1)}, f32[128,2048]{1,0:T(8,128)S(1)}, bf16[128,2048]{1,0:T(8,128)(2,1)S(1)}, bf16[128,2048]{1,0:T(8,128)(2,1)S(1)}, bf16[128,2048]{1,0:T(8,128)(2,1)S(1)}) custom-call(f32[512,1024]{1,0:T(8,128)S(1)} %get-tuple-element.84.base, bf16[512,1024]{1,0:T(8,128)(2,1)S(1)} %get-tuple-element.85.first, ...), custom_call_target="tpu_custom_call" | custom-call | flops 2147483648 | bytes 7372800 | tf_op jit(solution)/shard_map/pallas_call | solution.py:310
  213.6 3.0 %shard_map.68 = (bf16[4,1024,256]{2,1,0:T(8,128)(2,1)S(1)}, bf16[1024,512]{1,0:T(8,128)(2,1)S(1)}) custom-call(bf16[512,1024]{1,0:T(8,128)(2,1)S(1)} %get-tuple-element.88.adjoint, bf16[512,2048]{1,0:T(8,128)(2,1)S(1)} %copy-done.1), custom_call_target="tpu_custom_call" | custom-call | flops 1073741824 | bytes 3145728 | tf_op jit(solution)/shard_map/pallas_call | solution.py:310
  216.6 1.1 collective-permute-start.7
  217.9 2.1 collective-permute-start.12
  220.0 0.8 collective-permute-start.13
  220.8 0.7 collective-permute-done.7.cross
  221.4 2.9 %shard_map.69 = (f32[1024,256]{1,0:T(8,128)S(1)}, bf16[1024,256]{1,0:T(8,128)(2,1)S(1)}, bf16[1024,256]{1,0:T(8,128)(2,1)S(1)}, bf16[1024,256]{1,0:T(8,128)(2,1)S(1)}) custom-call(bf16[1024,512]{1,0:T(8,128)(2,1)S(1)} %get-tuple-element.89.turned, bf16[512,2048]{1,0:T(8,128)(2,1)S(1)} %copy-done.1, bf16[4,1024,256]{2,1,0:T(8,128)(2,1)S(1)} %collective-permute-done.7.cross), custom_call_target="tpu_custom_call" | custom-call | flops 1073741824 | bytes 5242880 | tf_op jit(solution)/shard_map/pallas_call | solution.py:310
  224.4 8.2 %collective-permute-done.11.refs_0_ = bf16[128,2048]{1,0:T(8,128)(2,1)S(1)} collective-permute-done((bf16[128,2048]{1,0:T(8,128)(2,1)S(1)}, bf16[128,2048]{1,0:T(8,128)(2,1)S(1)}, u32[]{:S(2)}, u32[]{:S(2)}) %collective-permute-start.11) | collective-permute-done | bytes 524320 | tf_op jit(solution)/shard_map/ppermute | solution.py:324
  232.6 10.6 %collective-permute-done.12.refs_1_ = bf16[128,2048]{1,0:T(8,128)(2,1)S(1)} collective-permute-done((bf16[128,2048]{1,0:T(8,128)(2,1)S(1)}, bf16[128,2048]{1,0:T(8,128)(2,1)S(1)}, u32[]{:S(2)}, u32[]{:S(2)}) %collective-permute-start.12) | collective-permute-done | bytes 524320 | tf_op jit(solution)/shard_map/ppermute | solution.py:324
  243.2 0.6 collective-permute-done.13.refs_2_
  243.8 1.0 shard_map.71
  244.9 3.5 %all-to-all-start.15 = ((bf16[8,16,2048]{2,1,0:T(8,128)(2,1)}), bf16[8,16,2048]{2,1,0:T(8,128)(2,1)S(1)}, u32[]{:S(2)}, u32[]{:S(2)}) async-start(bf16[8,16,2048]{2,1,0:T(8,128)(2,1)} %shard_map.71), calls=%async_computation.15 | async-start | bytes 1048576 | tf_op jit(solution)/shard_map/all_to_all | solution.py:439
  248.7 1.8 collective-permute-start.9
  250.5 0.8 collective-permute-start.10
  251.3 11.2 %collective-permute-done.8.refs_0_ = bf16[1024,256]{1,0:T(8,128)(2,1)S(1)} collective-permute-done((bf16[1024,256]{1,0:T(8,128)(2,1)S(1)}, bf16[1024,256]{1,0:T(8,128)(2,1)S(1)}, u32[]{:S(2)}, u32[]{:S(2)}) %collective-permute-start.8) | collective-permute-done | bytes 524320 | tf_op jit(solution)/shard_map/ppermute | solution.py:324
  262.5 10.0 %collective-permute-done.9.refs_1_ = bf16[1024,256]{1,0:T(8,128)(2,1)S(1)} collective-permute-done((bf16[1024,256]{1,0:T(8,128)(2,1)S(1)}, bf16[1024,256]{1,0:T(8,128)(2,1)S(1)}, u32[]{:S(2)}, u32[]{:S(2)}) %collective-permute-start.9) | collective-permute-done | bytes 524320 | tf_op jit(solution)/shard_map/ppermute | solution.py:324
  272.6 1.6 collective-permute-done.10.refs_2_
  274.1 1.0 shard_map.70
  275.1 0.7 shard_map.72
  (43 shorter events, 5.6 us)
Async XLA Ops:
  0.6 30.5 %copy-start = (bf16[512,2048]{1,0:T(8,128)(2,1)S(1)}, bf16[512,2048]{1,0:T(8,128)(2,1)}, u32[]{:S(2)}) copy-start(bf16[512,2048]{1,0:T(8,128)(2,1)} %cent.5) | copy-start | bytes 6291460
  0.6 14.8 %collective-permute-start.1 = (bf16[1024,256]{1,0:T(8,128)(2,1)}, bf16[1024,256]{1,0:T(8,128)(2,1)S(1)}, u32[]{:S(2)}, u32[]{:S(2)}) collective-permute-start(bf16[1024,256]{1,0:T(8,128)(2,1)} %refs_0_.1), channel_id=1, source_target_pairs={{0,4},{2,6},{4,0},{6,2},{1,5},{3,7},{5,1},{7,3},{8,12},{10,14},{12... | collective-permute-start | bytes 1572872 | tf_op jit(solution)/shard_map/ppermute | solution.py:324
  4.5 23.8 %collective-permute-start = (bf16[1024,256]{1,0:T(8,128)(2,1)}, bf16[1024,256]{1,0:T(8,128)(2,1)S(1)}, u32[]{:S(2)}, u32[]{:S(2)}) collective-permute-start(bf16[1024,256]{1,0:T(8,128)(2,1)} %refs_0_.1), channel_id=1, source_target_pairs={{0,2},{2,4},{4,6},{6,0},{1,3},{3,5},{5,7},{7,1},{8,10},{10,12},{12... | collective-permute-start | bytes 1572872 | tf_op jit(solution)/shard_map/ppermute | solution.py:324
  4.9 23.9 %collective-permute-start.2 = (bf16[1024,256]{1,0:T(8,128)(2,1)}, bf16[1024,256]{1,0:T(8,128)(2,1)S(1)}, u32[]{:S(2)}, u32[]{:S(2)}) collective-permute-start(bf16[1024,256]{1,0:T(8,128)(2,1)} %refs_0_.1), channel_id=1, source_target_pairs={{0,6},{2,0},{4,2},{6,4},{1,7},{3,1},{5,3},{7,5},{8,14},{10,8},{12,... | collective-permute-start | bytes 1572872 | tf_op jit(solution)/shard_map/ppermute | solution.py:324
  7.1 23.7 %collective-permute-start.3 = (bf16[1024,256]{1,0:T(8,128)(2,1)}, bf16[1024,256]{1,0:T(8,128)(2,1)S(1)}, u32[]{:S(2)}, u32[]{:S(2)}) collective-permute-start(bf16[1024,256]{1,0:T(8,128)(2,1)} %refs_0_.1), channel_id=1, source_target_pairs={{0,1},{1,0},{2,3},{3,2},{4,5},{5,4},{6,7},{7,6},{8,9},{9,8},{10,11... | collective-permute-start | bytes 1572872 | tf_op jit(solution)/shard_map/ppermute | solution.py:324
  15.5 20.2 %copy-start.4 = (bf16[1024,256]{1,0:T(8,128)(2,1)}, bf16[1024,256]{1,0:T(8,128)(2,1)S(1)}, u32[]{:S(2)}) copy-start(bf16[1024,256]{1,0:T(8,128)(2,1)S(1)} %collective-permute-done.1.refs_2_) | copy-start | bytes 1572868
  15.5 15.3 %collective-permute-start.5 = (bf16[1024,256]{1,0:T(8,128)(2,1)S(1)}, bf16[1024,256]{1,0:T(8,128)(2,1)S(1)}, u32[]{:S(2)}, u32[]{:S(2)}) collective-permute-start(bf16[1024,256]{1,0:T(8,128)(2,1)S(1)} %collective-permute-done.1.refs_2_), channel_id=1, source_target_pairs={{0,1},{1,0},{2,3},{3,2},{4,5},{5,4},{6,7},{7,6},{8,9},{9,8},{10,11... | collective-permute-start | bytes 1572872 | tf_op jit(solution)/shard_map/ppermute | solution.py:324
  28.3 7.4 %copy-start.5 = (bf16[1024,256]{1,0:T(8,128)(2,1)}, bf16[1024,256]{1,0:T(8,128)(2,1)S(1)}, u32[]{:S(2)}) copy-start(bf16[1024,256]{1,0:T(8,128)(2,1)S(1)} %collective-permute-done.refs_1_) | copy-start | bytes 1572868
  28.3 2.5 collective-permute-start.4
  28.8 6.9 %copy-start.6 = (bf16[1024,256]{1,0:T(8,128)(2,1)}, bf16[1024,256]{1,0:T(8,128)(2,1)S(1)}, u32[]{:S(2)}) copy-start(bf16[1024,256]{1,0:T(8,128)(2,1)S(1)} %collective-permute-done.2.refs_3_) | copy-start | bytes 1572868
  28.8 2.3 collective-permute-start.6
  29.2 1.2 copy-start.2
  30.8 4.9 %copy-start.7 = (bf16[1024,256]{1,0:T(8,128)(2,1)}, bf16[1024,256]{1,0:T(8,128)(2,1)S(1)}, u32[]{:S(2)}) copy-start(bf16[1024,256]{1,0:T(8,128)(2,1)S(1)} %collective-permute-done.3.refs_4_) | copy-start | bytes 1572868
  30.8 4.9 %copy-start.8 = (bf16[1024,256]{1,0:T(8,128)(2,1)}, bf16[1024,256]{1,0:T(8,128)(2,1)S(1)}, u32[]{:S(2)}) copy-start(bf16[1024,256]{1,0:T(8,128)(2,1)S(1)} %collective-permute-done.5.refs_6_) | copy-start | bytes 1572868
  30.8 4.9 %copy-start.9 = (bf16[1024,256]{1,0:T(8,128)(2,1)}, bf16[1024,256]{1,0:T(8,128)(2,1)S(1)}, u32[]{:S(2)}) copy-start(bf16[1024,256]{1,0:T(8,128)(2,1)S(1)} %collective-permute-done.4.refs_5_) | copy-start | bytes 1572868
  31.1 1.3 copy-start.3
  32.4 3.4 %copy-start.10 = (bf16[1024,256]{1,0:T(8,128)(2,1)}, bf16[1024,256]{1,0:T(8,128)(2,1)S(1)}, u32[]{:S(2)}) copy-start(bf16[1024,256]{1,0:T(8,128)(2,1)S(1)} %collective-permute-done.6.refs_7_) | copy-start | bytes 1572868
  196.2 9.9 %all-to-all-start.14 = ((f32[8,8,128]{2,1,0:T(8,128)}), f32[8,8,128]{2,1,0:T(8,128)S(1)}, u32[]{:S(2)}, u32[]{:S(2)}) async-start(f32[8,8,128]{2,1,0:T(8,128)} %get-tuple-element.86), calls=%async_computation.14 | async-start | bytes 65536 | tf_op jit(solution)/shard_map/all_to_all | solution.py:344
  206.2 7.4 %copy-start.1 = (bf16[512,2048]{1,0:T(8,128)(2,1)S(1)}, bf16[512,2048]{1,0:T(8,128)(2,1)}, u32[]{:S(2)}) copy-start(bf16[512,2048]{1,0:T(8,128)(2,1)} %cent.5) | copy-start | bytes 6291460
  216.6 4.8 %collective-permute-start.7 = (bf16[4,1024,256]{2,1,0:T(8,128)(2,1)S(1)}, bf16[4,1024,256]{2,1,0:T(8,128)(2,1)S(1)}, u32[]{:S(2)}, u32[]{:S(2)}) collective-permute-start(bf16[4,1024,256]{2,1,0:T(8,128)(2,1)S(1)} %get-tuple-element.90), channel_id=1, source_target_pairs={{0,1},{1,0},{2,3},{3,2},{4,5},{5,4},{6,7},{7,6},{8,9},{9,8},{10,11... | collective-permute-start | bytes 6291464 | tf_op jit(solution)/shard_map/ppermute | solution.py:324
  217.7 14.9 %collective-permute-start.11 = (bf16[128,2048]{1,0:T(8,128)(2,1)S(1)}, bf16[128,2048]{1,0:T(8,128)(2,1)S(1)}, u32[]{:S(2)}, u32[]{:S(2)}) collective-permute-start(bf16[128,2048]{1,0:T(8,128)(2,1)S(1)} %get-tuple-element.97), channel_id=1, source_target_pairs={{0,8},{8,16},{16,24},{24,0},{1,9},{9,17},{17,25},{25,1},{2,10},{10... | collective-permute-start | bytes 1572872 | tf_op jit(solution)/shard_map/ppermute | solution.py:324
  217.9 25.3 %collective-permute-start.12 = (bf16[128,2048]{1,0:T(8,128)(2,1)S(1)}, bf16[128,2048]{1,0:T(8,128)(2,1)S(1)}, u32[]{:S(2)}, u32[]{:S(2)}) collective-permute-start(bf16[128,2048]{1,0:T(8,128)(2,1)S(1)} %get-tuple-element.98), channel_id=1, source_target_pairs={{0,16},{8,24},{16,0},{24,8},{1,17},{9,25},{17,1},{25,9},{2,18},{10... | collective-permute-start | bytes 1572872 | tf_op jit(solution)/shard_map/ppermute | solution.py:324
  220.0 23.9 %collective-permute-start.13 = (bf16[128,2048]{1,0:T(8,128)(2,1)S(1)}, bf16[128,2048]{1,0:T(8,128)(2,1)S(1)}, u32[]{:S(2)}, u32[]{:S(2)}) collective-permute-start(bf16[128,2048]{1,0:T(8,128)(2,1)S(1)} %get-tuple-element.99), channel_id=1, source_target_pairs={{0,24},{8,0},{16,8},{24,16},{1,25},{9,1},{17,9},{25,17},{2,26},{10... | collective-permute-start | bytes 1572872 | tf_op jit(solution)/shard_map/ppermute | solution.py:324
  244.9 30.3 %all-to-all-start.15 = ((bf16[8,16,2048]{2,1,0:T(8,128)(2,1)}), bf16[8,16,2048]{2,1,0:T(8,128)(2,1)S(1)}, u32[]{:S(2)}, u32[]{:S(2)}) async-start(bf16[8,16,2048]{2,1,0:T(8,128)(2,1)} %shard_map.71), calls=%async_computation.15 | async-start | bytes 1048576 | tf_op jit(solution)/shard_map/all_to_all | solution.py:439
  248.4 14.2 %collective-permute-start.8 = (bf16[1024,256]{1,0:T(8,128)(2,1)S(1)}, bf16[1024,256]{1,0:T(8,128)(2,1)S(1)}, u32[]{:S(2)}, u32[]{:S(2)}) collective-permute-start(bf16[1024,256]{1,0:T(8,128)(2,1)S(1)} %get-tuple-element.93), channel_id=1, source_target_pairs={{0,2},{2,4},{4,6},{6,0},{1,3},{3,5},{5,7},{7,1},{8,10},{10,12},{12... | collective-permute-start | bytes 1572872 | tf_op jit(solution)/shard_map/ppermute | solution.py:324
  248.7 23.8 %collective-permute-start.9 = (bf16[1024,256]{1,0:T(8,128)(2,1)S(1)}, bf16[1024,256]{1,0:T(8,128)(2,1)S(1)}, u32[]{:S(2)}, u32[]{:S(2)}) collective-permute-start(bf16[1024,256]{1,0:T(8,128)(2,1)S(1)} %get-tuple-element.94), channel_id=1, source_target_pairs={{0,4},{2,6},{4,0},{6,2},{1,5},{3,7},{5,1},{7,3},{8,12},{10,14},{12... | collective-permute-start | bytes 1572872 | tf_op jit(solution)/shard_map/ppermute | solution.py:324
  250.5 23.6 %collective-permute-start.10 = (bf16[1024,256]{1,0:T(8,128)(2,1)S(1)}, bf16[1024,256]{1,0:T(8,128)(2,1)S(1)}, u32[]{:S(2)}, u32[]{:S(2)}) collective-permute-start(bf16[1024,256]{1,0:T(8,128)(2,1)S(1)} %get-tuple-element.95), channel_id=1, source_target_pairs={{0,6},{2,0},{4,2},{6,4},{1,7},{3,1},{5,3},{7,5},{8,14},{10,8},{12,... | collective-permute-start | bytes 1572872 | tf_op jit(solution)/shard_map/ppermute | solution.py:324

commit v4 on v3

--- a/solution.py
+++ b/solution.py
@@ -55,7 +55,11 @@
 
 
 def total(recv):
-    return jnp.sum(recv[...], axis=0)
+    return jnp.sum(recv[...].astype(F32), axis=0)
+
+
+def put_cols(out, part):
+    out[...] = jnp.broadcast_to(gather_cols(part)[None], out.shape).astype(out.dtype)
 
 
 def merge(recv):
@@ -76,6 +80,14 @@
 def target(ny, k, cross):
     core = 1 - lax.axis_index("core") if cross else lax.axis_index("core")
     return lax.rem(lax.axis_index("y") + k, ny) * 2 + core
+
+
+def by_z():
+    return (0,)
+
+
+def by_x(n):
+    return tuple(k for k in range(n) if k not in by_z())
 
 
 def span(at, width):
@@ -137,7 +149,7 @@
 def k_col(weights, recv, row_mul, send):
     a = 1.0 / total(recv)
     row_mul[...] = a
-    send[...] = jnp.broadcast_to(gather_cols(weighted(weights, a))[None], send.shape)
+    put_cols(send, weighted(weights, a))
 
 
 def k_row(ratio, weights, recv, col_mul, send):
@@ -157,8 +169,8 @@
         step = lanes(weights, r) * a[r : r + 1, :]
         part = part + step
         bar = bar + step * lanes(grad, r).astype(F32)
-    send[:, 0] = jnp.broadcast_to(gather_cols(part)[None], send[:, 0].shape)
-    send[:, 1] = jnp.broadcast_to(gather_cols(bar)[None], send[:, 1].shape)
+    both = jnp.stack([gather_cols(part), gather_cols(bar)])
+    send[...] = jnp.broadcast_to(both[None], send.shape).astype(send.dtype)
 
 
 def k_adj_row(ratio, weights, grad, recv, col_mul, col_adj, send):
@@ -181,7 +193,7 @@
     a = row_mul[...]
     y = sign * a * a * total(recv)
     row_adj[...] = y
-    send[...] = jnp.broadcast_to(gather_cols(weighted(weights, y))[None], send.shape)
+    put_cols(send, weighted(weights, y))
 
 
 def k_back_row(ratio, weights, *refs):
@@ -218,75 +230,90 @@
         base[:, r * L : (r + 1) * L] = tile * inner
 
 
-def k_adjoint(scale, n, nx, base, first, recv, *refs):
-    pieces, adjoint, keep = refs[:n], refs[n], refs[n + 1]
-    sends, (held, turned, stage, sems, out_sems) = refs[n + 2 : n + 1 + nx], refs[n + 1 + nx :]
-    copies = [
-        pltpu.make_async_copy(piece, held.at[k], sems.at[k]) for k, piece in enumerate(pieces)
-    ]
-    for c in copies:
-        c.start()
+def k_adjoint(scale, base, first, recv, cent_hbm, adjoint, turned_hbm, cross, cent, turned, sems):
+    copy = pltpu.make_async_copy(cent_hbm, cent, sems.at[0])
+    copy.start()
     y = -total(recv)
     for r in range(y.shape[0]):
-        adjoint[:, r * L : (r + 1) * L] = (
-            lanes(base, r) - lanes(first, r).astype(F32) * y[r : r + 1, :]
-        ).astype(BF16)
+        tile = lanes(base, r) - lanes(first, r).astype(F32) * y[r : r + 1, :]
+        tile = tile.astype(BF16)
+        adjoint[:, r * L : (r + 1) * L] = tile
+        turned[r * L : (r + 1) * L, :] = tile.T
+    back = pltpu.make_async_copy(turned, turned_hbm, sems.at[1])
+    back.start()
+    copy.wait()
+    ny, _, width = cross.shape
+    for k in range(ny):
+        block = cent[:, span(target(ny, k, True), width)]
+        part = scale * lax.dot_general(turned[...], block, NN, preferred_element_type=F32)
+        cross[k] = part.astype(BF16)
+    back.wait()
+
+
+def k_cent(scale, n, nx, adjoint, *refs):
+    pieces, straight, keep = refs[:n], refs[n], refs[n + 1]
+    sends, (picked, wide, own, narrow, sems) = refs[n + 2 : n + 1 + nx], refs[n + 1 + nx :]
     per = keep.shape[0]
     group = 16
     for k in range(nx):
         to = lax.rem(lax.axis_index("x") + k, nx)
         for iz in range(per // group):
             at = pl.multiple_of((iz * nx + to) * group, group)
-            turned[k * per + iz * group : k * per + (iz + 1) * group, :] = adjoint[pl.ds(at, group), :]
-    width = held.shape[2]
+            picked[k * per + iz * group : k * per + (iz + 1) * group, :] = adjoint[pl.ds(at, group), :]
+    width = pieces[0].shape[1]
     outs = []
-    for p in range(n):
-        copies[p].wait()
-        part = scale * lax.dot_general(turned[...], held[p], NN, preferred_element_type=F32)
-        cols = span(source(n // 2, p), width)
-        keep[:, cols] = part[:per, :]
+
+    def leave(src, dst):
+        outs.append(pltpu.make_async_copy(src, dst, sems.at[len(outs)]))
+        outs[-1].start()
+
+    for i, p in enumerate(by_z()):
+        part = scale * lax.dot_general(adjoint[...], pieces[p][...], NN, preferred_element_type=F32)
+        narrow[i] = part.astype(BF16).reshape(narrow.shape[1:])
+        leave(narrow.at[i], straight.at[:, :, pl.ds(i * width, width)])
+    for i, p in enumerate(by_x(n)):
+        part = scale * lax.dot_general(picked[...], pieces[p][...], NN, preferred_element_type=F32)
+        own[i] = part[:per, :]
+        leave(own.at[i], keep.at[:, pl.ds(i * width, width)])
         for k in range(1, nx):
-            stage[p, k - 1] = part[k * per : (k + 1) * per, :].astype(BF16)
-            outs.append(
-                pltpu.make_async_copy(
-                    stage.at[p, k - 1], sends[k - 1].at[:, cols], out_sems.at[p, k - 1]
-                )
-            )
-            outs[-1].start()
+            wide[i, k - 1] = part[k * per : (k + 1) * per, :].astype(BF16)
+            leave(wide.at[i, k - 1], sends[k - 1].at[:, pl.ds(i * width, width)])
     for c in outs:
         c.wait()
 
 
-def k_cross(scale, adjoint, cent, cross, turned, stage, sems):
-    turned[...] = adjoint[...].T
+def k_pair(scale, turned, cent, cross, first, *rest):
     ny, _, width = cross.shape
-    outs = []
-    for k in range(ny):
-        block = cent[:, span(target(ny, k, True), width)]
-        part = scale * lax.dot_general(turned[...], block, NN, preferred_element_type=F32)
-        stage[k] = part.astype(cross.dtype)
-        outs.append(pltpu.make_async_copy(stage.at[k], cross.at[k], sems.at[k]))
-        outs[-1].start()
-    for c in outs:
-        c.wait()
-
-
-def k_pair(scale, turned, cent, cross, first, *refs):
-    rest, (stage, sems) = refs[:-2], refs[-2:]
-    ny, _, width = cross.shape
-    outs = []
-    for k in range(ny - 1, -1, -1):
+    for k, out in enumerate((first, *rest)):
         block = cent[:, span(target(ny, k, False), width)]
         part = scale * lax.dot_general(turned[...], block, NN, preferred_element_type=F32)
-        part = part + cross[k].astype(F32)
-        if k:
-            stage[k - 1] = part.astype(BF16)
-            outs.append(pltpu.make_async_copy(stage.at[k - 1], rest[k - 1], sems.at[k - 1]))
-            outs[-1].start()
-        else:
-            first[...] = part
-    for c in outs:
-        c.wait()
+        out[...] = (part + cross[k].astype(F32)).astype(out.dtype)
+
+
+def k_early(recv, keep, *refs):
+    sends, held = refs[:-1], refs[-1]
+    value = recv[0].astype(F32)
+    for k in range(1, recv.shape[0]):
+        value = value + recv[k].astype(F32)
+    held[...] = value
+    rows, nx = keep.shape[0], len(sends) + 1
+    for k, out in enumerate((keep, *sends)):
+        at = lax.rem(lax.axis_index("x") + k, nx) * rows
+        out[...] = held[pl.ds(pl.multiple_of(at, 16), rows), :].astype(out.dtype)
+
+
+def k_join(n, one, keep, *refs):
+    out = refs[-1]
+    width = out.shape[1] // n
+    first = one[0].astype(F32)
+    for k in range(1, one.shape[0]):
+        first = first + one[k].astype(F32)
+    second = keep[...]
+    for r in refs[:-1]:
+        second = second + r[...].astype(F32)
+    for value, pieces in ((first.astype(BF16), by_x(n)), (second.astype(BF16), by_z())):
+        for i, p in enumerate(pieces):
+            out[:, span(source(n // 2, p), width)] = value[:, i * width : (i + 1) * width]
 
 
 def k_add(first, *refs):
@@ -294,13 +321,6 @@
     for r in refs[:-1]:
         value = value + r[...].astype(F32)
     refs[-1][...] = value.astype(BF16).reshape(refs[-1].shape)
-
-
-def k_sum(recv, out):
-    value = recv[0].astype(F32)
-    for k in range(1, recv.shape[0]):
-        value = value + recv[k].astype(F32)
-    out[...] = value.astype(BF16)
 
 
 def call(body, outs, *args, limit=SMALL, flops=0, hbm_in=(), hbm_out=(), alias=None, scratch=()):
@@ -309,7 +329,10 @@
     size = sum(a.size * a.dtype.itemsize for a in args)
     return pl.pallas_call(
         body,
-        out_shape=[jax.ShapeDtypeStruct(s, d) for s, d in outs],
+        out_shape=[
+            pltpu.HBM(s, d) if i in hbm_out else jax.ShapeDtypeStruct(s, d)
+            for i, (s, d) in enumerate(outs)
+        ],
         in_specs=ins,
         out_specs=[far if i in hbm_out else spec for i in range(len(outs))],
         input_output_aliases=alias or {},
@@ -403,42 +426,57 @@
         flops=work, alias={0: 0, 1: 1},
     )
     per, n = cols // nx, len(pieces)
-    adjoint, near, *parts = call(
-        functools.partial(k_adjoint, scale, n, nx),
-        [((cols, rows), BF16), ((per, depth), F32)] + [((per, depth), BF16)] * (nx - 1),
-        base, first, recv,
-        *(pltpu.with_memory_space_constraint(p, pltpu.HBM) for p in pieces),
-        limit=LARGE, flops=work, hbm_in=range(3, 3 + n), hbm_out=range(2, 1 + nx),
+    adjoint, turned, cross = call(
+        functools.partial(k_adjoint, scale),
+        [((cols, rows), BF16), ((rows, cols), BF16), ((ny, rows, width), BF16)],
+        base, first, recv, pltpu.with_memory_space_constraint(centroids, pltpu.HBM),
+        limit=LARGE, flops=work // 2, hbm_in=(3,), hbm_out=(1,),
         scratch=[
-            pltpu.VMEM((n, rows, width), BF16),
+            pltpu.VMEM((cols, depth), BF16),
+            pltpu.VMEM((rows, cols), BF16),
+            pltpu.SemaphoreType.DMA((2,)),
+        ],
+    )
+    cross = shift(cross, "core", 1)
+    wide, narrow = len(by_x(n)) * width, len(by_z()) * width
+    straight, near, *parts = call(
+        functools.partial(k_cent, scale, n, nx),
+        [((nz, cols // nz, narrow), BF16), ((per, wide), F32)]
+        + [((per, wide), BF16)] * (nx - 1),
+        adjoint, *pieces,
+        limit=LARGE, flops=work, hbm_out=range(1 + nx),
+        scratch=[
             pltpu.VMEM((cols, rows), BF16),
-            pltpu.VMEM((n, nx - 1, per, width), BF16),
-            pltpu.SemaphoreType.DMA((n,)),
-            pltpu.SemaphoreType.DMA((n, nx - 1)),
+            pltpu.VMEM((len(by_x(n)), nx - 1, per, width), BF16),
+            pltpu.VMEM((len(by_x(n)), per, width), F32),
+            pltpu.VMEM((len(by_z()), nz, cols // nz, width), BF16),
+            pltpu.SemaphoreType.DMA((n * nx,)),
         ],
     )
     parts = [shift(p, "x", k + 1) for k, p in enumerate(parts)]
-    cross, turned = call(
-        functools.partial(k_cross, scale),
-        [((ny, rows, width), BF16), ((rows, cols), BF16)],
-        adjoint, centroids,
-        limit=LARGE, flops=work // 2, hbm_out=(0,),
-        scratch=[pltpu.VMEM((ny, rows, width), BF16), pltpu.SemaphoreType.DMA((ny,))],
-    )
-    cross = shift(cross, "core", 1)
+    straight = lax.all_to_all(straight, "z", 0, 0, tiled=True)
     own, *moved = call(
         functools.partial(k_pair, scale),
         [((rows, width), F32)] + [((rows, width), BF16)] * (ny - 1),
         turned, centroids, cross,
-        limit=LARGE, flops=work // 2, hbm_out=range(1, ny),
-        scratch=[pltpu.VMEM((ny - 1, rows, width), BF16), pltpu.SemaphoreType.DMA((ny - 1,))],
+        limit=LARGE, flops=work // 2,
     )
     near, own = lax.optimization_barrier((near, own))
     moved = [shift(m, "y", k + 1) for k, m in enumerate(moved)]
-    (parts,) = call(k_add, [((nz, per // nz, depth), BF16)], near, *parts, limit=LARGE)
+    (parts,) = call(k_add, [((nz, per // nz, wide), BF16)], near, *parts, limit=LARGE)
     parts = lax.all_to_all(parts, "z", 0, 0, tiled=True)
-    (centroid_grad,) = call(k_sum, [((per // nz, depth), BF16)], parts, limit=LARGE)
+    final = per // nz
+    last, *late = call(
+        k_early,
+        [((final, narrow), F32)] + [((final, narrow), BF16)] * (nx - 1),
+        straight,
+        limit=LARGE, scratch=[pltpu.VMEM((cols // nz, narrow), F32)],
+    )
+    late = [shift(p, "x", k + 1) for k, p in enumerate(late)]
     (embed_grad,) = call(k_add, [((rows, width), BF16)], own, *moved, limit=LARGE)
+    (centroid_grad,) = call(
+        functools.partial(k_join, n), [((final, depth), BF16)], parts, last, *late, limit=LARGE
+    )
     return embed_grad, centroid_grad
 
 

time: 277 us -> 277 us (level); the launches traced: 276 us -> 272 us
  waiting for transfers between devices: 60.3 us -> 42.5 us
  starting transfers between devices: 29.8 us -> 41.3 us
  local copies, waits for them, and re-layouts: 2.59 us -> 6.23 us
    ppermute x14 -> x17, waiting for transfers between devices: 57.8 us -> 40 us  [shift(): return lax.ppermute(value, axis, [(i, (i + step) % n) for i in range(n)])]
    ppermute x14 -> x17, starting transfers between devices: 21.1 us -> 29 us  [shift(): return lax.ppermute(value, axis, [(i, (i + step) % n) for i in range(n)])]
    unnamed x22 -> x54, local copies, waits for them, and re-layouts: 2.59 us -> 6.23 us
    all_to_all x0 -> x1, starting transfers between devices: none -> 3.63 us  [shards(): straight = lax.all_to_all(straight, 'z', 0, 0, tiled=True)]
    pallas_call x23 -> x24, Pallas kernels: 26.9 us -> 26 us  [call(): pl.pallas_call(body, out_shape=[pltpu.HBM(s, d) if i in hbm_out else jax....]
  transfers between devices with their start and end apart: 16 -> 20, of which waited for: 11 -> 10; matrix products, arithmetic and copies ran while one was open for 0% -> 0% of each run, Pallas kernels for 2% -> 4%
where the time goes in v4:
time: 277 us; the launch traced here: 272 us
  blocking collectives  155 us (56%)
  waiting for transfers between devices  42.5 us (15%)
  starting transfers between devices  41.3 us (15%)
  Pallas kernels  26 us (9%)
  local copies, waits for them, and re-layouts  6.23 us (2%)
    all_to_all x7, blocking collectives, over_prog(): return lax.all_to_all(send, ('z', 'x'), 0, 0, tiled=True)  91.8 us
    all_to_all x7, blocking collectives, over_clus(): return lax.all_to_all(send, ('y', 'core'), 0, 0, tiled=True)  63.6 us
    ppermute x17, waiting for transfers between devices, shift(): return lax.ppermute(value, axis, [(i, (i + step) % n) for i in range(n)])  40 us
    ppermute x17, starting transfers between devices, shift(): return lax.ppermute(value, axis, [(i, (i + step) % n) for i in range(n)])  29 us
    pallas_call x24, Pallas kernels, call(): pl.pallas_call(body, out_shape=[pltpu.HBM(s, d) if i in hbm_out else jax....  26 us
    unnamed x54, local copies, waits for them, and re-layouts  6.23 us
  transfers between devices with their start and end apart: 20, of which 10 were waited for; matrix products, arithmetic and copies ran while one was open for 0% of the time, Pallas kernels for 4%

profile of v4, /device:TPU:1, one launch (start us, length us, event | category | flops | bytes accessed | tf_op | source)
XLA Modules:
  0.0 272.5 jit_solution(16088205267373849743)
XLA Ops:
  0.6 3.8 %collective-permute-start.1 = (bf16[1024,256]{1,0:T(8,128)(2,1)}, bf16[1024,256]{1,0:T(8,128)(2,1)S(1)}, u32[]{:S(2)}, u32[]{:S(2)}) collective-permute-start(bf16[1024,256]{1,0:T(8,128)(2,1)} %refs_0_.1), channel_id=1, source_target_pairs={{0,4},{2,6},{4,0},{6,2},{1,5},{3,7},{5,1},{7,3},{8,12},{10,14},{12... | collective-permute-start | bytes 1572872 | tf_op jit(solution)/shard_map/ppermute | solution.py:347
  4.9 2.3 collective-permute-start.2
  7.1 1.5 collective-permute-start.3
  8.7 6.8 %collective-permute-done.1.refs_2_ = bf16[1024,256]{1,0:T(8,128)(2,1)S(1)} collective-permute-done((bf16[1024,256]{1,0:T(8,128)(2,1)}, bf16[1024,256]{1,0:T(8,128)(2,1)S(1)}, u32[]{:S(2)}, u32[]{:S(2)}) %collective-permute-start.1) | collective-permute-done | bytes 524320 | tf_op jit(solution)/shard_map/ppermute | solution.py:347
  15.5 5.0 %collective-permute-start.5 = (bf16[1024,256]{1,0:T(8,128)(2,1)S(1)}, bf16[1024,256]{1,0:T(8,128)(2,1)S(1)}, u32[]{:S(2)}, u32[]{:S(2)}) collective-permute-start(bf16[1024,256]{1,0:T(8,128)(2,1)S(1)} %collective-permute-done.1.refs_2_), channel_id=1, source_target_pairs={{0,1},{1,0},{2,3},{3,2},{4,5},{5,4},{6,7},{7,6},{8,9},{9,8},{10,11... | collective-permute-start | bytes 1572872 | tf_op jit(solution)/shard_map/ppermute | solution.py:347
  20.5 7.8 %collective-permute-done.refs_1_ = bf16[1024,256]{1,0:T(8,128)(2,1)S(1)} collective-permute-done((bf16[1024,256]{1,0:T(8,128)(2,1)}, bf16[1024,256]{1,0:T(8,128)(2,1)S(1)}, u32[]{:S(2)}, u32[]{:S(2)}) %collective-permute-start) | collective-permute-done | bytes 524320 | tf_op jit(solution)/shard_map/ppermute | solution.py:347
  29.2 1.2 copy-done.3
  31.1 1.3 copy-done.5
  32.4 3.3 %shard_map.51 = (f32[512,1024]{1,0:T(8,128)S(1)}, f32[8,2,8,128]{3,2,1,0:T(8,128)S(1)}) custom-call(bf16[512,2048]{1,0:T(8,128)(2,1)S(1)} %copy-done, bf16[1024,256]{1,0:T(8,128)(2,1)S(1)} %copy-done.5, bf16[1024,256]{1,0:T(8,128)(2,1)S(1)} %collective-permute-done.refs_1_, bf16[1024,256]{1,0:T(8,128)(2,1)S(1)} %collective-permute-done.1.refs_2_, ...), custom_call_target="tpu_custom_call" | custom-call | flops 2147483648 | bytes 6291456 | tf_op jit(solution)/shard_map/pallas_call | solution.py:330
  35.8 8.7 %all_to_all.85.recv = f32[8,2,8,128]{3,2,1,0:T(8,128)S(1)} all-to-all(f32[8,2,8,128]{3,2,1,0:T(8,128)S(1)} %get-tuple-element.58), channel_id=1, replica_groups=mesh['z'=8,'x'=4,'y'=4,'core'=2] {'y','core'}, dimensions={0} | all-to-all | bytes 131072 | tf_op jit(solution)/shard_map/all_to_all | solution.py:367
  45.0 20.2 %all_to_all.86.recv = f32[32,2,4,128]{3,2,1,0:T(4,128)S(1)} all-to-all(f32[32,2,4,128]{3,2,1,0:T(4,128)S(1)} %get-tuple-element.60), channel_id=1, replica_groups=mesh['z'=8,'x'=4,'y'=4,'core'=2] {'z','x'}, dimensions={0} | all-to-all | bytes 262144 | tf_op jit(solution)/shard_map/all_to_all | solution.py:370
  65.7 9.3 %all_to_all.87.recv = f32[8,8,128]{2,1,0:T(8,128)S(1)} all-to-all(f32[8,8,128]{2,1,0:T(8,128)S(1)} %get-tuple-element.64), channel_id=1, replica_groups=mesh['z'=8,'x'=4,'y'=4,'core'=2] {'y','core'}, dimensions={0} | all-to-all | bytes 65536 | tf_op jit(solution)/shard_map/all_to_all | solution.py:367
  75.3 11.8 %all_to_all.88.recv = f32[32,4,128]{2,1,0:T(4,128)S(1)} all-to-all(f32[32,4,128]{2,1,0:T(4,128)S(1)} %get-tuple-element.66), channel_id=1, replica_groups=mesh['z'=8,'x'=4,'y'=4,'core'=2] {'z','x'}, dimensions={0} | all-to-all | bytes 131072 | tf_op jit(solution)/shard_map/all_to_all | solution.py:370
  87.3 9.2 %all_to_all.89.recv = f32[8,8,128]{2,1,0:T(8,128)S(1)} all-to-all(f32[8,8,128]{2,1,0:T(8,128)S(1)} %get-tuple-element.67), channel_id=1, replica_groups=mesh['z'=8,'x'=4,'y'=4,'core'=2] {'y','core'}, dimensions={0} | all-to-all | bytes 65536 | tf_op jit(solution)/shard_map/all_to_all | solution.py:367
  96.8 11.8 %all_to_all.90.recv = f32[32,4,128]{2,1,0:T(4,128)S(1)} all-to-all(f32[32,4,128]{2,1,0:T(4,128)S(1)} %get-tuple-element.69), channel_id=1, replica_groups=mesh['z'=8,'x'=4,'y'=4,'core'=2] {'z','x'}, dimensions={0} | all-to-all | bytes 131072 | tf_op jit(solution)/shard_map/all_to_all | solution.py:370
  108.9 9.1 %all_to_all.91.recv = f32[8,8,128]{2,1,0:T(8,128)S(1)} all-to-all(f32[8,8,128]{2,1,0:T(8,128)S(1)} %get-tuple-element.70), channel_id=1, replica_groups=mesh['z'=8,'x'=4,'y'=4,'core'=2] {'y','core'}, dimensions={0} | all-to-all | bytes 65536 | tf_op jit(solution)/shard_map/all_to_all | solution.py:367
  118.4 12.4 %all_to_all.92.recv = f32[32,2,4,128]{3,2,1,0:T(4,128)S(1)} all-to-all(f32[32,2,4,128]{3,2,1,0:T(4,128)S(1)} %get-tuple-element.74), channel_id=1, replica_groups=mesh['z'=8,'x'=4,'y'=4,'core'=2] {'z','x'}, dimensions={0} | all-to-all | bytes 262144 | tf_op jit(solution)/shard_map/all_to_all | solution.py:370
  131.3 9.2 %all_to_all.93.recv = f32[8,8,128]{2,1,0:T(8,128)S(1)} all-to-all(f32[8,8,128]{2,1,0:T(8,128)S(1)} %get-tuple-element.76), channel_id=1, replica_groups=mesh['z'=8,'x'=4,'y'=4,'core'=2] {'y','core'}, dimensions={0} | all-to-all | bytes 65536 | tf_op jit(solution)/shard_map/all_to_all | solution.py:367
  140.7 11.9 %all_to_all.94.refs_1_ = f32[32,4,128]{2,1,0:T(4,128)S(1)} all-to-all(f32[32,4,128]{2,1,0:T(4,128)S(1)} %get-tuple-element.77), channel_id=1, replica_groups=mesh['z'=8,'x'=4,'y'=4,'core'=2] {'z','x'}, dimensions={0} | all-to-all | bytes 131072 | tf_op jit(solution)/shard_map/all_to_all | solution.py:370
  152.9 9.0 %all_to_all.95.recv = f32[8,8,128]{2,1,0:T(8,128)S(1)} all-to-all(f32[8,8,128]{2,1,0:T(8,128)S(1)} %get-tuple-element.78), channel_id=1, replica_groups=mesh['z'=8,'x'=4,'y'=4,'core'=2] {'y','core'}, dimensions={0} | all-to-all | bytes 65536 | tf_op jit(solution)/shard_map/all_to_all | solution.py:367
  162.1 11.8 %all_to_all.96.refs_1_ = f32[32,4,128]{2,1,0:T(4,128)S(1)} all-to-all(f32[32,4,128]{2,1,0:T(4,128)S(1)} %get-tuple-element.79), channel_id=1, replica_groups=mesh['z'=8,'x'=4,'y'=4,'core'=2] {'z','x'}, dimensions={0} | all-to-all | bytes 131072 | tf_op jit(solution)/shard_map/all_to_all | solution.py:370
  174.3 9.1 %all_to_all.97.recv = f32[8,8,128]{2,1,0:T(8,128)S(1)} all-to-all(f32[8,8,128]{2,1,0:T(8,128)S(1)} %get-tuple-element.80), channel_id=1, replica_groups=mesh['z'=8,'x'=4,'y'=4,'core'=2] {'y','core'}, dimensions={0} | all-to-all | bytes 65536 | tf_op jit(solution)/shard_map/all_to_all | solution.py:367
  183.5 11.8 %all_to_all.98.refs_0_ = f32[32,4,128]{2,1,0:T(4,128)S(1)} all-to-all(f32[32,4,128]{2,1,0:T(4,128)S(1)} %get-tuple-element.81), channel_id=1, replica_groups=mesh['z'=8,'x'=4,'y'=4,'core'=2] {'z','x'}, dimensions={0} | all-to-all | bytes 131072 | tf_op jit(solution)/shard_map/all_to_all | solution.py:370
  195.4 0.9 shard_map.65
  196.2 5.2 %all-to-all-start.14 = ((f32[8,8,128]{2,1,0:T(8,128)}), f32[8,8,128]{2,1,0:T(8,128)S(1)}, u32[]{:S(2)}, u32[]{:S(2)}) async-start(f32[8,8,128]{2,1,0:T(8,128)} %get-tuple-element.91), calls=%async_computation.14 | async-start | bytes 65536 | tf_op jit(solution)/shard_map/all_to_all | solution.py:367
  201.5 2.2 shard_map.66
  203.7 2.5 all-to-all-done.14.recv
  206.2 4.8 %shard_map.67 = (bf16[512,1024]{1,0:T(8,128)(2,1)S(1)}, bf16[1024,512]{1,0:T(8,128)(2,1)}, bf16[4,1024,256]{2,1,0:T(8,128)(2,1)}) custom-call(f32[512,1024]{1,0:T(8,128)S(1)} %get-tuple-element.89.base, bf16[512,1024]{1,0:T(8,128)(2,1)S(1)} %get-tuple-element.90.first, f32[8,8,128]{2,1,0:T(8,128)S(1)} %all-to-all-done.14.recv, bf16[512,2048]{1,0:T(8,128)(2,1)} %cent.3), custom_call_target="tpu_custom_call" | custom-call | flops 1073741824 | bytes 5275648 | tf_op jit(solution)/shard_map/pallas_call | solution.py:330
  211.1 0.8 collective-permute-start.7
  212.0 3.4 %shard_map.68 = (bf16[8,64,256]{2,1,0:T(8,128)(2,1)}, f32[128,1792]{1,0:T(8,128)}, bf16[128,1792]{1,0:T(8,128)(2,1)}, bf16[128,1792]{1,0:T(8,128)(2,1)}, bf16[128,1792]{1,0:T(8,128)(2,1)}) custom-call(bf16[512,1024]{1,0:T(8,128)(2,1)S(1)} %get-tuple-element.92.adjoint, bf16[1024,256]{1,0:T(8,128)(2,1)S(1)} %copy-done.6, bf16[1024,256]{1,0:T(8,128)(2,1)S(1)} %copy-done.10, ...), custom_call_target="tpu_custom_call" | custom-call | flops 2147483648 | bytes 5242880 | tf_op jit(solution)/shard_map/pallas_call | solution.py:330
  215.7 2.1 collective-permute-start.12
  217.8 0.8 collective-permute-start.13
  218.6 3.6 %all-to-all-start.16 = ((bf16[8,64,256]{2,1,0:T(8,128)(2,1)}), bf16[8,64,256]{2,1,0:T(8,128)(2,1)S(1)}, u32[]{:S(2)}, u32[]{:S(2)}) async-start(bf16[8,64,256]{2,1,0:T(8,128)(2,1)} %get-tuple-element.105), calls=%async_computation.16 | async-start | bytes 524288 | tf_op jit(solution)/shard_map/all_to_all | solution.py:457
  222.3 1.2 copy-done.2
  223.5 2.9 %shard_map.69 = (f32[1024,256]{1,0:T(8,128)S(1)}, bf16[1024,256]{1,0:T(8,128)(2,1)S(1)}, bf16[1024,256]{1,0:T(8,128)(2,1)S(1)}, bf16[1024,256]{1,0:T(8,128)(2,1)S(1)}) custom-call(bf16[1024,512]{1,0:T(8,128)(2,1)S(1)} %copy-done.2, bf16[512,2048]{1,0:T(8,128)(2,1)S(1)} %copy-done.1, bf16[4,1024,256]{2,1,0:T(8,128)(2,1)} %collective-permute-done.7.cross), custom_call_target="tpu_custom_call" | custom-call | flops 1073741824 | bytes 5242880 | tf_op jit(solution)/shard_map/pallas_call | solution.py:330
  226.5 0.8 copy-done.21
  229.4 9.2 %collective-permute-done.12.refs_1_ = bf16[128,1792]{1,0:T(8,128)(2,1)} collective-permute-done((bf16[128,1792]{1,0:T(8,128)(2,1)}, bf16[128,1792]{1,0:T(8,128)(2,1)}, u32[]{:S(2)}, u32[]{:S(2)}) %collective-permute-start.12) | collective-permute-done | bytes 458784 | tf_op jit(solution)/shard_map/ppermute | solution.py:347
  239.2 2.3 shard_map.71
  241.5 3.5 %all-to-all-start.15 = ((bf16[8,16,1792]{2,1,0:T(8,128)(2,1)}), bf16[8,16,1792]{2,1,0:T(8,128)(2,1)S(1)}, u32[]{:S(2)}, u32[]{:S(2)}) async-start(bf16[8,16,1792]{2,1,0:T(8,128)(2,1)} %shard_map.71), calls=%async_computation.15 | async-start | bytes 917504 | tf_op jit(solution)/shard_map/all_to_all | solution.py:467
  245.4 1.8 collective-permute-start.9
  247.1 0.8 collective-permute-start.10
  248.0 1.2 collective-permute-start.14
  249.2 3.1 %collective-permute-start.15 = (bf16[16,256]{1,0:T(8,128)(2,1)S(1)}, bf16[16,256]{1,0:T(8,128)(2,1)S(1)}, u32[]{:S(2)}, u32[]{:S(2)}) collective-permute-start(bf16[16,256]{1,0:T(8,128)(2,1)S(1)} %get-tuple-element.108), channel_id=1, source_target_pairs={{0,16},{8,24},{16,0},{24,8},{1,17},{9,25},{17,1},{25,9},{2,18},{10... | collective-permute-start | bytes 24584 | tf_op jit(solution)/shard_map/ppermute | solution.py:347
  252.3 6.9 %collective-permute-done.8.refs_0_ = bf16[1024,256]{1,0:T(8,128)(2,1)S(1)} collective-permute-done((bf16[1024,256]{1,0:T(8,128)(2,1)S(1)}, bf16[1024,256]{1,0:T(8,128)(2,1)S(1)}, u32[]{:S(2)}, u32[]{:S(2)}) %collective-permute-start.8) | collective-permute-done | bytes 524320 | tf_op jit(solution)/shard_map/ppermute | solution.py:347
  259.2 3.7 %collective-permute-start.16 = (bf16[16,256]{1,0:T(8,128)(2,1)S(1)}, bf16[16,256]{1,0:T(8,128)(2,1)S(1)}, u32[]{:S(2)}, u32[]{:S(2)}) collective-permute-start(bf16[16,256]{1,0:T(8,128)(2,1)S(1)} %get-tuple-element.109), channel_id=1, source_target_pairs={{0,24},{8,0},{16,8},{24,16},{1,25},{9,1},{17,9},{25,17},{2,26},{10... | collective-permute-start | bytes 24584 | tf_op jit(solution)/shard_map/ppermute | solution.py:347
  262.9 6.3 %collective-permute-done.9.refs_1_ = bf16[1024,256]{1,0:T(8,128)(2,1)S(1)} collective-permute-done((bf16[1024,256]{1,0:T(8,128)(2,1)S(1)}, bf16[1024,256]{1,0:T(8,128)(2,1)S(1)}, u32[]{:S(2)}, u32[]{:S(2)}) %collective-permute-start.9) | collective-permute-done | bytes 524320 | tf_op jit(solution)/shard_map/ppermute | solution.py:347
  269.2 1.5 collective-permute-done.10.refs_2_
  270.8 1.0 shard_map.70
  (84 shorter events, 10.3 us)
Async XLA Ops:
  0.6 30.5 %copy-start = (bf16[512,2048]{1,0:T(8,128)(2,1)S(1)}, bf16[512,2048]{1,0:T(8,128)(2,1)}, u32[]{:S(2)}) copy-start(bf16[512,2048]{1,0:T(8,128)(2,1)} %cent.3) | copy-start | bytes 6291460
  0.6 14.8 %collective-permute-start.1 = (bf16[1024,256]{1,0:T(8,128)(2,1)}, bf16[1024,256]{1,0:T(8,128)(2,1)S(1)}, u32[]{:S(2)}, u32[]{:S(2)}) collective-permute-start(bf16[1024,256]{1,0:T(8,128)(2,1)} %refs_0_.1), channel_id=1, source_target_pairs={{0,4},{2,6},{4,0},{6,2},{1,5},{3,7},{5,1},{7,3},{8,12},{10,14},{12... | collective-permute-start | bytes 1572872 | tf_op jit(solution)/shard_map/ppermute | solution.py:347
  4.5 23.8 %collective-permute-start = (bf16[1024,256]{1,0:T(8,128)(2,1)}, bf16[1024,256]{1,0:T(8,128)(2,1)S(1)}, u32[]{:S(2)}, u32[]{:S(2)}) collective-permute-start(bf16[1024,256]{1,0:T(8,128)(2,1)} %refs_0_.1), channel_id=1, source_target_pairs={{0,2},{2,4},{4,6},{6,0},{1,3},{3,5},{5,7},{7,1},{8,10},{10,12},{12... | collective-permute-start | bytes 1572872 | tf_op jit(solution)/shard_map/ppermute | solution.py:347
  4.9 23.9 %collective-permute-start.2 = (bf16[1024,256]{1,0:T(8,128)(2,1)}, bf16[1024,256]{1,0:T(8,128)(2,1)S(1)}, u32[]{:S(2)}, u32[]{:S(2)}) collective-permute-start(bf16[1024,256]{1,0:T(8,128)(2,1)} %refs_0_.1), channel_id=1, source_target_pairs={{0,6},{2,0},{4,2},{6,4},{1,7},{3,1},{5,3},{7,5},{8,14},{10,8},{12,... | collective-permute-start | bytes 1572872 | tf_op jit(solution)/shard_map/ppermute | solution.py:347
  7.1 23.7 %collective-permute-start.3 = (bf16[1024,256]{1,0:T(8,128)(2,1)}, bf16[1024,256]{1,0:T(8,128)(2,1)S(1)}, u32[]{:S(2)}, u32[]{:S(2)}) collective-permute-start(bf16[1024,256]{1,0:T(8,128)(2,1)} %refs_0_.1), channel_id=1, source_target_pairs={{0,1},{1,0},{2,3},{3,2},{4,5},{5,4},{6,7},{7,6},{8,9},{9,8},{10,11... | collective-permute-start | bytes 1572872 | tf_op jit(solution)/shard_map/ppermute | solution.py:347
  15.5 20.2 %copy-start.7 = (bf16[1024,256]{1,0:T(8,128)(2,1)}, bf16[1024,256]{1,0:T(8,128)(2,1)S(1)}, u32[]{:S(2)}) copy-start(bf16[1024,256]{1,0:T(8,128)(2,1)S(1)} %collective-permute-done.1.refs_2_) | copy-start | bytes 1572868
  15.5 15.3 %collective-permute-start.5 = (bf16[1024,256]{1,0:T(8,128)(2,1)S(1)}, bf16[1024,256]{1,0:T(8,128)(2,1)S(1)}, u32[]{:S(2)}, u32[]{:S(2)}) collective-permute-start(bf16[1024,256]{1,0:T(8,128)(2,1)S(1)} %collective-permute-done.1.refs_2_), channel_id=1, source_target_pairs={{0,1},{1,0},{2,3},{3,2},{4,5},{5,4},{6,7},{7,6},{8,9},{9,8},{10,11... | collective-permute-start | bytes 1572872 | tf_op jit(solution)/shard_map/ppermute | solution.py:347
  28.3 7.4 %copy-start.9 = (bf16[1024,256]{1,0:T(8,128)(2,1)}, bf16[1024,256]{1,0:T(8,128)(2,1)S(1)}, u32[]{:S(2)}) copy-start(bf16[1024,256]{1,0:T(8,128)(2,1)S(1)} %collective-permute-done.refs_1_) | copy-start | bytes 1572868
  28.3 2.5 collective-permute-start.4
  28.8 6.9 %copy-start.11 = (bf16[1024,256]{1,0:T(8,128)(2,1)}, bf16[1024,256]{1,0:T(8,128)(2,1)S(1)}, u32[]{:S(2)}) copy-start(bf16[1024,256]{1,0:T(8,128)(2,1)S(1)} %collective-permute-done.2.refs_3_) | copy-start | bytes 1572868
  28.8 2.3 collective-permute-start.6
  29.2 1.2 copy-start.3
  30.8 4.9 %copy-start.13 = (bf16[1024,256]{1,0:T(8,128)(2,1)}, bf16[1024,256]{1,0:T(8,128)(2,1)S(1)}, u32[]{:S(2)}) copy-start(bf16[1024,256]{1,0:T(8,128)(2,1)S(1)} %collective-permute-done.3.refs_4_) | copy-start | bytes 1572868
  30.8 4.9 %copy-start.15 = (bf16[1024,256]{1,0:T(8,128)(2,1)}, bf16[1024,256]{1,0:T(8,128)(2,1)S(1)}, u32[]{:S(2)}) copy-start(bf16[1024,256]{1,0:T(8,128)(2,1)S(1)} %collective-permute-done.5.refs_6_) | copy-start | bytes 1572868
  30.8 4.9 %copy-start.17 = (bf16[1024,256]{1,0:T(8,128)(2,1)}, bf16[1024,256]{1,0:T(8,128)(2,1)S(1)}, u32[]{:S(2)}) copy-start(bf16[1024,256]{1,0:T(8,128)(2,1)S(1)} %collective-permute-done.4.refs_5_) | copy-start | bytes 1572868
  31.1 1.3 copy-start.5
  32.4 3.4 %copy-start.19 = (bf16[1024,256]{1,0:T(8,128)(2,1)}, bf16[1024,256]{1,0:T(8,128)(2,1)S(1)}, u32[]{:S(2)}) copy-start(bf16[1024,256]{1,0:T(8,128)(2,1)S(1)} %collective-permute-done.6.refs_7_) | copy-start | bytes 1572868
  196.2 9.9 %all-to-all-start.14 = ((f32[8,8,128]{2,1,0:T(8,128)}), f32[8,8,128]{2,1,0:T(8,128)S(1)}, u32[]{:S(2)}, u32[]{:S(2)}) async-start(f32[8,8,128]{2,1,0:T(8,128)} %get-tuple-element.91), calls=%async_computation.14 | async-start | bytes 65536 | tf_op jit(solution)/shard_map/all_to_all | solution.py:367
  206.2 5.7 %copy-start.6 = (bf16[1024,256]{1,0:T(8,128)(2,1)S(1)}, bf16[1024,256]{1,0:T(8,128)(2,1)}, u32[]{:S(2)}) copy-start(bf16[1024,256]{1,0:T(8,128)(2,1)} %refs_0_.1) | copy-start | bytes 1572868
  206.2 5.7 %copy-start.8 = (bf16[1024,256]{1,0:T(8,128)(2,1)S(1)}, bf16[1024,256]{1,0:T(8,128)(2,1)}, u32[]{:S(2)}) copy-start(bf16[1024,256]{1,0:T(8,128)(2,1)} %copy-done.7) | copy-start | bytes 1572868
  206.2 5.7 %copy-start.10 = (bf16[1024,256]{1,0:T(8,128)(2,1)S(1)}, bf16[1024,256]{1,0:T(8,128)(2,1)}, u32[]{:S(2)}) copy-start(bf16[1024,256]{1,0:T(8,128)(2,1)} %copy-done.9) | copy-start | bytes 1572868
  206.2 5.7 %copy-start.12 = (bf16[1024,256]{1,0:T(8,128)(2,1)S(1)}, bf16[1024,256]{1,0:T(8,128)(2,1)}, u32[]{:S(2)}) copy-start(bf16[1024,256]{1,0:T(8,128)(2,1)} %copy-done.11) | copy-start | bytes 1572868
  206.2 5.7 %copy-start.14 = (bf16[1024,256]{1,0:T(8,128)(2,1)S(1)}, bf16[1024,256]{1,0:T(8,128)(2,1)}, u32[]{:S(2)}) copy-start(bf16[1024,256]{1,0:T(8,128)(2,1)} %copy-done.13) | copy-start | bytes 1572868
  206.2 5.7 %copy-start.16 = (bf16[1024,256]{1,0:T(8,128)(2,1)S(1)}, bf16[1024,256]{1,0:T(8,128)(2,1)}, u32[]{:S(2)}) copy-start(bf16[1024,256]{1,0:T(8,128)(2,1)} %copy-done.15) | copy-start | bytes 1572868
  206.2 5.7 %copy-start.18 = (bf16[1024,256]{1,0:T(8,128)(2,1)S(1)}, bf16[1024,256]{1,0:T(8,128)(2,1)}, u32[]{:S(2)}) copy-start(bf16[1024,256]{1,0:T(8,128)(2,1)} %copy-done.17) | copy-start | bytes 1572868
  206.2 5.7 %copy-start.20 = (bf16[1024,256]{1,0:T(8,128)(2,1)S(1)}, bf16[1024,256]{1,0:T(8,128)(2,1)}, u32[]{:S(2)}) copy-start(bf16[1024,256]{1,0:T(8,128)(2,1)} %copy-done.19) | copy-start | bytes 1572868
  211.1 11.2 %collective-permute-start.7 = (bf16[4,1024,256]{2,1,0:T(8,128)(2,1)}, bf16[4,1024,256]{2,1,0:T(8,128)(2,1)}, u32[]{:S(2)}, u32[]{:S(2)}) collective-permute-start(bf16[4,1024,256]{2,1,0:T(8,128)(2,1)} %get-tuple-element.95), channel_id=1, source_target_pairs={{0,1},{1,0},{2,3},{3,2},{4,5},{5,4},{6,7},{7,6},{8,9},{9,8},{10,11... | collective-permute-start | bytes 6291464 | tf_op jit(solution)/shard_map/ppermute | solution.py:347
  212.0 10.3 %copy-start.1 = (bf16[512,2048]{1,0:T(8,128)(2,1)S(1)}, bf16[512,2048]{1,0:T(8,128)(2,1)}, u32[]{:S(2)}) copy-start(bf16[512,2048]{1,0:T(8,128)(2,1)} %cent.3) | copy-start | bytes 6291460
  215.4 14.0 %collective-permute-start.11 = (bf16[128,1792]{1,0:T(8,128)(2,1)}, bf16[128,1792]{1,0:T(8,128)(2,1)}, u32[]{:S(2)}, u32[]{:S(2)}) collective-permute-start(bf16[128,1792]{1,0:T(8,128)(2,1)} %get-tuple-element.102), channel_id=1, source_target_pairs={{0,8},{8,16},{16,24},{24,0},{1,9},{9,17},{17,25},{25,1},{2,10},{10... | collective-permute-start | bytes 1376264 | tf_op jit(solution)/shard_map/ppermute | solution.py:347
  215.7 22.9 %collective-permute-start.12 = (bf16[128,1792]{1,0:T(8,128)(2,1)}, bf16[128,1792]{1,0:T(8,128)(2,1)}, u32[]{:S(2)}, u32[]{:S(2)}) collective-permute-start(bf16[128,1792]{1,0:T(8,128)(2,1)} %get-tuple-element.103), channel_id=1, source_target_pairs={{0,16},{8,24},{16,0},{24,8},{1,17},{9,25},{17,1},{25,9},{2,18},{10... | collective-permute-start | bytes 1376264 | tf_op jit(solution)/shard_map/ppermute | solution.py:347
  217.8 21.4 %collective-permute-start.13 = (bf16[128,1792]{1,0:T(8,128)(2,1)}, bf16[128,1792]{1,0:T(8,128)(2,1)}, u32[]{:S(2)}, u32[]{:S(2)}) collective-permute-start(bf16[128,1792]{1,0:T(8,128)(2,1)} %get-tuple-element.104), channel_id=1, source_target_pairs={{0,24},{8,0},{16,8},{24,16},{1,25},{9,1},{17,9},{25,17},{2,26},{10... | collective-permute-start | bytes 1376264 | tf_op jit(solution)/shard_map/ppermute | solution.py:347
  218.6 22.9 %all-to-all-start.16 = ((bf16[8,64,256]{2,1,0:T(8,128)(2,1)}), bf16[8,64,256]{2,1,0:T(8,128)(2,1)S(1)}, u32[]{:S(2)}, u32[]{:S(2)}) async-start(bf16[8,64,256]{2,1,0:T(8,128)(2,1)} %get-tuple-element.105), calls=%async_computation.16 | async-start | bytes 524288 | tf_op jit(solution)/shard_map/all_to_all | solution.py:457
  222.3 1.2 copy-start.2
  223.5 15.7 %copy-start.4 = (f32[128,1792]{1,0:T(8,128)S(1)}, f32[128,1792]{1,0:T(8,128)}, u32[]{:S(2)}) copy-start(f32[128,1792]{1,0:T(8,128)} %get-tuple-element.101.first) | copy-start | bytes 2752516
  226.4 0.8 copy-start.21
  227.3 0.8 copy-start.23
  228.0 0.8 copy-start.25
  228.8 16.1 %copy-start.26 = (bf16[1024,256]{1,0:T(8,128)(2,1)S(1)}, bf16[1024,256]{1,0:T(8,128)(2,1)}, u32[]{:S(2)}) copy-start(bf16[1024,256]{1,0:T(8,128)(2,1)} %copy-done.25) | copy-start | bytes 1572868
  228.8 16.5 %copy-start.24 = (bf16[1024,256]{1,0:T(8,128)(2,1)S(1)}, bf16[1024,256]{1,0:T(8,128)(2,1)}, u32[]{:S(2)}) copy-start(bf16[1024,256]{1,0:T(8,128)(2,1)} %copy-done.23) | copy-start | bytes 1572868
  228.8 18.3 %copy-start.22 = (bf16[1024,256]{1,0:T(8,128)(2,1)S(1)}, bf16[1024,256]{1,0:T(8,128)(2,1)}, u32[]{:S(2)}) copy-start(bf16[1024,256]{1,0:T(8,128)(2,1)} %copy-done.21) | copy-start | bytes 1572868
  241.5 30.3 %all-to-all-start.15 = ((bf16[8,16,1792]{2,1,0:T(8,128)(2,1)}), bf16[8,16,1792]{2,1,0:T(8,128)(2,1)S(1)}, u32[]{:S(2)}, u32[]{:S(2)}) async-start(bf16[8,16,1792]{2,1,0:T(8,128)(2,1)} %shard_map.71), calls=%async_computation.15 | async-start | bytes 917504 | tf_op jit(solution)/shard_map/all_to_all | solution.py:467
  245.0 14.2 %collective-permute-start.8 = (bf16[1024,256]{1,0:T(8,128)(2,1)S(1)}, bf16[1024,256]{1,0:T(8,128)(2,1)S(1)}, u32[]{:S(2)}, u32[]{:S(2)}) collective-permute-start(bf16[1024,256]{1,0:T(8,128)(2,1)S(1)} %copy-done.26), channel_id=1, source_target_pairs={{0,2},{2,4},{4,6},{6,0},{1,3},{3,5},{5,7},{7,1},{8,10},{10,12},{12... | collective-permute-start | bytes 1572872 | tf_op jit(solution)/shard_map/ppermute | solution.py:347
  245.4 23.9 %collective-permute-start.9 = (bf16[1024,256]{1,0:T(8,128)(2,1)S(1)}, bf16[1024,256]{1,0:T(8,128)(2,1)S(1)}, u32[]{:S(2)}, u32[]{:S(2)}) collective-permute-start(bf16[1024,256]{1,0:T(8,128)(2,1)S(1)} %copy-done.24), channel_id=1, source_target_pairs={{0,4},{2,6},{4,0},{6,2},{1,5},{3,7},{5,1},{7,3},{8,12},{10,14},{12... | collective-permute-start | bytes 1572872 | tf_op jit(solution)/shard_map/ppermute | solution.py:347
  247.1 23.6 %collective-permute-start.10 = (bf16[1024,256]{1,0:T(8,128)(2,1)S(1)}, bf16[1024,256]{1,0:T(8,128)(2,1)S(1)}, u32[]{:S(2)}, u32[]{:S(2)}) collective-permute-start(bf16[1024,256]{1,0:T(8,128)(2,1)S(1)} %copy-done.22), channel_id=1, source_target_pairs={{0,6},{2,0},{4,2},{6,4},{1,7},{3,1},{5,3},{7,5},{8,14},{10,8},{12,... | collective-permute-start | bytes 1572872 | tf_op jit(solution)/shard_map/ppermute | solution.py:347
  248.0 23.8 %collective-permute-start.14 = (bf16[16,256]{1,0:T(8,128)(2,1)S(1)}, bf16[16,256]{1,0:T(8,128)(2,1)S(1)}, u32[]{:S(2)}, u32[]{:S(2)}) collective-permute-start(bf16[16,256]{1,0:T(8,128)(2,1)S(1)} %get-tuple-element.107), channel_id=1, source_target_pairs={{0,8},{8,16},{16,24},{24,0},{1,9},{9,17},{17,25},{25,1},{2,10},{10... | collective-permute-start | bytes 24584 | tf_op jit(solution)/shard_map/ppermute | solution.py:347
  249.2 22.6 %collective-permute-start.15 = (bf16[16,256]{1,0:T(8,128)(2,1)S(1)}, bf16[16,256]{1,0:T(8,128)(2,1)S(1)}, u32[]{:S(2)}, u32[]{:S(2)}) collective-permute-start(bf16[16,256]{1,0:T(8,128)(2,1)S(1)} %get-tuple-element.108), channel_id=1, source_target_pairs={{0,16},{8,24},{16,0},{24,8},{1,17},{9,25},{17,1},{25,9},{2,18},{10... | collective-permute-start | bytes 24584 | tf_op jit(solution)/shard_map/ppermute | solution.py:347
  259.2 12.6 %collective-permute-start.16 = (bf16[16,256]{1,0:T(8,128)(2,1)S(1)}, bf16[16,256]{1,0:T(8,128)(2,1)S(1)}, u32[]{:S(2)}, u32[]{:S(2)}) collective-permute-start(bf16[16,256]{1,0:T(8,128)(2,1)S(1)} %get-tuple-element.109), channel_id=1, source_target_pairs={{0,24},{8,0},{16,8},{24,16},{1,25},{9,1},{17,9},{25,17},{2,26},{10... | collective-permute-start | bytes 24584 | tf_op jit(solution)/shard_map/ppermute | solution.py:347

commit v5 on v4

--- a/solution.py
+++ b/solution.py
@@ -94,11 +94,25 @@
     return pl.ds(pl.multiple_of(at * width, L), width)
 
 
-def k_logits(scale, cent, *refs):
-    n = len(refs) - 3
-    pieces, (logits, send, held) = refs[:n], refs[n:]
-    for k, piece in enumerate(pieces):
-        held[:, span(source(n // 2, k), piece.shape[1])] = piece[...]
+def grouped(refs, counts):
+    out, at = [], 0
+    for c in counts:
+        out.append(refs[at : at + c])
+        at += c
+    return out
+
+
+def k_logits(scale, counts, cent, *refs):
+    n = len(counts)
+    pieces, (logits, send, whole, held, sem) = grouped(refs, counts), refs[sum(counts) :]
+    for k, blocks in enumerate(pieces):
+        at = 0
+        for block in blocks:
+            rows = slice(at, at + block.shape[0])
+            held[rows, span(source(n // 2, k), block.shape[1])] = block[...]
+            at += block.shape[0]
+    copy = pltpu.make_async_copy(held, whole, sem)
+    copy.start()
     logits[...] = scale * lax.dot_general(cent[...], held[...], NT, preferred_element_type=F32)
     count = logits.shape[1] // L
     tops, sums = [], []
@@ -109,6 +123,7 @@
         sums.append(jnp.sum(jnp.exp(tile - top), axis=0, keepdims=True))
     send[:, 0] = jnp.broadcast_to(jnp.concatenate(tops, axis=0)[None], send[:, 0].shape)
     send[:, 1] = jnp.broadcast_to(jnp.concatenate(sums, axis=0)[None], send[:, 1].shape)
+    copy.wait()
 
 
 def k_first_col(logits, recv, row_pot, send):
@@ -230,29 +245,26 @@
         base[:, r * L : (r + 1) * L] = tile * inner
 
 
-def k_adjoint(scale, base, first, recv, cent_hbm, adjoint, turned_hbm, cross, cent, turned, sems):
-    copy = pltpu.make_async_copy(cent_hbm, cent, sems.at[0])
-    copy.start()
+def k_adjoint(base, first, recv, adjoint, turned):
     y = -total(recv)
     for r in range(y.shape[0]):
         tile = lanes(base, r) - lanes(first, r).astype(F32) * y[r : r + 1, :]
         tile = tile.astype(BF16)
         adjoint[:, r * L : (r + 1) * L] = tile
         turned[r * L : (r + 1) * L, :] = tile.T
-    back = pltpu.make_async_copy(turned, turned_hbm, sems.at[1])
-    back.start()
-    copy.wait()
-    ny, _, width = cross.shape
-    for k in range(ny):
-        block = cent[:, span(target(ny, k, True), width)]
-        part = scale * lax.dot_general(turned[...], block, NN, preferred_element_type=F32)
-        cross[k] = part.astype(BF16)
-    back.wait()
-
-
-def k_cent(scale, n, nx, adjoint, *refs):
-    pieces, straight, keep = refs[:n], refs[n], refs[n + 1]
-    sends, (picked, wide, own, narrow, sems) = refs[n + 2 : n + 1 + nx], refs[n + 1 + nx :]
+
+
+def k_cent(scale, n, nx, adjoint, whole_hbm, straight, keep, *refs):
+    sends, (whole, picked, wide, own, narrow, sems, in_sems) = refs[: nx - 1], refs[nx - 1 :]
+    width = whole.shape[2]
+    copies = [
+        pltpu.make_async_copy(
+            whole_hbm.at[:, span(source(n // 2, p), width)], whole.at[p], in_sems.at[p]
+        )
+        for p in range(n)
+    ]
+    for p in (*by_x(n), *by_z()):
+        copies[p].start()
     per = keep.shape[0]
     group = 16
     for k in range(nx):
@@ -260,34 +272,72 @@
         for iz in range(per // group):
             at = pl.multiple_of((iz * nx + to) * group, group)
             picked[k * per + iz * group : k * per + (iz + 1) * group, :] = adjoint[pl.ds(at, group), :]
-    width = pieces[0].shape[1]
     outs = []
 
     def leave(src, dst):
         outs.append(pltpu.make_async_copy(src, dst, sems.at[len(outs)]))
         outs[-1].start()
 
-    for i, p in enumerate(by_z()):
-        part = scale * lax.dot_general(adjoint[...], pieces[p][...], NN, preferred_element_type=F32)
-        narrow[i] = part.astype(BF16).reshape(narrow.shape[1:])
-        leave(narrow.at[i], straight.at[:, :, pl.ds(i * width, width)])
+    def product(left, p):
+        copies[p].wait()
+        return scale * lax.dot_general(left[...], whole[p], NN, preferred_element_type=F32)
+
     for i, p in enumerate(by_x(n)):
-        part = scale * lax.dot_general(picked[...], pieces[p][...], NN, preferred_element_type=F32)
-        own[i] = part[:per, :]
-        leave(own.at[i], keep.at[:, pl.ds(i * width, width)])
+        part = product(picked, p)
         for k in range(1, nx):
             wide[i, k - 1] = part[k * per : (k + 1) * per, :].astype(BF16)
             leave(wide.at[i, k - 1], sends[k - 1].at[:, pl.ds(i * width, width)])
+        own[i] = part[:per, :]
+        leave(own.at[i], keep.at[:, pl.ds(i * width, width)])
+    for i, p in enumerate(by_z()):
+        part = product(adjoint, p)
+        narrow[i] = part.astype(BF16).reshape(narrow.shape[1:])
+        leave(narrow.at[i], straight.at[:, :, pl.ds(i * width, width)])
     for c in outs:
         c.wait()
 
 
-def k_pair(scale, turned, cent, cross, first, *rest):
+def k_cross(scale, turned, cent, cross_hbm, turned_hbm, cross, sems):
     ny, _, width = cross.shape
-    for k, out in enumerate((first, *rest)):
+    outs = [pltpu.make_async_copy(turned, turned_hbm, sems.at[ny])]
+    outs[0].start()
+    for k in range(ny):
+        block = cent[:, span(target(ny, k, True), width)]
+        part = scale * lax.dot_general(turned[...], block, NN, preferred_element_type=F32)
+        cross[k] = part.astype(BF16)
+        outs.append(pltpu.make_async_copy(cross.at[k], cross_hbm.at[k], sems.at[k]))
+        outs[-1].start()
+    for c in outs:
+        c.wait()
+
+
+def k_pair(scale, turned_hbm, cent, cross_hbm, first, *refs):
+    rest, (turned, cross, own, stage, sems, out_sems) = refs[:-6], refs[-6:]
+    ny, _, width = cross.shape
+    bring = pltpu.make_async_copy(turned_hbm, turned, sems.at[ny])
+    bring.start()
+    copies = [
+        pltpu.make_async_copy(cross_hbm.at[k], cross.at[k], sems.at[k]) for k in range(ny)
+    ]
+    for k in range(ny - 1, -1, -1):
+        copies[k].start()
+    bring.wait()
+    outs = []
+    for k in range(ny - 1, -1, -1):
         block = cent[:, span(target(ny, k, False), width)]
         part = scale * lax.dot_general(turned[...], block, NN, preferred_element_type=F32)
-        out[...] = (part + cross[k].astype(F32)).astype(out.dtype)
+        copies[k].wait()
+        part = part + cross[k].astype(F32)
+        if k:
+            stage[k - 1] = part.astype(BF16)
+            src, dst = stage.at[k - 1], rest[k - 1]
+        else:
+            own[...] = part
+            src, dst = own, first
+        outs.append(pltpu.make_async_copy(src, dst, out_sems.at[k]))
+        outs[-1].start()
+    for c in outs:
+        c.wait()
 
 
 def k_early(recv, keep, *refs):
@@ -357,11 +407,15 @@
     log_b = math.log(ratio)
     rv, cv = (rows // L, L), (cols // L, L)
 
-    mine = [embeddings] + [shift(embeddings, "y", k) for k in range(1, ny)]
-    theirs = [shift(m, "core", 1) for m in mine]
+    half = rows // 2
+    left, right = shift(embeddings, "y", 1), shift(embeddings, "y", ny - 1)
+    opposite = [shift(left[:half], "y", 1), shift(right[half:], "y", ny - 1)]
+    mine = [[embeddings], [left], opposite, [right]]
+    theirs = [[shift(m, "core", 1) for m in blocks] for blocks in mine]
     (grad,) = call(k_prepare, [((cols, rows), BF16)], plan_grad)
-    mine[0], grad = lax.optimization_barrier((mine[0], grad))
-    pieces = [*mine, *theirs]
+    mine[0][0], grad = lax.optimization_barrier((mine[0][0], grad))
+    counts = [len(blocks) for blocks in (*mine, *theirs)]
+    pieces = [m for blocks in (*mine, *theirs) for m in blocks]
 
     def over_clus(send):
         return lax.all_to_all(send, ("y", "core"), 0, 0, tiled=True)
@@ -375,12 +429,12 @@
     a_row, a_col = (rv, F32), (cv, F32)
 
     work = 2 * rows * cols * depth
-    logits, send = call(
-        functools.partial(k_logits, scale),
-        [block, row_pair],
+    logits, send, whole = call(
+        functools.partial(k_logits, scale, counts),
+        [block, row_pair, ((rows, depth), BF16)],
         centroids, *pieces,
-        limit=LARGE, flops=work,
-        scratch=[pltpu.VMEM((rows, depth), BF16)],
+        limit=LARGE, flops=work, hbm_out=(2,),
+        scratch=[pltpu.VMEM((rows, depth), BF16), pltpu.SemaphoreType.DMA],
     )
     row_pot, send = call(k_first_col, [a_row, col_pair], logits, over_clus(send))
     col_pot, weights, send = call(
@@ -425,41 +479,53 @@
         weights, grad, col_pot, *row_mul, *col_mul, *col_adj, *row_adj,
         flops=work, alias={0: 0, 1: 1},
     )
-    per, n = cols // nx, len(pieces)
-    adjoint, turned, cross = call(
-        functools.partial(k_adjoint, scale),
-        [((cols, rows), BF16), ((rows, cols), BF16), ((ny, rows, width), BF16)],
-        base, first, recv, pltpu.with_memory_space_constraint(centroids, pltpu.HBM),
-        limit=LARGE, flops=work // 2, hbm_in=(3,), hbm_out=(1,),
-        scratch=[
-            pltpu.VMEM((cols, depth), BF16),
-            pltpu.VMEM((rows, cols), BF16),
-            pltpu.SemaphoreType.DMA((2,)),
-        ],
-    )
-    cross = shift(cross, "core", 1)
+    per, n = cols // nx, len(counts)
+    adjoint, turned = call(
+        k_adjoint,
+        [((cols, rows), BF16), ((rows, cols), BF16)],
+        base, first, recv,
+    )
     wide, narrow = len(by_x(n)) * width, len(by_z()) * width
     straight, near, *parts = call(
         functools.partial(k_cent, scale, n, nx),
         [((nz, cols // nz, narrow), BF16), ((per, wide), F32)]
         + [((per, wide), BF16)] * (nx - 1),
-        adjoint, *pieces,
-        limit=LARGE, flops=work, hbm_out=range(1 + nx),
+        adjoint, pltpu.with_memory_space_constraint(whole, pltpu.HBM),
+        limit=LARGE, flops=work, hbm_in=(1,), hbm_out=range(1 + nx),
         scratch=[
+            pltpu.VMEM((n, rows, width), BF16),
             pltpu.VMEM((cols, rows), BF16),
             pltpu.VMEM((len(by_x(n)), nx - 1, per, width), BF16),
             pltpu.VMEM((len(by_x(n)), per, width), F32),
             pltpu.VMEM((len(by_z()), nz, cols // nz, width), BF16),
             pltpu.SemaphoreType.DMA((n * nx,)),
+            pltpu.SemaphoreType.DMA((n,)),
         ],
     )
     parts = [shift(p, "x", k + 1) for k, p in enumerate(parts)]
+    cross, turned = call(
+        functools.partial(k_cross, scale),
+        [((ny, rows, width), BF16), ((rows, cols), BF16)],
+        turned, centroids,
+        limit=LARGE, flops=work // 2, hbm_out=(0, 1),
+        scratch=[pltpu.VMEM((ny, rows, width), BF16), pltpu.SemaphoreType.DMA((ny + 1,))],
+    )
+    cross = shift(cross, "core", 1)
     straight = lax.all_to_all(straight, "z", 0, 0, tiled=True)
     own, *moved = call(
         functools.partial(k_pair, scale),
         [((rows, width), F32)] + [((rows, width), BF16)] * (ny - 1),
-        turned, centroids, cross,
-        limit=LARGE, flops=work // 2,
+        pltpu.with_memory_space_constraint(turned, pltpu.HBM), centroids,
+        pltpu.with_memory_space_constraint(cross, pltpu.HBM),
+        limit=LARGE, flops=work // 2, hbm_in=(0, 2), hbm_out=range(ny),
+        scratch=[
+            pltpu.VMEM((rows, cols), BF16),
+            pltpu.VMEM((ny, rows, width), BF16),
+            pltpu.VMEM((rows, width), F32),
+            pltpu.VMEM((ny - 1, rows, width), BF16),
+            pltpu.SemaphoreType.DMA((ny + 1,)),
+            pltpu.SemaphoreType.DMA((ny,)),
+        ],
     )
     near, own = lax.optimization_barrier((near, own))
     moved = [shift(m, "y", k + 1) for k, m in enumerate(moved)]

time: 277 us -> 277 us (level)
  waiting for transfers between devices: 42.5 us -> 36.4 us
  Pallas kernels: 26 us -> 31 us
  local copies, waits for them, and re-layouts: 6.23 us -> 3.01 us
  starting transfers between devices: 41.3 us -> 44.3 us
    ppermute x17 -> x19, waiting for transfers between devices: 40 us -> 33.8 us  [shift(): return lax.ppermute(value, axis, [(i, (i + step) % n) for i in range(n)])]
    pallas_call x24 -> x25, Pallas kernels: 26 us -> 31 us  [call(): pl.pallas_call(body, out_shape=[pltpu.HBM(s, d) if i in hbm_out else jax....]
    unnamed x54 -> x14, local copies, waits for them, and re-layouts: 6.23 us -> 2.98 us
    ppermute x17 -> x19, starting transfers between devices: 29 us -> 32.2 us  [shift(): return lax.ppermute(value, axis, [(i, (i + step) % n) for i in range(n)])]
  transfers between devices with their start and end apart: 20 -> 22, of which waited for: 10 -> 9; matrix products, arithmetic and copies ran while one was open for 0% -> 0% of each run, Pallas kernels for 4% -> 7%
where the time goes in v5:
time: 277 us; the launch traced here: 272 us
  blocking collectives  157 us (57%)
  starting transfers between devices  44.3 us (16%)
  waiting for transfers between devices  36.4 us (13%)
  Pallas kernels  31 us (11%)
  local copies, waits for them, and re-layouts  3.01 us (1%)
    all_to_all x7, blocking collectives, over_prog(): return lax.all_to_all(send, ('z', 'x'), 0, 0, tiled=True)  92.4 us
    all_to_all x7, blocking collectives, over_clus(): return lax.all_to_all(send, ('y', 'core'), 0, 0, tiled=True)  64.2 us
    ppermute x19, waiting for transfers between devices, shift(): return lax.ppermute(value, axis, [(i, (i + step) % n) for i in range(n)])  33.8 us
    ppermute x19, starting transfers between devices, shift(): return lax.ppermute(value, axis, [(i, (i + step) % n) for i in range(n)])  32.2 us
    pallas_call x25, Pallas kernels, call(): pl.pallas_call(body, out_shape=[pltpu.HBM(s, d) if i in hbm_out else jax....  31 us
  transfers between devices with their start and end apart: 22, of which 9 were waited for; matrix products, arithmetic and copies ran while one was open for 0% of the time, Pallas kernels for 7%

profile of v5, /device:TPU:1, one launch (start us, length us, event | category | flops | bytes accessed | tf_op | source)
XLA Modules:
  0.0 272.3 jit_solution(766085852624985312)
XLA Ops:
  0.6 2.2 collective-permute-start
  2.8 1.5 collective-permute-start.2
  4.4 2.8 %collective-permute-start.4 = (bf16[1024,256]{1,0:T(8,128)(2,1)}, bf16[1024,256]{1,0:T(8,128)(2,1)S(1)}, u32[]{:S(2)}, u32[]{:S(2)}) collective-permute-start(bf16[1024,256]{1,0:T(8,128)(2,1)} %refs_0_), channel_id=1, source_target_pairs={{0,1},{1,0},{2,3},{3,2},{4,5},{5,4},{6,7},{7,6},{8,9},{9,8},{10,11... | collective-permute-start | bytes 1572872 | tf_op jit(solution)/shard_map/ppermute | solution.py:397
  7.2 7.0 %collective-permute-done.refs_1_ = bf16[1024,256]{1,0:T(8,128)(2,1)S(1)} collective-permute-done((bf16[1024,256]{1,0:T(8,128)(2,1)}, bf16[1024,256]{1,0:T(8,128)(2,1)S(1)}, u32[]{:S(2)}, u32[]{:S(2)}) %collective-permute-start) | collective-permute-done | bytes 524320 | tf_op jit(solution)/shard_map/ppermute | solution.py:397
  14.2 1.6 collective-permute-start.1
  15.8 1.7 collective-permute-start.3
  17.5 3.3 %collective-permute-start.5 = (bf16[1024,256]{1,0:T(8,128)(2,1)S(1)}, bf16[1024,256]{1,0:T(8,128)(2,1)S(1)}, u32[]{:S(2)}, u32[]{:S(2)}) collective-permute-start(bf16[1024,256]{1,0:T(8,128)(2,1)S(1)} %collective-permute-done.refs_1_), channel_id=1, source_target_pairs={{0,1},{1,0},{2,3},{3,2},{4,5},{5,4},{6,7},{7,6},{8,9},{9,8},{10,11... | collective-permute-start | bytes 1572872 | tf_op jit(solution)/shard_map/ppermute | solution.py:397
  21.2 3.9 %collective-permute-start.6 = (bf16[512,256]{1,0:T(8,128)(2,1)S(1)}, bf16[512,256]{1,0:T(8,128)(2,1)S(1)}, u32[]{:S(2)}, u32[]{:S(2)}) collective-permute-start(bf16[512,256]{1,0:T(8,128)(2,1)S(1)} %collective-permute-done.1.refs_2_), channel_id=1, source_target_pairs={{0,1},{1,0},{2,3},{3,2},{4,5},{5,4},{6,7},{7,6},{8,9},{9,8},{10,11... | collective-permute-start | bytes 786440 | tf_op jit(solution)/shard_map/ppermute | solution.py:397
  25.1 1.2 copy-done.4
  27.3 3.3 %shard_map.51 = (f32[512,1024]{1,0:T(8,128)S(1)}, f32[8,2,8,128]{3,2,1,0:T(8,128)S(1)}, bf16[1024,2048]{1,0:T(8,128)(2,1)}) custom-call(bf16[512,2048]{1,0:T(8,128)(2,1)S(1)} %copy-done, bf16[1024,256]{1,0:T(8,128)(2,1)S(1)} %copy-done.6, bf16[1024,256]{1,0:T(8,128)(2,1)S(1)} %collective-permute-done.refs_1_, ...), custom_call_target="tpu_custom_call" | custom-call | flops 2147483648 | bytes 6291456 | tf_op jit(solution)/shard_map/pallas_call | solution.py:380
  30.6 9.4 %all_to_all.85.recv = f32[8,2,8,128]{3,2,1,0:T(8,128)S(1)} all-to-all(f32[8,2,8,128]{3,2,1,0:T(8,128)S(1)} %get-tuple-element.60), channel_id=1, replica_groups=mesh['z'=8,'x'=4,'y'=4,'core'=2] {'y','core'}, dimensions={0} | all-to-all | bytes 131072 | tf_op jit(solution)/shard_map/all_to_all | solution.py:421
  40.6 20.8 %all_to_all.86.recv = f32[32,2,4,128]{3,2,1,0:T(4,128)S(1)} all-to-all(f32[32,2,4,128]{3,2,1,0:T(4,128)S(1)} %get-tuple-element.62), channel_id=1, replica_groups=mesh['z'=8,'x'=4,'y'=4,'core'=2] {'z','x'}, dimensions={0} | all-to-all | bytes 262144 | tf_op jit(solution)/shard_map/all_to_all | solution.py:424
  61.8 9.3 %all_to_all.87.recv = f32[8,8,128]{2,1,0:T(8,128)S(1)} all-to-all(f32[8,8,128]{2,1,0:T(8,128)S(1)} %get-tuple-element.66), channel_id=1, replica_groups=mesh['z'=8,'x'=4,'y'=4,'core'=2] {'y','core'}, dimensions={0} | all-to-all | bytes 65536 | tf_op jit(solution)/shard_map/all_to_all | solution.py:421
  71.4 11.8 %all_to_all.88.recv = f32[32,4,128]{2,1,0:T(4,128)S(1)} all-to-all(f32[32,4,128]{2,1,0:T(4,128)S(1)} %get-tuple-element.68), channel_id=1, replica_groups=mesh['z'=8,'x'=4,'y'=4,'core'=2] {'z','x'}, dimensions={0} | all-to-all | bytes 131072 | tf_op jit(solution)/shard_map/all_to_all | solution.py:424
  83.4 9.2 %all_to_all.89.recv = f32[8,8,128]{2,1,0:T(8,128)S(1)} all-to-all(f32[8,8,128]{2,1,0:T(8,128)S(1)} %get-tuple-element.69), channel_id=1, replica_groups=mesh['z'=8,'x'=4,'y'=4,'core'=2] {'y','core'}, dimensions={0} | all-to-all | bytes 65536 | tf_op jit(solution)/shard_map/all_to_all | solution.py:421
  92.9 11.8 %all_to_all.90.recv = f32[32,4,128]{2,1,0:T(4,128)S(1)} all-to-all(f32[32,4,128]{2,1,0:T(4,128)S(1)} %get-tuple-element.71), channel_id=1, replica_groups=mesh['z'=8,'x'=4,'y'=4,'core'=2] {'z','x'}, dimensions={0} | all-to-all | bytes 131072 | tf_op jit(solution)/shard_map/all_to_all | solution.py:424
  105.0 9.1 %all_to_all.91.recv = f32[8,8,128]{2,1,0:T(8,128)S(1)} all-to-all(f32[8,8,128]{2,1,0:T(8,128)S(1)} %get-tuple-element.72), channel_id=1, replica_groups=mesh['z'=8,'x'=4,'y'=4,'core'=2] {'y','core'}, dimensions={0} | all-to-all | bytes 65536 | tf_op jit(solution)/shard_map/all_to_all | solution.py:421
  114.5 12.4 %all_to_all.92.recv = f32[32,2,4,128]{3,2,1,0:T(4,128)S(1)} all-to-all(f32[32,2,4,128]{3,2,1,0:T(4,128)S(1)} %get-tuple-element.76), channel_id=1, replica_groups=mesh['z'=8,'x'=4,'y'=4,'core'=2] {'z','x'}, dimensions={0} | all-to-all | bytes 262144 | tf_op jit(solution)/shard_map/all_to_all | solution.py:424
  127.4 9.2 %all_to_all.93.recv = f32[8,8,128]{2,1,0:T(8,128)S(1)} all-to-all(f32[8,8,128]{2,1,0:T(8,128)S(1)} %get-tuple-element.78), channel_id=1, replica_groups=mesh['z'=8,'x'=4,'y'=4,'core'=2] {'y','core'}, dimensions={0} | all-to-all | bytes 65536 | tf_op jit(solution)/shard_map/all_to_all | solution.py:421
  136.8 11.9 %all_to_all.94.refs_1_ = f32[32,4,128]{2,1,0:T(4,128)S(1)} all-to-all(f32[32,4,128]{2,1,0:T(4,128)S(1)} %get-tuple-element.79), channel_id=1, replica_groups=mesh['z'=8,'x'=4,'y'=4,'core'=2] {'z','x'}, dimensions={0} | all-to-all | bytes 131072 | tf_op jit(solution)/shard_map/all_to_all | solution.py:424
  149.0 9.0 %all_to_all.95.recv = f32[8,8,128]{2,1,0:T(8,128)S(1)} all-to-all(f32[8,8,128]{2,1,0:T(8,128)S(1)} %get-tuple-element.80), channel_id=1, replica_groups=mesh['z'=8,'x'=4,'y'=4,'core'=2] {'y','core'}, dimensions={0} | all-to-all | bytes 65536 | tf_op jit(solution)/shard_map/all_to_all | solution.py:421
  158.3 11.8 %all_to_all.96.refs_1_ = f32[32,4,128]{2,1,0:T(4,128)S(1)} all-to-all(f32[32,4,128]{2,1,0:T(4,128)S(1)} %get-tuple-element.81), channel_id=1, replica_groups=mesh['z'=8,'x'=4,'y'=4,'core'=2] {'z','x'}, dimensions={0} | all-to-all | bytes 131072 | tf_op jit(solution)/shard_map/all_to_all | solution.py:424
  170.4 9.1 %all_to_all.97.recv = f32[8,8,128]{2,1,0:T(8,128)S(1)} all-to-all(f32[8,8,128]{2,1,0:T(8,128)S(1)} %get-tuple-element.82), channel_id=1, replica_groups=mesh['z'=8,'x'=4,'y'=4,'core'=2] {'y','core'}, dimensions={0} | all-to-all | bytes 65536 | tf_op jit(solution)/shard_map/all_to_all | solution.py:421
  179.7 11.8 %all_to_all.98.refs_0_ = f32[32,4,128]{2,1,0:T(4,128)S(1)} all-to-all(f32[32,4,128]{2,1,0:T(4,128)S(1)} %get-tuple-element.83), channel_id=1, replica_groups=mesh['z'=8,'x'=4,'y'=4,'core'=2] {'z','x'}, dimensions={0} | all-to-all | bytes 131072 | tf_op jit(solution)/shard_map/all_to_all | solution.py:424
  191.5 0.9 shard_map.65
  192.4 5.2 %all-to-all-start.14 = ((f32[8,8,128]{2,1,0:T(8,128)}), f32[8,8,128]{2,1,0:T(8,128)S(1)}, u32[]{:S(2)}, u32[]{:S(2)}) async-start(f32[8,8,128]{2,1,0:T(8,128)} %get-tuple-element.93), calls=%async_computation.14 | async-start | bytes 65536 | tf_op jit(solution)/shard_map/all_to_all | solution.py:421
  197.6 2.2 shard_map.66
  199.8 2.5 all-to-all-done.14.recv
  202.8 1.1 copy-done.1
  203.9 2.4 shard_map.69
  206.3 0.8 collective-permute-start.9
  207.1 7.8 %shard_map.68 = (bf16[8,64,256]{2,1,0:T(8,128)(2,1)}, f32[128,1792]{1,0:T(8,128)}, bf16[128,1792]{1,0:T(8,128)(2,1)}, bf16[128,1792]{1,0:T(8,128)(2,1)}, bf16[128,1792]{1,0:T(8,128)(2,1)}) custom-call(bf16[512,1024]{1,0:T(8,128)(2,1)S(1)} %get-tuple-element.94.adjoint, bf16[1024,2048]{1,0:T(8,128)(2,1)} %get-tuple-element.95.whole_hbm), custom_call_target="tpu_custom_call" | custom-call | flops 2147483648 | bytes 5242880 | tf_op jit(solution)/shard_map/pallas_call | solution.py:380
  215.5 2.1 collective-permute-start.14
  218.3 3.4 %all-to-all-start.16 = ((bf16[8,64,256]{2,1,0:T(8,128)(2,1)}), bf16[8,64,256]{2,1,0:T(8,128)(2,1)S(1)}, u32[]{:S(2)}, u32[]{:S(2)}) async-start(bf16[8,64,256]{2,1,0:T(8,128)(2,1)} %get-tuple-element.109), calls=%async_computation.16 | async-start | bytes 524288 | tf_op jit(solution)/shard_map/all_to_all | solution.py:514
  221.8 5.8 %shard_map.70 = (f32[1024,256]{1,0:T(8,128)}, bf16[1024,256]{1,0:T(8,128)(2,1)}, bf16[1024,256]{1,0:T(8,128)(2,1)}, bf16[1024,256]{1,0:T(8,128)(2,1)}) custom-call(bf16[1024,512]{1,0:T(8,128)(2,1)} %get-tuple-element.98.turned_hbm, bf16[512,2048]{1,0:T(8,128)(2,1)S(1)} %copy-done.2, bf16[4,1024,256]{2,1,0:T(8,128)(2,1)} %collective-permute-done.9.cross_hbm), custom_call_target="tpu_custom_call" | custom-call | flops 1073741824 | bytes 5242880 | tf_op jit(solution)/shard_map/pallas_call | solution.py:380
  227.6 1.4 collective-permute-done.13.refs_0_
  229.0 9.2 %collective-permute-done.14.refs_1_ = bf16[128,1792]{1,0:T(8,128)(2,1)S(1)} collective-permute-done((bf16[128,1792]{1,0:T(8,128)(2,1)}, bf16[128,1792]{1,0:T(8,128)(2,1)S(1)}, u32[]{:S(2)}, u32[]{:S(2)}) %collective-permute-start.14) | collective-permute-done | bytes 458784 | tf_op jit(solution)/shard_map/ppermute | solution.py:397
  239.0 2.0 shard_map.72
  241.0 3.5 %all-to-all-start.15 = ((bf16[8,16,1792]{2,1,0:T(8,128)(2,1)}), bf16[8,16,1792]{2,1,0:T(8,128)(2,1)S(1)}, u32[]{:S(2)}, u32[]{:S(2)}) async-start(bf16[8,16,1792]{2,1,0:T(8,128)(2,1)} %shard_map.72), calls=%async_computation.15 | async-start | bytes 917504 | tf_op jit(solution)/shard_map/all_to_all | solution.py:533
  244.8 1.8 collective-permute-start.11
  246.6 0.8 collective-permute-start.12
  247.5 1.2 collective-permute-start.16
  248.6 3.1 %collective-permute-start.17 = (bf16[16,256]{1,0:T(8,128)(2,1)S(1)}, bf16[16,256]{1,0:T(8,128)(2,1)S(1)}, u32[]{:S(2)}, u32[]{:S(2)}) collective-permute-start(bf16[16,256]{1,0:T(8,128)(2,1)S(1)} %get-tuple-element.112), channel_id=1, source_target_pairs={{0,16},{8,24},{16,0},{24,8},{1,17},{9,25},{17,1},{25,9},{2,18},{10... | collective-permute-start | bytes 24584 | tf_op jit(solution)/shard_map/ppermute | solution.py:397
  251.8 7.1 %collective-permute-done.10.refs_0_ = bf16[1024,256]{1,0:T(8,128)(2,1)S(1)} collective-permute-done((bf16[1024,256]{1,0:T(8,128)(2,1)}, bf16[1024,256]{1,0:T(8,128)(2,1)S(1)}, u32[]{:S(2)}, u32[]{:S(2)}) %collective-permute-start.10) | collective-permute-done | bytes 524320 | tf_op jit(solution)/shard_map/ppermute | solution.py:397
  258.9 3.7 %collective-permute-start.18 = (bf16[16,256]{1,0:T(8,128)(2,1)S(1)}, bf16[16,256]{1,0:T(8,128)(2,1)S(1)}, u32[]{:S(2)}, u32[]{:S(2)}) collective-permute-start(bf16[16,256]{1,0:T(8,128)(2,1)S(1)} %get-tuple-element.113), channel_id=1, source_target_pairs={{0,24},{8,0},{16,8},{24,16},{1,25},{9,1},{17,9},{25,17},{2,26},{10... | collective-permute-start | bytes 24584 | tf_op jit(solution)/shard_map/ppermute | solution.py:397
  262.6 6.3 %collective-permute-done.11.refs_1_ = bf16[1024,256]{1,0:T(8,128)(2,1)S(1)} collective-permute-done((bf16[1024,256]{1,0:T(8,128)(2,1)}, bf16[1024,256]{1,0:T(8,128)(2,1)S(1)}, u32[]{:S(2)}, u32[]{:S(2)}) %collective-permute-start.11) | collective-permute-done | bytes 524320 | tf_op jit(solution)/shard_map/ppermute | solution.py:397
  268.9 1.6 collective-permute-done.12.refs_2_
  270.5 1.0 shard_map.71
  (51 shorter events, 9.2 us)
Async XLA Ops:
  0.6 26.1 %copy-start = (bf16[512,2048]{1,0:T(8,128)(2,1)S(1)}, bf16[512,2048]{1,0:T(8,128)(2,1)}, u32[]{:S(2)}) copy-start(bf16[512,2048]{1,0:T(8,128)(2,1)} %cent.5) | copy-start | bytes 6291460
  0.6 13.5 %collective-permute-start = (bf16[1024,256]{1,0:T(8,128)(2,1)}, bf16[1024,256]{1,0:T(8,128)(2,1)S(1)}, u32[]{:S(2)}, u32[]{:S(2)}) collective-permute-start(bf16[1024,256]{1,0:T(8,128)(2,1)} %refs_0_), channel_id=1, source_target_pairs={{0,2},{2,4},{4,6},{6,0},{1,3},{3,5},{5,7},{7,1},{8,10},{10,12},{12... | collective-permute-start | bytes 1572872 | tf_op jit(solution)/shard_map/ppermute | solution.py:397
  2.8 13.0 %collective-permute-start.2 = (bf16[1024,256]{1,0:T(8,128)(2,1)}, bf16[1024,256]{1,0:T(8,128)(2,1)S(1)}, u32[]{:S(2)}, u32[]{:S(2)}) collective-permute-start(bf16[1024,256]{1,0:T(8,128)(2,1)} %refs_0_), channel_id=1, source_target_pairs={{0,6},{2,0},{4,2},{6,4},{1,7},{3,1},{5,3},{7,5},{8,14},{10,8},{12,... | collective-permute-start | bytes 1572872 | tf_op jit(solution)/shard_map/ppermute | solution.py:397
  4.4 22.3 %collective-permute-start.4 = (bf16[1024,256]{1,0:T(8,128)(2,1)}, bf16[1024,256]{1,0:T(8,128)(2,1)S(1)}, u32[]{:S(2)}, u32[]{:S(2)}) collective-permute-start(bf16[1024,256]{1,0:T(8,128)(2,1)} %refs_0_), channel_id=1, source_target_pairs={{0,1},{1,0},{2,3},{3,2},{4,5},{5,4},{6,7},{7,6},{8,9},{9,8},{10,11... | collective-permute-start | bytes 1572872 | tf_op jit(solution)/shard_map/ppermute | solution.py:397
  14.2 6.9 %collective-permute-start.1 = (bf16[512,256]{1,0:T(8,128)(2,1)S(1)}, bf16[512,256]{1,0:T(8,128)(2,1)S(1)}, u32[]{:S(2)}, u32[]{:S(2)}) collective-permute-start(bf16[512,256]{1,0:T(8,128)(2,1)S(1)} %slice.8), channel_id=1, source_target_pairs={{0,2},{2,4},{4,6},{6,0},{1,3},{3,5},{5,7},{7,1},{8,10},{10,12},{12... | collective-permute-start | bytes 786440 | tf_op jit(solution)/shard_map/ppermute | solution.py:397
  15.8 9.2 %collective-permute-start.3 = (bf16[512,256]{1,0:T(8,128)(2,1)S(1)}, bf16[512,256]{1,0:T(8,128)(2,1)S(1)}, u32[]{:S(2)}, u32[]{:S(2)}) collective-permute-start(bf16[512,256]{1,0:T(8,128)(2,1)S(1)} %slice.9), channel_id=1, source_target_pairs={{0,6},{2,0},{4,2},{6,4},{1,7},{3,1},{5,3},{7,5},{8,14},{10,8},{12,... | collective-permute-start | bytes 786440 | tf_op jit(solution)/shard_map/ppermute | solution.py:397
  17.5 9.1 %collective-permute-start.5 = (bf16[1024,256]{1,0:T(8,128)(2,1)S(1)}, bf16[1024,256]{1,0:T(8,128)(2,1)S(1)}, u32[]{:S(2)}, u32[]{:S(2)}) collective-permute-start(bf16[1024,256]{1,0:T(8,128)(2,1)S(1)} %collective-permute-done.refs_1_), channel_id=1, source_target_pairs={{0,1},{1,0},{2,3},{3,2},{4,5},{5,4},{6,7},{7,6},{8,9},{9,8},{10,11... | collective-permute-start | bytes 1572872 | tf_op jit(solution)/shard_map/ppermute | solution.py:397
  20.8 5.9 %collective-permute-start.8 = (bf16[1024,256]{1,0:T(8,128)(2,1)S(1)}, bf16[1024,256]{1,0:T(8,128)(2,1)S(1)}, u32[]{:S(2)}, u32[]{:S(2)}) collective-permute-start(bf16[1024,256]{1,0:T(8,128)(2,1)S(1)} %collective-permute-done.2.refs_4_), channel_id=1, source_target_pairs={{0,1},{1,0},{2,3},{3,2},{4,5},{5,4},{6,7},{7,6},{8,9},{9,8},{10,11... | collective-permute-start | bytes 1572872 | tf_op jit(solution)/shard_map/ppermute | solution.py:397
  21.2 5.5 %collective-permute-start.6 = (bf16[512,256]{1,0:T(8,128)(2,1)S(1)}, bf16[512,256]{1,0:T(8,128)(2,1)S(1)}, u32[]{:S(2)}, u32[]{:S(2)}) collective-permute-start(bf16[512,256]{1,0:T(8,128)(2,1)S(1)} %collective-permute-done.1.refs_2_), channel_id=1, source_target_pairs={{0,1},{1,0},{2,3},{3,2},{4,5},{5,4},{6,7},{7,6},{8,9},{9,8},{10,11... | collective-permute-start | bytes 786440 | tf_op jit(solution)/shard_map/ppermute | solution.py:397
  25.0 1.6 collective-permute-start.7
  25.1 1.2 copy-start.4
  26.3 1.0 copy-start.6
  192.4 9.9 %all-to-all-start.14 = ((f32[8,8,128]{2,1,0:T(8,128)}), f32[8,8,128]{2,1,0:T(8,128)S(1)}, u32[]{:S(2)}, u32[]{:S(2)}) async-start(f32[8,8,128]{2,1,0:T(8,128)} %get-tuple-element.93), calls=%async_computation.14 | async-start | bytes 65536 | tf_op jit(solution)/shard_map/all_to_all | solution.py:421
  202.3 1.6 copy-start.1
  206.3 15.5 %collective-permute-start.9 = (bf16[4,1024,256]{2,1,0:T(8,128)(2,1)}, bf16[4,1024,256]{2,1,0:T(8,128)(2,1)}, u32[]{:S(2)}, u32[]{:S(2)}) collective-permute-start(bf16[4,1024,256]{2,1,0:T(8,128)(2,1)} %get-tuple-element.99), channel_id=1, source_target_pairs={{0,1},{1,0},{2,3},{3,2},{4,5},{5,4},{6,7},{7,6},{8,9},{9,8},{10,11... | collective-permute-start | bytes 6291464 | tf_op jit(solution)/shard_map/ppermute | solution.py:397
  207.1 14.7 %copy-start.2 = (bf16[512,2048]{1,0:T(8,128)(2,1)S(1)}, bf16[512,2048]{1,0:T(8,128)(2,1)}, u32[]{:S(2)}) copy-start(bf16[512,2048]{1,0:T(8,128)(2,1)} %cent.5) | copy-start | bytes 6291460
  214.9 14.1 %collective-permute-start.13 = (bf16[128,1792]{1,0:T(8,128)(2,1)}, bf16[128,1792]{1,0:T(8,128)(2,1)S(1)}, u32[]{:S(2)}, u32[]{:S(2)}) collective-permute-start(bf16[128,1792]{1,0:T(8,128)(2,1)} %get-tuple-element.106), channel_id=1, source_target_pairs={{0,8},{8,16},{16,24},{24,0},{1,9},{9,17},{17,25},{25,1},{2,10},{10... | collective-permute-start | bytes 1376264 | tf_op jit(solution)/shard_map/ppermute | solution.py:397
  215.5 22.8 %collective-permute-start.14 = (bf16[128,1792]{1,0:T(8,128)(2,1)}, bf16[128,1792]{1,0:T(8,128)(2,1)S(1)}, u32[]{:S(2)}, u32[]{:S(2)}) collective-permute-start(bf16[128,1792]{1,0:T(8,128)(2,1)} %get-tuple-element.107), channel_id=1, source_target_pairs={{0,16},{8,24},{16,0},{24,8},{1,17},{9,25},{17,1},{25,9},{2,18},{10... | collective-permute-start | bytes 1376264 | tf_op jit(solution)/shard_map/ppermute | solution.py:397
  217.6 21.4 %collective-permute-start.15 = (bf16[128,1792]{1,0:T(8,128)(2,1)}, bf16[128,1792]{1,0:T(8,128)(2,1)}, u32[]{:S(2)}, u32[]{:S(2)}) collective-permute-start(bf16[128,1792]{1,0:T(8,128)(2,1)} %get-tuple-element.108), channel_id=1, source_target_pairs={{0,24},{8,0},{16,8},{24,16},{1,25},{9,1},{17,9},{25,17},{2,26},{10... | collective-permute-start | bytes 1376264 | tf_op jit(solution)/shard_map/ppermute | solution.py:397
  218.3 22.6 %all-to-all-start.16 = ((bf16[8,64,256]{2,1,0:T(8,128)(2,1)}), bf16[8,64,256]{2,1,0:T(8,128)(2,1)S(1)}, u32[]{:S(2)}, u32[]{:S(2)}) async-start(bf16[8,64,256]{2,1,0:T(8,128)(2,1)} %get-tuple-element.109), calls=%async_computation.16 | async-start | bytes 524288 | tf_op jit(solution)/shard_map/all_to_all | solution.py:514
  221.8 17.2 %copy-start.5 = (f32[128,1792]{1,0:T(8,128)S(1)}, f32[128,1792]{1,0:T(8,128)}, u32[]{:S(2)}) copy-start(f32[128,1792]{1,0:T(8,128)} %get-tuple-element.105.first) | copy-start | bytes 2752516
  227.6 43.0 %copy-start.3 = (f32[1024,256]{1,0:T(8,128)S(1)}, f32[1024,256]{1,0:T(8,128)}, u32[]{:S(2)}) copy-start(f32[1024,256]{1,0:T(8,128)} %get-tuple-element.101.first) | copy-start | bytes 3145732
  241.0 30.6 %all-to-all-start.15 = ((bf16[8,16,1792]{2,1,0:T(8,128)(2,1)}), bf16[8,16,1792]{2,1,0:T(8,128)(2,1)S(1)}, u32[]{:S(2)}, u32[]{:S(2)}) async-start(bf16[8,16,1792]{2,1,0:T(8,128)(2,1)} %shard_map.72), calls=%async_computation.15 | async-start | bytes 917504 | tf_op jit(solution)/shard_map/all_to_all | solution.py:533
  244.5 14.4 %collective-permute-start.10 = (bf16[1024,256]{1,0:T(8,128)(2,1)}, bf16[1024,256]{1,0:T(8,128)(2,1)S(1)}, u32[]{:S(2)}, u32[]{:S(2)}) collective-permute-start(bf16[1024,256]{1,0:T(8,128)(2,1)} %get-tuple-element.102), channel_id=1, source_target_pairs={{0,2},{2,4},{4,6},{6,0},{1,3},{3,5},{5,7},{7,1},{8,10},{10,12},{12... | collective-permute-start | bytes 1572872 | tf_op jit(solution)/shard_map/ppermute | solution.py:397
  244.8 24.1 %collective-permute-start.11 = (bf16[1024,256]{1,0:T(8,128)(2,1)}, bf16[1024,256]{1,0:T(8,128)(2,1)S(1)}, u32[]{:S(2)}, u32[]{:S(2)}) collective-permute-start(bf16[1024,256]{1,0:T(8,128)(2,1)} %get-tuple-element.103), channel_id=1, source_target_pairs={{0,4},{2,6},{4,0},{6,2},{1,5},{3,7},{5,1},{7,3},{8,12},{10,14},{12... | collective-permute-start | bytes 1572872 | tf_op jit(solution)/shard_map/ppermute | solution.py:397
  246.6 23.9 %collective-permute-start.12 = (bf16[1024,256]{1,0:T(8,128)(2,1)}, bf16[1024,256]{1,0:T(8,128)(2,1)S(1)}, u32[]{:S(2)}, u32[]{:S(2)}) collective-permute-start(bf16[1024,256]{1,0:T(8,128)(2,1)} %get-tuple-element.104), channel_id=1, source_target_pairs={{0,6},{2,0},{4,2},{6,4},{1,7},{3,1},{5,3},{7,5},{8,14},{10,8},{12,... | collective-permute-start | bytes 1572872 | tf_op jit(solution)/shard_map/ppermute | solution.py:397
  247.5 24.1 %collective-permute-start.16 = (bf16[16,256]{1,0:T(8,128)(2,1)S(1)}, bf16[16,256]{1,0:T(8,128)(2,1)S(1)}, u32[]{:S(2)}, u32[]{:S(2)}) collective-permute-start(bf16[16,256]{1,0:T(8,128)(2,1)S(1)} %get-tuple-element.111), channel_id=1, source_target_pairs={{0,8},{8,16},{16,24},{24,0},{1,9},{9,17},{17,25},{25,1},{2,10},{10... | collective-permute-start | bytes 24584 | tf_op jit(solution)/shard_map/ppermute | solution.py:397
  248.6 22.9 %collective-permute-start.17 = (bf16[16,256]{1,0:T(8,128)(2,1)S(1)}, bf16[16,256]{1,0:T(8,128)(2,1)S(1)}, u32[]{:S(2)}, u32[]{:S(2)}) collective-permute-start(bf16[16,256]{1,0:T(8,128)(2,1)S(1)} %get-tuple-element.112), channel_id=1, source_target_pairs={{0,16},{8,24},{16,0},{24,8},{1,17},{9,25},{17,1},{25,9},{2,18},{10... | collective-permute-start | bytes 24584 | tf_op jit(solution)/shard_map/ppermute | solution.py:397
  258.9 12.7 %collective-permute-start.18 = (bf16[16,256]{1,0:T(8,128)(2,1)S(1)}, bf16[16,256]{1,0:T(8,128)(2,1)S(1)}, u32[]{:S(2)}, u32[]{:S(2)}) collective-permute-start(bf16[16,256]{1,0:T(8,128)(2,1)S(1)} %get-tuple-element.113), channel_id=1, source_target_pairs={{0,24},{8,0},{16,8},{24,16},{1,25},{9,1},{17,9},{25,17},{2,26},{10... | collective-permute-start | bytes 24584 | tf_op jit(solution)/shard_map/ppermute | solution.py:397

commit v6 on v5

--- a/solution.py
+++ b/solution.py
@@ -104,15 +104,20 @@
 
 def k_logits(scale, counts, cent, *refs):
     n = len(counts)
-    pieces, (logits, send, whole, held, sem) = grouped(refs, counts), refs[sum(counts) :]
+    pieces, (logits, send, whole, held, sems) = grouped(refs, counts), refs[sum(counts) :]
+    copies = []
     for k, blocks in enumerate(pieces):
         at = 0
         for block in blocks:
-            rows = slice(at, at + block.shape[0])
-            held[rows, span(source(n // 2, k), block.shape[1])] = block[...]
-            at += block.shape[0]
-    copy = pltpu.make_async_copy(held, whole, sem)
-    copy.start()
+            size = block.shape[0]
+            copies.append(
+                pltpu.make_async_copy(
+                    block, whole.at[k, pl.ds(at, size), :], sems.at[len(copies)]
+                )
+            )
+            copies[-1].start()
+            held[at : at + size, span(source(n // 2, k), block.shape[1])] = block[...]
+            at += size
     logits[...] = scale * lax.dot_general(cent[...], held[...], NT, preferred_element_type=F32)
     count = logits.shape[1] // L
     tops, sums = [], []
@@ -123,7 +128,8 @@
         sums.append(jnp.sum(jnp.exp(tile - top), axis=0, keepdims=True))
     send[:, 0] = jnp.broadcast_to(jnp.concatenate(tops, axis=0)[None], send[:, 0].shape)
     send[:, 1] = jnp.broadcast_to(jnp.concatenate(sums, axis=0)[None], send[:, 1].shape)
-    copy.wait()
+    for c in copies:
+        c.wait()
 
 
 def k_first_col(logits, recv, row_pot, send):
@@ -258,10 +264,7 @@
     sends, (whole, picked, wide, own, narrow, sems, in_sems) = refs[: nx - 1], refs[nx - 1 :]
     width = whole.shape[2]
     copies = [
-        pltpu.make_async_copy(
-            whole_hbm.at[:, span(source(n // 2, p), width)], whole.at[p], in_sems.at[p]
-        )
-        for p in range(n)
+        pltpu.make_async_copy(whole_hbm.at[p], whole.at[p], in_sems.at[p]) for p in range(n)
     ]
     for p in (*by_x(n), *by_z()):
         copies[p].start()
@@ -311,33 +314,35 @@
         c.wait()
 
 
-def k_pair(scale, turned_hbm, cent, cross_hbm, first, *refs):
-    rest, (turned, cross, own, stage, sems, out_sems) = refs[:-6], refs[-6:]
-    ny, _, width = cross.shape
-    bring = pltpu.make_async_copy(turned_hbm, turned, sems.at[ny])
+def k_pair(scale, turned_hbm, cent, cross_hbm, *refs):
+    ny = cross_hbm.shape[0]
+    sends, (turned, cross, stage, sems, out_sems) = refs[: ny - 1], refs[ny - 1 :]
+    width = cross.shape[2]
+    bring = pltpu.make_async_copy(turned_hbm, turned, sems.at[0])
     bring.start()
     copies = [
-        pltpu.make_async_copy(cross_hbm.at[k], cross.at[k], sems.at[k]) for k in range(ny)
+        pltpu.make_async_copy(cross_hbm.at[k], cross.at[k - 1], sems.at[k]) for k in range(1, ny)
     ]
-    for k in range(ny - 1, -1, -1):
-        copies[k].start()
+    for c in copies:
+        c.start()
     bring.wait()
     outs = []
-    for k in range(ny - 1, -1, -1):
+    for k in range(1, ny):
         block = cent[:, span(target(ny, k, False), width)]
         part = scale * lax.dot_general(turned[...], block, NN, preferred_element_type=F32)
-        copies[k].wait()
-        part = part + cross[k].astype(F32)
-        if k:
-            stage[k - 1] = part.astype(BF16)
-            src, dst = stage.at[k - 1], rest[k - 1]
-        else:
-            own[...] = part
-            src, dst = own, first
-        outs.append(pltpu.make_async_copy(src, dst, out_sems.at[k]))
+        copies[k - 1].wait()
+        stage[k - 1] = (part + cross[k - 1].astype(F32)).astype(BF16)
+        outs.append(pltpu.make_async_copy(stage.at[k - 1], sends[k - 1], out_sems.at[k - 1]))
         outs[-1].start()
     for c in outs:
         c.wait()
+
+
+def k_own(scale, turned, cent, cross, out):
+    ny, width = cross.shape[0], cross.shape[2]
+    block = cent[:, span(target(ny, 0, False), width)]
+    part = scale * lax.dot_general(turned[...], block, NN, preferred_element_type=F32)
+    out[...] = part + cross[0].astype(F32)
 
 
 def k_early(recv, keep, *refs):
@@ -431,10 +436,10 @@
     work = 2 * rows * cols * depth
     logits, send, whole = call(
         functools.partial(k_logits, scale, counts),
-        [block, row_pair, ((rows, depth), BF16)],
+        [block, row_pair, ((len(counts), rows, width), BF16)],
         centroids, *pieces,
         limit=LARGE, flops=work, hbm_out=(2,),
-        scratch=[pltpu.VMEM((rows, depth), BF16), pltpu.SemaphoreType.DMA],
+        scratch=[pltpu.VMEM((rows, depth), BF16), pltpu.SemaphoreType.DMA((len(pieces),))],
     )
     row_pot, send = call(k_first_col, [a_row, col_pair], logits, over_clus(send))
     col_pot, weights, send = call(
@@ -512,23 +517,28 @@
     )
     cross = shift(cross, "core", 1)
     straight = lax.all_to_all(straight, "z", 0, 0, tiled=True)
-    own, *moved = call(
+    moved = call(
         functools.partial(k_pair, scale),
-        [((rows, width), F32)] + [((rows, width), BF16)] * (ny - 1),
+        [((rows, width), BF16)] * (ny - 1),
         pltpu.with_memory_space_constraint(turned, pltpu.HBM), centroids,
         pltpu.with_memory_space_constraint(cross, pltpu.HBM),
-        limit=LARGE, flops=work // 2, hbm_in=(0, 2), hbm_out=range(ny),
+        limit=LARGE, flops=work // 2, hbm_in=(0, 2), hbm_out=range(ny - 1),
         scratch=[
             pltpu.VMEM((rows, cols), BF16),
-            pltpu.VMEM((ny, rows, width), BF16),
-            pltpu.VMEM((rows, width), F32),
             pltpu.VMEM((ny - 1, rows, width), BF16),
-            pltpu.SemaphoreType.DMA((ny + 1,)),
+            pltpu.VMEM((ny - 1, rows, width), BF16),
             pltpu.SemaphoreType.DMA((ny,)),
+            pltpu.SemaphoreType.DMA((ny - 1,)),
         ],
     )
-    near, own = lax.optimization_barrier((near, own))
+    near, *moved = lax.optimization_barrier((near, *moved))
     moved = [shift(m, "y", k + 1) for k, m in enumerate(moved)]
+    (own,) = call(
+        functools.partial(k_own, scale),
+        [((rows, width), F32)],
+        turned, centroids, cross,
+        limit=LARGE, flops=work // 8,
+    )
     (parts,) = call(k_add, [((nz, per // nz, wide), BF16)], near, *parts, limit=LARGE)
     parts = lax.all_to_all(parts, "z", 0, 0, tiled=True)
     final = per // nz

time: 277 us -> 280 us (1.011)
    pallas_call x25 -> x26, Pallas kernels: 31 us -> 32.8 us  [call(): pl.pallas_call(body, out_shape=[pltpu.HBM(s, d) if i in hbm_out else jax....]
where the time goes in v6:
time: 280 us; the launch traced here: 275 us
  blocking collectives  157 us (56%)
  starting transfers between devices  45 us (16%)
  waiting for transfers between devices  35.6 us (13%)
  Pallas kernels  32.8 us (12%)
  local copies, waits for them, and re-layouts  3.83 us (1%)
    all_to_all x7, blocking collectives, over_prog(): return lax.all_to_all(send, ('z', 'x'), 0, 0, tiled=True)  92.4 us
    all_to_all x7, blocking collectives, over_clus(): return lax.all_to_all(send, ('y', 'core'), 0, 0, tiled=True)  64.2 us
    ppermute x19, waiting for transfers between devices, shift(): return lax.ppermute(value, axis, [(i, (i + step) % n) for i in range(n)])  33 us
    pallas_call x26, Pallas kernels, call(): pl.pallas_call(body, out_shape=[pltpu.HBM(s, d) if i in hbm_out else jax....  32.8 us
    ppermute x19, starting transfers between devices, shift(): return lax.ppermute(value, axis, [(i, (i + step) % n) for i in range(n)])  32.3 us
  transfers between devices with their start and end apart: 22, of which 9 were waited for; matrix products, arithmetic and copies ran while one was open for 0% of the time, Pallas kernels for 7%

profile of v6, /device:TPU:1, one launch (start us, length us, event | category | flops | bytes accessed | tf_op | source)
XLA Modules:
  0.0 274.8 jit_solution(13812480842826817965)
XLA Ops:
  0.6 2.2 collective-permute-start
  2.8 1.5 collective-permute-start.2
  4.4 2.8 %collective-permute-start.4 = (bf16[1024,256]{1,0:T(8,128)(2,1)}, bf16[1024,256]{1,0:T(8,128)(2,1)S(1)}, u32[]{:S(2)}, u32[]{:S(2)}) collective-permute-start(bf16[1024,256]{1,0:T(8,128)(2,1)} %refs_0_), channel_id=1, source_target_pairs={{0,1},{1,0},{2,3},{3,2},{4,5},{5,4},{6,7},{7,6},{8,9},{9,8},{10,11... | collective-permute-start | bytes 1572872 | tf_op jit(solution)/shard_map/ppermute | solution.py:402
  7.2 7.0 %collective-permute-done.refs_1_ = bf16[1024,256]{1,0:T(8,128)(2,1)S(1)} collective-permute-done((bf16[1024,256]{1,0:T(8,128)(2,1)}, bf16[1024,256]{1,0:T(8,128)(2,1)S(1)}, u32[]{:S(2)}, u32[]{:S(2)}) %collective-permute-start) | collective-permute-done | bytes 524320 | tf_op jit(solution)/shard_map/ppermute | solution.py:402
  14.2 1.6 collective-permute-start.1
  15.8 1.7 collective-permute-start.3
  17.5 3.3 %collective-permute-start.5 = (bf16[1024,256]{1,0:T(8,128)(2,1)S(1)}, bf16[1024,256]{1,0:T(8,128)(2,1)S(1)}, u32[]{:S(2)}, u32[]{:S(2)}) collective-permute-start(bf16[1024,256]{1,0:T(8,128)(2,1)S(1)} %collective-permute-done.refs_1_), channel_id=1, source_target_pairs={{0,1},{1,0},{2,3},{3,2},{4,5},{5,4},{6,7},{7,6},{8,9},{9,8},{10,11... | collective-permute-start | bytes 1572872 | tf_op jit(solution)/shard_map/ppermute | solution.py:402
  21.2 3.9 %collective-permute-start.6 = (bf16[512,256]{1,0:T(8,128)(2,1)S(1)}, bf16[512,256]{1,0:T(8,128)(2,1)S(1)}, u32[]{:S(2)}, u32[]{:S(2)}) collective-permute-start(bf16[512,256]{1,0:T(8,128)(2,1)S(1)} %collective-permute-done.1.refs_2_), channel_id=1, source_target_pairs={{0,1},{1,0},{2,3},{3,2},{4,5},{5,4},{6,7},{7,6},{8,9},{9,8},{10,11... | collective-permute-start | bytes 786440 | tf_op jit(solution)/shard_map/ppermute | solution.py:402
  25.1 1.2 copy-done.5
  27.3 3.8 %shard_map.51 = (f32[512,1024]{1,0:T(8,128)S(1)}, f32[8,2,8,128]{3,2,1,0:T(8,128)S(1)}, bf16[8,1024,256]{2,1,0:T(8,128)(2,1)}) custom-call(bf16[512,2048]{1,0:T(8,128)(2,1)S(1)} %copy-done, bf16[1024,256]{1,0:T(8,128)(2,1)S(1)} %copy-done.7, bf16[1024,256]{1,0:T(8,128)(2,1)S(1)} %collective-permute-done.refs_1_, ...), custom_call_target="tpu_custom_call" | custom-call | flops 2147483648 | bytes 6291456 | tf_op jit(solution)/shard_map/pallas_call | solution.py:385
  31.1 9.4 %all_to_all.85.recv = f32[8,2,8,128]{3,2,1,0:T(8,128)S(1)} all-to-all(f32[8,2,8,128]{3,2,1,0:T(8,128)S(1)} %get-tuple-element.61), channel_id=1, replica_groups=mesh['z'=8,'x'=4,'y'=4,'core'=2] {'y','core'}, dimensions={0} | all-to-all | bytes 131072 | tf_op jit(solution)/shard_map/all_to_all | solution.py:426
  41.1 20.8 %all_to_all.86.recv = f32[32,2,4,128]{3,2,1,0:T(4,128)S(1)} all-to-all(f32[32,2,4,128]{3,2,1,0:T(4,128)S(1)} %get-tuple-element.63), channel_id=1, replica_groups=mesh['z'=8,'x'=4,'y'=4,'core'=2] {'z','x'}, dimensions={0} | all-to-all | bytes 262144 | tf_op jit(solution)/shard_map/all_to_all | solution.py:429
  62.4 9.3 %all_to_all.87.recv = f32[8,8,128]{2,1,0:T(8,128)S(1)} all-to-all(f32[8,8,128]{2,1,0:T(8,128)S(1)} %get-tuple-element.67), channel_id=1, replica_groups=mesh['z'=8,'x'=4,'y'=4,'core'=2] {'y','core'}, dimensions={0} | all-to-all | bytes 65536 | tf_op jit(solution)/shard_map/all_to_all | solution.py:426
  71.9 11.8 %all_to_all.88.recv = f32[32,4,128]{2,1,0:T(4,128)S(1)} all-to-all(f32[32,4,128]{2,1,0:T(4,128)S(1)} %get-tuple-element.69), channel_id=1, replica_groups=mesh['z'=8,'x'=4,'y'=4,'core'=2] {'z','x'}, dimensions={0} | all-to-all | bytes 131072 | tf_op jit(solution)/shard_map/all_to_all | solution.py:429
  84.0 9.2 %all_to_all.89.recv = f32[8,8,128]{2,1,0:T(8,128)S(1)} all-to-all(f32[8,8,128]{2,1,0:T(8,128)S(1)} %get-tuple-element.70), channel_id=1, replica_groups=mesh['z'=8,'x'=4,'y'=4,'core'=2] {'y','core'}, dimensions={0} | all-to-all | bytes 65536 | tf_op jit(solution)/shard_map/all_to_all | solution.py:426
  93.4 11.8 %all_to_all.90.recv = f32[32,4,128]{2,1,0:T(4,128)S(1)} all-to-all(f32[32,4,128]{2,1,0:T(4,128)S(1)} %get-tuple-element.72), channel_id=1, replica_groups=mesh['z'=8,'x'=4,'y'=4,'core'=2] {'z','x'}, dimensions={0} | all-to-all | bytes 131072 | tf_op jit(solution)/shard_map/all_to_all | solution.py:429
  105.5 9.1 %all_to_all.91.recv = f32[8,8,128]{2,1,0:T(8,128)S(1)} all-to-all(f32[8,8,128]{2,1,0:T(8,128)S(1)} %get-tuple-element.73), channel_id=1, replica_groups=mesh['z'=8,'x'=4,'y'=4,'core'=2] {'y','core'}, dimensions={0} | all-to-all | bytes 65536 | tf_op jit(solution)/shard_map/all_to_all | solution.py:426
  115.1 12.4 %all_to_all.92.recv = f32[32,2,4,128]{3,2,1,0:T(4,128)S(1)} all-to-all(f32[32,2,4,128]{3,2,1,0:T(4,128)S(1)} %get-tuple-element.77), channel_id=1, replica_groups=mesh['z'=8,'x'=4,'y'=4,'core'=2] {'z','x'}, dimensions={0} | all-to-all | bytes 262144 | tf_op jit(solution)/shard_map/all_to_all | solution.py:429
  127.9 9.2 %all_to_all.93.recv = f32[8,8,128]{2,1,0:T(8,128)S(1)} all-to-all(f32[8,8,128]{2,1,0:T(8,128)S(1)} %get-tuple-element.79), channel_id=1, replica_groups=mesh['z'=8,'x'=4,'y'=4,'core'=2] {'y','core'}, dimensions={0} | all-to-all | bytes 65536 | tf_op jit(solution)/shard_map/all_to_all | solution.py:426
  137.4 11.9 %all_to_all.94.refs_1_ = f32[32,4,128]{2,1,0:T(4,128)S(1)} all-to-all(f32[32,4,128]{2,1,0:T(4,128)S(1)} %get-tuple-element.80), channel_id=1, replica_groups=mesh['z'=8,'x'=4,'y'=4,'core'=2] {'z','x'}, dimensions={0} | all-to-all | bytes 131072 | tf_op jit(solution)/shard_map/all_to_all | solution.py:429
  149.6 9.0 %all_to_all.95.recv = f32[8,8,128]{2,1,0:T(8,128)S(1)} all-to-all(f32[8,8,128]{2,1,0:T(8,128)S(1)} %get-tuple-element.81), channel_id=1, replica_groups=mesh['z'=8,'x'=4,'y'=4,'core'=2] {'y','core'}, dimensions={0} | all-to-all | bytes 65536 | tf_op jit(solution)/shard_map/all_to_all | solution.py:426
  158.8 11.8 %all_to_all.96.refs_1_ = f32[32,4,128]{2,1,0:T(4,128)S(1)} all-to-all(f32[32,4,128]{2,1,0:T(4,128)S(1)} %get-tuple-element.82), channel_id=1, replica_groups=mesh['z'=8,'x'=4,'y'=4,'core'=2] {'z','x'}, dimensions={0} | all-to-all | bytes 131072 | tf_op jit(solution)/shard_map/all_to_all | solution.py:429
  170.9 9.1 %all_to_all.97.recv = f32[8,8,128]{2,1,0:T(8,128)S(1)} all-to-all(f32[8,8,128]{2,1,0:T(8,128)S(1)} %get-tuple-element.83), channel_id=1, replica_groups=mesh['z'=8,'x'=4,'y'=4,'core'=2] {'y','core'}, dimensions={0} | all-to-all | bytes 65536 | tf_op jit(solution)/shard_map/all_to_all | solution.py:426
  180.2 11.8 %all_to_all.98.refs_0_ = f32[32,4,128]{2,1,0:T(4,128)S(1)} all-to-all(f32[32,4,128]{2,1,0:T(4,128)S(1)} %get-tuple-element.84), channel_id=1, replica_groups=mesh['z'=8,'x'=4,'y'=4,'core'=2] {'z','x'}, dimensions={0} | all-to-all | bytes 131072 | tf_op jit(solution)/shard_map/all_to_all | solution.py:429
  192.0 0.9 shard_map.65
  192.9 5.2 %all-to-all-start.14 = ((f32[8,8,128]{2,1,0:T(8,128)}), f32[8,8,128]{2,1,0:T(8,128)S(1)}, u32[]{:S(2)}, u32[]{:S(2)}) async-start(f32[8,8,128]{2,1,0:T(8,128)} %get-tuple-element.94), calls=%async_computation.14 | async-start | bytes 65536 | tf_op jit(solution)/shard_map/all_to_all | solution.py:426
  198.1 2.2 shard_map.66
  200.3 2.5 all-to-all-done.14.recv
  203.3 1.1 copy-done.1
  204.4 2.4 shard_map.68
  207.6 7.8 %shard_map.70 = (bf16[8,64,256]{2,1,0:T(8,128)(2,1)}, f32[128,1792]{1,0:T(8,128)}, bf16[128,1792]{1,0:T(8,128)(2,1)}, bf16[128,1792]{1,0:T(8,128)(2,1)}, bf16[128,1792]{1,0:T(8,128)(2,1)}) custom-call(bf16[512,1024]{1,0:T(8,128)(2,1)S(1)} %get-tuple-element.98.adjoint, bf16[8,1024,256]{2,1,0:T(8,128)(2,1)} %get-tuple-element.99.whole_hbm), custom_call_target="tpu_custom_call" | custom-call | flops 2147483648 | bytes 5242880 | tf_op jit(solution)/shard_map/pallas_call | solution.py:385
  216.0 2.1 collective-permute-start.14
  218.9 3.4 %all-to-all-start.16 = ((bf16[8,64,256]{2,1,0:T(8,128)(2,1)}), bf16[8,64,256]{2,1,0:T(8,128)(2,1)S(1)}, u32[]{:S(2)}, u32[]{:S(2)}) async-start(bf16[8,64,256]{2,1,0:T(8,128)(2,1)} %get-tuple-element.111), calls=%async_computation.16 | async-start | bytes 524288 | tf_op jit(solution)/shard_map/all_to_all | solution.py:519
  222.3 4.5 %shard_map.71 = (bf16[1024,256]{1,0:T(8,128)(2,1)}, bf16[1024,256]{1,0:T(8,128)(2,1)}, bf16[1024,256]{1,0:T(8,128)(2,1)}) custom-call(bf16[1024,512]{1,0:T(8,128)(2,1)} %get-tuple-element.96.turned.turned_hbm, bf16[512,2048]{1,0:T(8,128)(2,1)S(1)} %copy-done.2, bf16[4,1024,256]{2,1,0:T(8,128)(2,1)} %collective-permute-done.9.cross.cross_hbm), custom_call_target="tpu_custom_call" | custom-call | flops 1073741824 | bytes 5242880 | tf_op jit(solution)/shard_map/pallas_call | solution.py:385
  226.8 2.8 %collective-permute-done.13.refs_0_ = bf16[128,1792]{1,0:T(8,128)(2,1)} collective-permute-done((bf16[128,1792]{1,0:T(8,128)(2,1)}, bf16[128,1792]{1,0:T(8,128)(2,1)}, u32[]{:S(2)}, u32[]{:S(2)}) %collective-permute-start.13) | collective-permute-done | bytes 458784 | tf_op jit(solution)/shard_map/ppermute | solution.py:402
  229.7 9.2 %collective-permute-done.14.refs_1_ = bf16[128,1792]{1,0:T(8,128)(2,1)} collective-permute-done((bf16[128,1792]{1,0:T(8,128)(2,1)}, bf16[128,1792]{1,0:T(8,128)(2,1)}, u32[]{:S(2)}, u32[]{:S(2)}) %collective-permute-start.14) | collective-permute-done | bytes 458784 | tf_op jit(solution)/shard_map/ppermute | solution.py:402
  239.5 1.5 shard_map.73
  241.8 4.1 %all-to-all-start.15 = ((bf16[8,16,1792]{2,1,0:T(8,128)(2,1)}), bf16[8,16,1792]{2,1,0:T(8,128)(2,1)}, u32[]{:S(2)}, u32[]{:S(2)}) async-start(bf16[8,16,1792]{2,1,0:T(8,128)(2,1)} %copy-done.4), calls=%async_computation.15 | async-start | bytes 917504 | tf_op jit(solution)/shard_map/all_to_all | solution.py:543
  246.3 1.8 collective-permute-start.11
  249.0 1.1 collective-permute-start.16
  250.1 3.1 %collective-permute-start.17 = (bf16[16,256]{1,0:T(8,128)(2,1)S(1)}, bf16[16,256]{1,0:T(8,128)(2,1)S(1)}, u32[]{:S(2)}, u32[]{:S(2)}) collective-permute-start(bf16[16,256]{1,0:T(8,128)(2,1)S(1)} %get-tuple-element.114), channel_id=1, source_target_pairs={{0,16},{8,24},{16,0},{24,8},{1,17},{9,25},{17,1},{25,9},{2,18},{10... | collective-permute-start | bytes 24584 | tf_op jit(solution)/shard_map/ppermute | solution.py:402
  253.2 7.1 %collective-permute-done.10.refs_0_ = bf16[1024,256]{1,0:T(8,128)(2,1)S(1)} collective-permute-done((bf16[1024,256]{1,0:T(8,128)(2,1)}, bf16[1024,256]{1,0:T(8,128)(2,1)S(1)}, u32[]{:S(2)}, u32[]{:S(2)}) %collective-permute-start.10) | collective-permute-done | bytes 524320 | tf_op jit(solution)/shard_map/ppermute | solution.py:402
  260.4 3.8 %collective-permute-start.18 = (bf16[16,256]{1,0:T(8,128)(2,1)S(1)}, bf16[16,256]{1,0:T(8,128)(2,1)S(1)}, u32[]{:S(2)}, u32[]{:S(2)}) collective-permute-start(bf16[16,256]{1,0:T(8,128)(2,1)S(1)} %get-tuple-element.115), channel_id=1, source_target_pairs={{0,24},{8,0},{16,8},{24,16},{1,25},{9,1},{17,9},{25,17},{2,26},{10... | collective-permute-start | bytes 24584 | tf_op jit(solution)/shard_map/ppermute | solution.py:402
  264.2 2.0 shard_map.69.first
  266.2 4.2 %collective-permute-done.11.refs_1_ = bf16[1024,256]{1,0:T(8,128)(2,1)S(1)} collective-permute-done((bf16[1024,256]{1,0:T(8,128)(2,1)}, bf16[1024,256]{1,0:T(8,128)(2,1)S(1)}, u32[]{:S(2)}, u32[]{:S(2)}) %collective-permute-start.11) | collective-permute-done | bytes 524320 | tf_op jit(solution)/shard_map/ppermute | solution.py:402
  270.4 1.6 collective-permute-done.12.refs_2_
  272.0 1.0 shard_map.72
  273.1 1.7 shard_map.75
  (54 shorter events, 10.9 us)
Async XLA Ops:
  0.6 26.1 %copy-start = (bf16[512,2048]{1,0:T(8,128)(2,1)S(1)}, bf16[512,2048]{1,0:T(8,128)(2,1)}, u32[]{:S(2)}) copy-start(bf16[512,2048]{1,0:T(8,128)(2,1)} %cent.7) | copy-start | bytes 6291460
  0.6 13.5 %collective-permute-start = (bf16[1024,256]{1,0:T(8,128)(2,1)}, bf16[1024,256]{1,0:T(8,128)(2,1)S(1)}, u32[]{:S(2)}, u32[]{:S(2)}) collective-permute-start(bf16[1024,256]{1,0:T(8,128)(2,1)} %refs_0_), channel_id=1, source_target_pairs={{0,2},{2,4},{4,6},{6,0},{1,3},{3,5},{5,7},{7,1},{8,10},{10,12},{12... | collective-permute-start | bytes 1572872 | tf_op jit(solution)/shard_map/ppermute | solution.py:402
  2.8 13.0 %collective-permute-start.2 = (bf16[1024,256]{1,0:T(8,128)(2,1)}, bf16[1024,256]{1,0:T(8,128)(2,1)S(1)}, u32[]{:S(2)}, u32[]{:S(2)}) collective-permute-start(bf16[1024,256]{1,0:T(8,128)(2,1)} %refs_0_), channel_id=1, source_target_pairs={{0,6},{2,0},{4,2},{6,4},{1,7},{3,1},{5,3},{7,5},{8,14},{10,8},{12,... | collective-permute-start | bytes 1572872 | tf_op jit(solution)/shard_map/ppermute | solution.py:402
  4.4 22.3 %collective-permute-start.4 = (bf16[1024,256]{1,0:T(8,128)(2,1)}, bf16[1024,256]{1,0:T(8,128)(2,1)S(1)}, u32[]{:S(2)}, u32[]{:S(2)}) collective-permute-start(bf16[1024,256]{1,0:T(8,128)(2,1)} %refs_0_), channel_id=1, source_target_pairs={{0,1},{1,0},{2,3},{3,2},{4,5},{5,4},{6,7},{7,6},{8,9},{9,8},{10,11... | collective-permute-start | bytes 1572872 | tf_op jit(solution)/shard_map/ppermute | solution.py:402
  14.2 6.9 %collective-permute-start.1 = (bf16[512,256]{1,0:T(8,128)(2,1)S(1)}, bf16[512,256]{1,0:T(8,128)(2,1)S(1)}, u32[]{:S(2)}, u32[]{:S(2)}) collective-permute-start(bf16[512,256]{1,0:T(8,128)(2,1)S(1)} %slice.8), channel_id=1, source_target_pairs={{0,2},{2,4},{4,6},{6,0},{1,3},{3,5},{5,7},{7,1},{8,10},{10,12},{12... | collective-permute-start | bytes 786440 | tf_op jit(solution)/shard_map/ppermute | solution.py:402
  15.8 9.2 %collective-permute-start.3 = (bf16[512,256]{1,0:T(8,128)(2,1)S(1)}, bf16[512,256]{1,0:T(8,128)(2,1)S(1)}, u32[]{:S(2)}, u32[]{:S(2)}) collective-permute-start(bf16[512,256]{1,0:T(8,128)(2,1)S(1)} %slice.9), channel_id=1, source_target_pairs={{0,6},{2,0},{4,2},{6,4},{1,7},{3,1},{5,3},{7,5},{8,14},{10,8},{12,... | collective-permute-start | bytes 786440 | tf_op jit(solution)/shard_map/ppermute | solution.py:402
  17.5 9.1 %collective-permute-start.5 = (bf16[1024,256]{1,0:T(8,128)(2,1)S(1)}, bf16[1024,256]{1,0:T(8,128)(2,1)S(1)}, u32[]{:S(2)}, u32[]{:S(2)}) collective-permute-start(bf16[1024,256]{1,0:T(8,128)(2,1)S(1)} %collective-permute-done.refs_1_), channel_id=1, source_target_pairs={{0,1},{1,0},{2,3},{3,2},{4,5},{5,4},{6,7},{7,6},{8,9},{9,8},{10,11... | collective-permute-start | bytes 1572872 | tf_op jit(solution)/shard_map/ppermute | solution.py:402
  20.8 5.9 %collective-permute-start.8 = (bf16[1024,256]{1,0:T(8,128)(2,1)S(1)}, bf16[1024,256]{1,0:T(8,128)(2,1)S(1)}, u32[]{:S(2)}, u32[]{:S(2)}) collective-permute-start(bf16[1024,256]{1,0:T(8,128)(2,1)S(1)} %collective-permute-done.2.refs_4_), channel_id=1, source_target_pairs={{0,1},{1,0},{2,3},{3,2},{4,5},{5,4},{6,7},{7,6},{8,9},{9,8},{10,11... | collective-permute-start | bytes 1572872 | tf_op jit(solution)/shard_map/ppermute | solution.py:402
  21.2 5.5 %collective-permute-start.6 = (bf16[512,256]{1,0:T(8,128)(2,1)S(1)}, bf16[512,256]{1,0:T(8,128)(2,1)S(1)}, u32[]{:S(2)}, u32[]{:S(2)}) collective-permute-start(bf16[512,256]{1,0:T(8,128)(2,1)S(1)} %collective-permute-done.1.refs_2_), channel_id=1, source_target_pairs={{0,1},{1,0},{2,3},{3,2},{4,5},{5,4},{6,7},{7,6},{8,9},{9,8},{10,11... | collective-permute-start | bytes 786440 | tf_op jit(solution)/shard_map/ppermute | solution.py:402
  25.0 1.6 collective-permute-start.7
  25.1 1.2 copy-start.5
  26.3 1.0 copy-start.7
  192.9 9.9 %all-to-all-start.14 = ((f32[8,8,128]{2,1,0:T(8,128)}), f32[8,8,128]{2,1,0:T(8,128)S(1)}, u32[]{:S(2)}, u32[]{:S(2)}) async-start(f32[8,8,128]{2,1,0:T(8,128)} %get-tuple-element.94), calls=%async_computation.14 | async-start | bytes 65536 | tf_op jit(solution)/shard_map/all_to_all | solution.py:426
  202.8 1.6 copy-start.1
  206.8 15.5 %collective-permute-start.9 = (bf16[4,1024,256]{2,1,0:T(8,128)(2,1)}, bf16[4,1024,256]{2,1,0:T(8,128)(2,1)}, u32[]{:S(2)}, u32[]{:S(2)}) collective-permute-start(bf16[4,1024,256]{2,1,0:T(8,128)(2,1)} %get-tuple-element.97), channel_id=1, source_target_pairs={{0,1},{1,0},{2,3},{3,2},{4,5},{5,4},{6,7},{7,6},{8,9},{9,8},{10,11... | collective-permute-start | bytes 6291464 | tf_op jit(solution)/shard_map/ppermute | solution.py:402
  207.6 14.7 %copy-start.2 = (bf16[512,2048]{1,0:T(8,128)(2,1)S(1)}, bf16[512,2048]{1,0:T(8,128)(2,1)}, u32[]{:S(2)}) copy-start(bf16[512,2048]{1,0:T(8,128)(2,1)} %cent.7) | copy-start | bytes 6291460
  215.4 14.2 %collective-permute-start.13 = (bf16[128,1792]{1,0:T(8,128)(2,1)}, bf16[128,1792]{1,0:T(8,128)(2,1)}, u32[]{:S(2)}, u32[]{:S(2)}) collective-permute-start(bf16[128,1792]{1,0:T(8,128)(2,1)} %get-tuple-element.108), channel_id=1, source_target_pairs={{0,8},{8,16},{16,24},{24,0},{1,9},{9,17},{17,25},{25,1},{2,10},{10... | collective-permute-start | bytes 1376264 | tf_op jit(solution)/shard_map/ppermute | solution.py:402
  216.0 22.9 %collective-permute-start.14 = (bf16[128,1792]{1,0:T(8,128)(2,1)}, bf16[128,1792]{1,0:T(8,128)(2,1)}, u32[]{:S(2)}, u32[]{:S(2)}) collective-permute-start(bf16[128,1792]{1,0:T(8,128)(2,1)} %get-tuple-element.109), channel_id=1, source_target_pairs={{0,16},{8,24},{16,0},{24,8},{1,17},{9,25},{17,1},{25,9},{2,18},{10... | collective-permute-start | bytes 1376264 | tf_op jit(solution)/shard_map/ppermute | solution.py:402
  218.1 21.4 %collective-permute-start.15 = (bf16[128,1792]{1,0:T(8,128)(2,1)}, bf16[128,1792]{1,0:T(8,128)(2,1)}, u32[]{:S(2)}, u32[]{:S(2)}) collective-permute-start(bf16[128,1792]{1,0:T(8,128)(2,1)} %get-tuple-element.110), channel_id=1, source_target_pairs={{0,24},{8,0},{16,8},{24,16},{1,25},{9,1},{17,9},{25,17},{2,26},{10... | collective-permute-start | bytes 1376264 | tf_op jit(solution)/shard_map/ppermute | solution.py:402
  218.9 23.0 %all-to-all-start.16 = ((bf16[8,64,256]{2,1,0:T(8,128)(2,1)}), bf16[8,64,256]{2,1,0:T(8,128)(2,1)S(1)}, u32[]{:S(2)}, u32[]{:S(2)}) async-start(bf16[8,64,256]{2,1,0:T(8,128)(2,1)} %get-tuple-element.111), calls=%async_computation.16 | async-start | bytes 524288 | tf_op jit(solution)/shard_map/all_to_all | solution.py:519
  222.3 17.2 %copy-start.6 = (f32[128,1792]{1,0:T(8,128)S(1)}, f32[128,1792]{1,0:T(8,128)}, u32[]{:S(2)}) copy-start(f32[128,1792]{1,0:T(8,128)} %get-tuple-element.107.first) | copy-start | bytes 2752516
  226.8 37.4 %copy-start.3 = (bf16[1024,512]{1,0:T(8,128)(2,1)S(1)}, bf16[1024,512]{1,0:T(8,128)(2,1)}, u32[]{:S(2)}) copy-start(bf16[1024,512]{1,0:T(8,128)(2,1)} %get-tuple-element.96.turned.turned_hbm) | copy-start | bytes 3145732
  241.0 0.8 copy-start.4
  241.8 31.2 %all-to-all-start.15 = ((bf16[8,16,1792]{2,1,0:T(8,128)(2,1)}), bf16[8,16,1792]{2,1,0:T(8,128)(2,1)}, u32[]{:S(2)}, u32[]{:S(2)}) async-start(bf16[8,16,1792]{2,1,0:T(8,128)(2,1)} %copy-done.4), calls=%async_computation.15 | async-start | bytes 917504 | tf_op jit(solution)/shard_map/all_to_all | solution.py:543
  245.9 14.4 %collective-permute-start.10 = (bf16[1024,256]{1,0:T(8,128)(2,1)}, bf16[1024,256]{1,0:T(8,128)(2,1)S(1)}, u32[]{:S(2)}, u32[]{:S(2)}) collective-permute-start(bf16[1024,256]{1,0:T(8,128)(2,1)} %get-tuple-element.104), channel_id=1, source_target_pairs={{0,2},{2,4},{4,6},{6,0},{1,3},{3,5},{5,7},{7,1},{8,10},{10,12},{12... | collective-permute-start | bytes 1572872 | tf_op jit(solution)/shard_map/ppermute | solution.py:402
  246.3 24.1 %collective-permute-start.11 = (bf16[1024,256]{1,0:T(8,128)(2,1)}, bf16[1024,256]{1,0:T(8,128)(2,1)S(1)}, u32[]{:S(2)}, u32[]{:S(2)}) collective-permute-start(bf16[1024,256]{1,0:T(8,128)(2,1)} %get-tuple-element.105), channel_id=1, source_target_pairs={{0,4},{2,6},{4,0},{6,2},{1,5},{3,7},{5,1},{7,3},{8,12},{10,14},{12... | collective-permute-start | bytes 1572872 | tf_op jit(solution)/shard_map/ppermute | solution.py:402
  248.1 23.9 %collective-permute-start.12 = (bf16[1024,256]{1,0:T(8,128)(2,1)}, bf16[1024,256]{1,0:T(8,128)(2,1)S(1)}, u32[]{:S(2)}, u32[]{:S(2)}) collective-permute-start(bf16[1024,256]{1,0:T(8,128)(2,1)} %get-tuple-element.106), channel_id=1, source_target_pairs={{0,6},{2,0},{4,2},{6,4},{1,7},{3,1},{5,3},{7,5},{8,14},{10,8},{12,... | collective-permute-start | bytes 1572872 | tf_op jit(solution)/shard_map/ppermute | solution.py:402
  249.0 24.1 %collective-permute-start.16 = (bf16[16,256]{1,0:T(8,128)(2,1)S(1)}, bf16[16,256]{1,0:T(8,128)(2,1)S(1)}, u32[]{:S(2)}, u32[]{:S(2)}) collective-permute-start(bf16[16,256]{1,0:T(8,128)(2,1)S(1)} %get-tuple-element.113), channel_id=1, source_target_pairs={{0,8},{8,16},{16,24},{24,0},{1,9},{9,17},{17,25},{25,1},{2,10},{10... | collective-permute-start | bytes 24584 | tf_op jit(solution)/shard_map/ppermute | solution.py:402
  250.1 22.9 %collective-permute-start.17 = (bf16[16,256]{1,0:T(8,128)(2,1)S(1)}, bf16[16,256]{1,0:T(8,128)(2,1)S(1)}, u32[]{:S(2)}, u32[]{:S(2)}) collective-permute-start(bf16[16,256]{1,0:T(8,128)(2,1)S(1)} %get-tuple-element.114), channel_id=1, source_target_pairs={{0,16},{8,24},{16,0},{24,8},{1,17},{9,25},{17,1},{25,9},{2,18},{10... | collective-permute-start | bytes 24584 | tf_op jit(solution)/shard_map/ppermute | solution.py:402
  260.4 12.7 %collective-permute-start.18 = (bf16[16,256]{1,0:T(8,128)(2,1)S(1)}, bf16[16,256]{1,0:T(8,128)(2,1)S(1)}, u32[]{:S(2)}, u32[]{:S(2)}) collective-permute-start(bf16[16,256]{1,0:T(8,128)(2,1)S(1)} %get-tuple-element.115), channel_id=1, source_target_pairs={{0,24},{8,0},{16,8},{24,16},{1,25},{9,1},{17,9},{25,17},{2,26},{10... | collective-permute-start | bytes 24584 | tf_op jit(solution)/shard_map/ppermute | solution.py:402

commit v7 on v6

--- a/solution.py
+++ b/solution.py
@@ -82,12 +82,12 @@
     return lax.rem(lax.axis_index("y") + k, ny) * 2 + core
 
 
-def by_z():
-    return (0,)
+def by_z(n):
+    return (0, n // 2)
 
 
 def by_x(n):
-    return tuple(k for k in range(n) if k not in by_z())
+    return tuple(k for k in range(n) if k not in by_z(n))
 
 
 def span(at, width):
@@ -104,20 +104,15 @@
 
 def k_logits(scale, counts, cent, *refs):
     n = len(counts)
-    pieces, (logits, send, whole, held, sems) = grouped(refs, counts), refs[sum(counts) :]
-    copies = []
+    pieces, (logits, send, whole, held, sem) = grouped(refs, counts), refs[sum(counts) :]
     for k, blocks in enumerate(pieces):
         at = 0
         for block in blocks:
-            size = block.shape[0]
-            copies.append(
-                pltpu.make_async_copy(
-                    block, whole.at[k, pl.ds(at, size), :], sems.at[len(copies)]
-                )
-            )
-            copies[-1].start()
-            held[at : at + size, span(source(n // 2, k), block.shape[1])] = block[...]
-            at += size
+            rows = slice(at, at + block.shape[0])
+            held[rows, span(source(n // 2, k), block.shape[1])] = block[...]
+            at += block.shape[0]
+    copy = pltpu.make_async_copy(held, whole, sem)
+    copy.start()
     logits[...] = scale * lax.dot_general(cent[...], held[...], NT, preferred_element_type=F32)
     count = logits.shape[1] // L
     tops, sums = [], []
@@ -128,8 +123,7 @@
         sums.append(jnp.sum(jnp.exp(tile - top), axis=0, keepdims=True))
     send[:, 0] = jnp.broadcast_to(jnp.concatenate(tops, axis=0)[None], send[:, 0].shape)
     send[:, 1] = jnp.broadcast_to(jnp.concatenate(sums, axis=0)[None], send[:, 1].shape)
-    for c in copies:
-        c.wait()
+    copy.wait()
 
 
 def k_first_col(logits, recv, row_pot, send):
@@ -251,23 +245,29 @@
         base[:, r * L : (r + 1) * L] = tile * inner
 
 
-def k_adjoint(base, first, recv, adjoint, turned):
+def k_adjoint(scale, base, first, recv, cent_hbm, adjoint, turned_hbm, cross, cent, turned, sems):
+    copy = pltpu.make_async_copy(cent_hbm, cent, sems.at[0])
+    copy.start()
     y = -total(recv)
     for r in range(y.shape[0]):
         tile = lanes(base, r) - lanes(first, r).astype(F32) * y[r : r + 1, :]
         tile = tile.astype(BF16)
         adjoint[:, r * L : (r + 1) * L] = tile
         turned[r * L : (r + 1) * L, :] = tile.T
-
-
-def k_cent(scale, n, nx, adjoint, whole_hbm, straight, keep, *refs):
-    sends, (whole, picked, wide, own, narrow, sems, in_sems) = refs[: nx - 1], refs[nx - 1 :]
-    width = whole.shape[2]
-    copies = [
-        pltpu.make_async_copy(whole_hbm.at[p], whole.at[p], in_sems.at[p]) for p in range(n)
-    ]
-    for p in (*by_x(n), *by_z()):
-        copies[p].start()
+    back = pltpu.make_async_copy(turned, turned_hbm, sems.at[1])
+    back.start()
+    copy.wait()
+    ny, _, width = cross.shape
+    for k in range(ny):
+        block = cent[:, span(target(ny, k, True), width)]
+        part = scale * lax.dot_general(turned[...], block, NN, preferred_element_type=F32)
+        cross[k] = part.astype(BF16)
+    back.wait()
+
+
+def k_cent(scale, n, nx, adjoint, whole, straight, keep, *refs):
+    sends, (picked, wide, own, narrow, sems) = refs[: nx - 1], refs[nx - 1 :]
+    width = whole.shape[1] // n
     per = keep.shape[0]
     group = 16
     for k in range(nx):
@@ -282,8 +282,8 @@
         outs[-1].start()
 
     def product(left, p):
-        copies[p].wait()
-        return scale * lax.dot_general(left[...], whole[p], NN, preferred_element_type=F32)
+        right = whole[:, span(source(n // 2, p), width)]
+        return scale * lax.dot_general(left[...], right, NN, preferred_element_type=F32)
 
     for i, p in enumerate(by_x(n)):
         part = product(picked, p)
@@ -292,24 +292,10 @@
             leave(wide.at[i, k - 1], sends[k - 1].at[:, pl.ds(i * width, width)])
         own[i] = part[:per, :]
         leave(own.at[i], keep.at[:, pl.ds(i * width, width)])
-    for i, p in enumerate(by_z()):
+    for i, p in enumerate(by_z(n)):
         part = product(adjoint, p)
         narrow[i] = part.astype(BF16).reshape(narrow.shape[1:])
         leave(narrow.at[i], straight.at[:, :, pl.ds(i * width, width)])
-    for c in outs:
-        c.wait()
-
-
-def k_cross(scale, turned, cent, cross_hbm, turned_hbm, cross, sems):
-    ny, _, width = cross.shape
-    outs = [pltpu.make_async_copy(turned, turned_hbm, sems.at[ny])]
-    outs[0].start()
-    for k in range(ny):
-        block = cent[:, span(target(ny, k, True), width)]
-        part = scale * lax.dot_general(turned[...], block, NN, preferred_element_type=F32)
-        cross[k] = part.astype(BF16)
-        outs.append(pltpu.make_async_copy(cross.at[k], cross_hbm.at[k], sems.at[k]))
-        outs[-1].start()
     for c in outs:
         c.wait()
 
@@ -366,7 +352,7 @@
     second = keep[...]
     for r in refs[:-1]:
         second = second + r[...].astype(F32)
-    for value, pieces in ((first.astype(BF16), by_x(n)), (second.astype(BF16), by_z())):
+    for value, pieces in ((first.astype(BF16), by_x(n)), (second.astype(BF16), by_z(n))):
         for i, p in enumerate(pieces):
             out[:, span(source(n // 2, p), width)] = value[:, i * width : (i + 1) * width]
 
@@ -436,10 +422,10 @@
     work = 2 * rows * cols * depth
     logits, send, whole = call(
         functools.partial(k_logits, scale, counts),
-        [block, row_pair, ((len(counts), rows, width), BF16)],
+        [block, row_pair, ((rows, depth), BF16)],
         centroids, *pieces,
         limit=LARGE, flops=work, hbm_out=(2,),
-        scratch=[pltpu.VMEM((rows, depth), BF16), pltpu.SemaphoreType.DMA((len(pieces),))],
+        scratch=[pltpu.VMEM((rows, depth), BF16), pltpu.SemaphoreType.DMA],
     )
     row_pot, send = call(k_first_col, [a_row, col_pair], logits, over_clus(send))
     col_pot, weights, send = call(
@@ -485,37 +471,34 @@
         flops=work, alias={0: 0, 1: 1},
     )
     per, n = cols // nx, len(counts)
-    adjoint, turned = call(
-        k_adjoint,
-        [((cols, rows), BF16), ((rows, cols), BF16)],
-        base, first, recv,
-    )
-    wide, narrow = len(by_x(n)) * width, len(by_z()) * width
+    adjoint, turned, cross = call(
+        functools.partial(k_adjoint, scale),
+        [((cols, rows), BF16), ((rows, cols), BF16), ((ny, rows, width), BF16)],
+        base, first, recv, pltpu.with_memory_space_constraint(centroids, pltpu.HBM),
+        limit=LARGE, flops=work // 2, hbm_in=(3,), hbm_out=(1,),
+        scratch=[
+            pltpu.VMEM((cols, depth), BF16),
+            pltpu.VMEM((rows, cols), BF16),
+            pltpu.SemaphoreType.DMA((2,)),
+        ],
+    )
+    cross = shift(cross, "core", 1)
+    wide, narrow = len(by_x(n)) * width, len(by_z(n)) * width
     straight, near, *parts = call(
         functools.partial(k_cent, scale, n, nx),
         [((nz, cols // nz, narrow), BF16), ((per, wide), F32)]
         + [((per, wide), BF16)] * (nx - 1),
-        adjoint, pltpu.with_memory_space_constraint(whole, pltpu.HBM),
-        limit=LARGE, flops=work, hbm_in=(1,), hbm_out=range(1 + nx),
+        adjoint, whole,
+        limit=LARGE, flops=work, hbm_out=range(1 + nx),
         scratch=[
-            pltpu.VMEM((n, rows, width), BF16),
             pltpu.VMEM((cols, rows), BF16),
             pltpu.VMEM((len(by_x(n)), nx - 1, per, width), BF16),
             pltpu.VMEM((len(by_x(n)), per, width), F32),
-            pltpu.VMEM((len(by_z()), nz, cols // nz, width), BF16),
+            pltpu.VMEM((len(by_z(n)), nz, cols // nz, width), BF16),
             pltpu.SemaphoreType.DMA((n * nx,)),
-            pltpu.SemaphoreType.DMA((n,)),
         ],
     )
     parts = [shift(p, "x", k + 1) for k, p in enumerate(parts)]
-    cross, turned = call(
-        functools.partial(k_cross, scale),
-        [((ny, rows, width), BF16), ((rows, cols), BF16)],
-        turned, centroids,
-        limit=LARGE, flops=work // 2, hbm_out=(0, 1),
-        scratch=[pltpu.VMEM((ny, rows, width), BF16), pltpu.SemaphoreType.DMA((ny + 1,))],
-    )
-    cross = shift(cross, "core", 1)
     straight = lax.all_to_all(straight, "z", 0, 0, tiled=True)
     moved = call(
         functools.partial(k_pair, scale),
@@ -537,7 +520,7 @@
         functools.partial(k_own, scale),
         [((rows, width), F32)],
         turned, centroids, cross,
-        limit=LARGE, flops=work // 8,
+        limit=60 << 20, flops=work // 8,
     )
     (parts,) = call(k_add, [((nz, per // nz, wide), BF16)], near, *parts, limit=LARGE)
     parts = lax.all_to_all(parts, "z", 0, 0, tiled=True)

time: 280 us -> 280 us (level)
  the two profiles are of different devices: /device:TPU:1 before, /device:TPU:32 now
where the time goes in v7:
time: 280 us; the launch traced here: 279 us
  blocking collectives  156 us (56%)
  waiting for transfers between devices  49.9 us (18%)
  starting transfers between devices  38.4 us (14%)
  Pallas kernels  30.4 us (11%)
  local copies, waits for them, and re-layouts  3.14 us (1%)
    all_to_all x7, blocking collectives, over_prog(): return lax.all_to_all(send, ('z', 'x'), 0, 0, tiled=True)  99.9 us
    all_to_all x7, blocking collectives, over_clus(): return lax.all_to_all(send, ('y', 'core'), 0, 0, tiled=True)  56.3 us
    ppermute x19, waiting for transfers between devices, shift(): return lax.ppermute(value, axis, [(i, (i + step) % n) for i in range(n)])  46.7 us
    pallas_call x25, Pallas kernels, call(): pl.pallas_call(body, out_shape=[pltpu.HBM(s, d) if i in hbm_out else jax....  30.4 us
    ppermute x19, starting transfers between devices, shift(): return lax.ppermute(value, axis, [(i, (i + step) % n) for i in range(n)])  23.3 us
    all_to_all x1, starting transfers between devices, shards(): parts = lax.all_to_all(parts, 'z', 0, 0, tiled=True)  7.23 us
  transfers between devices with their start and end apart: 22, of which 6 were waited for; matrix products, arithmetic and copies ran while one was open for 0% of the time, Pallas kernels for 6%

profile of v7, /device:TPU:32, one launch (start us, length us, event | category | flops | bytes accessed | tf_op | source)
XLA Modules:
  0.0 279.0 jit_solution(4195551455207690223)
XLA Ops:
  0.6 1.7 collective-permute-start
  2.3 1.7 collective-permute-start.2
  4.0 11.9 %collective-permute-done.refs_1_ = bf16[1024,256]{1,0:T(8,128)(2,1)S(1)} collective-permute-done((bf16[1024,256]{1,0:T(8,128)(2,1)}, bf16[1024,256]{1,0:T(8,128)(2,1)S(1)}, u32[]{:S(2)}, u32[]{:S(2)}) %collective-permute-start) | collective-permute-done | bytes 524320 | tf_op jit(solution)/shard_map/ppermute | solution.py:388
  16.3 3.0 %collective-permute-start.3 = (bf16[512,256]{1,0:T(8,128)(2,1)S(1)}, bf16[512,256]{1,0:T(8,128)(2,1)S(1)}, u32[]{:S(2)}, u32[]{:S(2)}) collective-permute-start(bf16[512,256]{1,0:T(8,128)(2,1)S(1)} %slice.9), channel_id=1, source_target_pairs={{0,6},{2,0},{4,2},{6,4},{1,7},{3,1},{5,3},{7,5},{8,14},{10,8},{12,... | collective-permute-start | bytes 786440 | tf_op jit(solution)/shard_map/ppermute | solution.py:388
  19.8 4.6 %collective-permute-done.1.refs_2_ = bf16[512,256]{1,0:T(8,128)(2,1)S(1)} collective-permute-done((bf16[512,256]{1,0:T(8,128)(2,1)S(1)}, bf16[512,256]{1,0:T(8,128)(2,1)S(1)}, u32[]{:S(2)}, u32[]{:S(2)}) %collective-permute-start.1) | collective-permute-done | bytes 262176 | tf_op jit(solution)/shard_map/ppermute | solution.py:388
  24.9 1.2 copy-done.3
  26.6 0.6 copy-done.5
  27.2 3.3 %shard_map.51 = (f32[512,1024]{1,0:T(8,128)S(1)}, f32[8,2,8,128]{3,2,1,0:T(8,128)S(1)}, bf16[1024,2048]{1,0:T(8,128)(2,1)}) custom-call(bf16[512,2048]{1,0:T(8,128)(2,1)S(1)} %copy-done, bf16[1024,256]{1,0:T(8,128)(2,1)S(1)} %copy-done.5, bf16[1024,256]{1,0:T(8,128)(2,1)S(1)} %collective-permute-done.refs_1_, ...), custom_call_target="tpu_custom_call" | custom-call | flops 2147483648 | bytes 6291456 | tf_op jit(solution)/shard_map/pallas_call | solution.py:371
  30.5 9.4 %all_to_all.85.recv = f32[8,2,8,128]{3,2,1,0:T(8,128)S(1)} all-to-all(f32[8,2,8,128]{3,2,1,0:T(8,128)S(1)} %get-tuple-element.60), channel_id=1, replica_groups=mesh['z'=8,'x'=4,'y'=4,'core'=2] {'y','core'}, dimensions={0} | all-to-all | bytes 131072 | tf_op jit(solution)/shard_map/all_to_all | solution.py:412
  39.9 0.6 shard_map.52
  40.4 20.6 %all_to_all.86.recv = f32[32,2,4,128]{3,2,1,0:T(4,128)S(1)} all-to-all(f32[32,2,4,128]{3,2,1,0:T(4,128)S(1)} %get-tuple-element.62), channel_id=1, replica_groups=mesh['z'=8,'x'=4,'y'=4,'core'=2] {'z','x'}, dimensions={0} | all-to-all | bytes 262144 | tf_op jit(solution)/shard_map/all_to_all | solution.py:415
  61.5 7.8 %all_to_all.87.recv = f32[8,8,128]{2,1,0:T(8,128)S(1)} all-to-all(f32[8,8,128]{2,1,0:T(8,128)S(1)} %get-tuple-element.66), channel_id=1, replica_groups=mesh['z'=8,'x'=4,'y'=4,'core'=2] {'y','core'}, dimensions={0} | all-to-all | bytes 65536 | tf_op jit(solution)/shard_map/all_to_all | solution.py:412
  69.6 13.2 %all_to_all.88.recv = f32[32,4,128]{2,1,0:T(4,128)S(1)} all-to-all(f32[32,4,128]{2,1,0:T(4,128)S(1)} %get-tuple-element.68), channel_id=1, replica_groups=mesh['z'=8,'x'=4,'y'=4,'core'=2] {'z','x'}, dimensions={0} | all-to-all | bytes 131072 | tf_op jit(solution)/shard_map/all_to_all | solution.py:415
  83.0 7.8 %all_to_all.89.recv = f32[8,8,128]{2,1,0:T(8,128)S(1)} all-to-all(f32[8,8,128]{2,1,0:T(8,128)S(1)} %get-tuple-element.69), channel_id=1, replica_groups=mesh['z'=8,'x'=4,'y'=4,'core'=2] {'y','core'}, dimensions={0} | all-to-all | bytes 65536 | tf_op jit(solution)/shard_map/all_to_all | solution.py:412
  91.1 13.1 %all_to_all.90.recv = f32[32,4,128]{2,1,0:T(4,128)S(1)} all-to-all(f32[32,4,128]{2,1,0:T(4,128)S(1)} %get-tuple-element.71), channel_id=1, replica_groups=mesh['z'=8,'x'=4,'y'=4,'core'=2] {'z','x'}, dimensions={0} | all-to-all | bytes 131072 | tf_op jit(solution)/shard_map/all_to_all | solution.py:415
  104.4 7.8 %all_to_all.91.recv = f32[8,8,128]{2,1,0:T(8,128)S(1)} all-to-all(f32[8,8,128]{2,1,0:T(8,128)S(1)} %get-tuple-element.72), channel_id=1, replica_groups=mesh['z'=8,'x'=4,'y'=4,'core'=2] {'y','core'}, dimensions={0} | all-to-all | bytes 65536 | tf_op jit(solution)/shard_map/all_to_all | solution.py:412
  112.7 13.7 %all_to_all.92.recv = f32[32,2,4,128]{3,2,1,0:T(4,128)S(1)} all-to-all(f32[32,2,4,128]{3,2,1,0:T(4,128)S(1)} %get-tuple-element.76), channel_id=1, replica_groups=mesh['z'=8,'x'=4,'y'=4,'core'=2] {'z','x'}, dimensions={0} | all-to-all | bytes 262144 | tf_op jit(solution)/shard_map/all_to_all | solution.py:415
  126.9 7.8 %all_to_all.93.recv = f32[8,8,128]{2,1,0:T(8,128)S(1)} all-to-all(f32[8,8,128]{2,1,0:T(8,128)S(1)} %get-tuple-element.78), channel_id=1, replica_groups=mesh['z'=8,'x'=4,'y'=4,'core'=2] {'y','core'}, dimensions={0} | all-to-all | bytes 65536 | tf_op jit(solution)/shard_map/all_to_all | solution.py:412
  135.0 13.1 %all_to_all.94.refs_1_ = f32[32,4,128]{2,1,0:T(4,128)S(1)} all-to-all(f32[32,4,128]{2,1,0:T(4,128)S(1)} %get-tuple-element.79), channel_id=1, replica_groups=mesh['z'=8,'x'=4,'y'=4,'core'=2] {'z','x'}, dimensions={0} | all-to-all | bytes 131072 | tf_op jit(solution)/shard_map/all_to_all | solution.py:415
  148.4 7.8 %all_to_all.95.recv = f32[8,8,128]{2,1,0:T(8,128)S(1)} all-to-all(f32[8,8,128]{2,1,0:T(8,128)S(1)} %get-tuple-element.80), channel_id=1, replica_groups=mesh['z'=8,'x'=4,'y'=4,'core'=2] {'y','core'}, dimensions={0} | all-to-all | bytes 65536 | tf_op jit(solution)/shard_map/all_to_all | solution.py:412
  156.4 13.1 %all_to_all.96.refs_1_ = f32[32,4,128]{2,1,0:T(4,128)S(1)} all-to-all(f32[32,4,128]{2,1,0:T(4,128)S(1)} %get-tuple-element.81), channel_id=1, replica_groups=mesh['z'=8,'x'=4,'y'=4,'core'=2] {'z','x'}, dimensions={0} | all-to-all | bytes 131072 | tf_op jit(solution)/shard_map/all_to_all | solution.py:415
  169.8 7.8 %all_to_all.97.recv = f32[8,8,128]{2,1,0:T(8,128)S(1)} all-to-all(f32[8,8,128]{2,1,0:T(8,128)S(1)} %get-tuple-element.82), channel_id=1, replica_groups=mesh['z'=8,'x'=4,'y'=4,'core'=2] {'y','core'}, dimensions={0} | all-to-all | bytes 65536 | tf_op jit(solution)/shard_map/all_to_all | solution.py:412
  177.8 13.1 %all_to_all.98.refs_0_ = f32[32,4,128]{2,1,0:T(4,128)S(1)} all-to-all(f32[32,4,128]{2,1,0:T(4,128)S(1)} %get-tuple-element.83), channel_id=1, replica_groups=mesh['z'=8,'x'=4,'y'=4,'core'=2] {'z','x'}, dimensions={0} | all-to-all | bytes 131072 | tf_op jit(solution)/shard_map/all_to_all | solution.py:415
  190.9 0.9 shard_map.65
  191.8 3.3 %all-to-all-start.14 = ((f32[8,8,128]{2,1,0:T(8,128)}), f32[8,8,128]{2,1,0:T(8,128)S(1)}, u32[]{:S(2)}, u32[]{:S(2)}) async-start(f32[8,8,128]{2,1,0:T(8,128)} %get-tuple-element.93), calls=%async_computation.14 | async-start | bytes 65536 | tf_op jit(solution)/shard_map/all_to_all | solution.py:412
  195.1 2.2 shard_map.66
  197.3 3.2 %all-to-all-done.14.recv = f32[8,8,128]{2,1,0:T(8,128)S(1)} async-done(((f32[8,8,128]{2,1,0:T(8,128)}), f32[8,8,128]{2,1,0:T(8,128)S(1)}, u32[]{:S(2)}, u32[]{:S(2)}) %all-to-all-start.14) | async-done | bytes 32800 | tf_op jit(solution)/shard_map/all_to_all | solution.py:412
  200.5 4.9 %shard_map.67 = (bf16[512,1024]{1,0:T(8,128)(2,1)S(1)}, bf16[1024,512]{1,0:T(8,128)(2,1)}, bf16[4,1024,256]{2,1,0:T(8,128)(2,1)}) custom-call(f32[512,1024]{1,0:T(8,128)S(1)} %get-tuple-element.91.base, bf16[512,1024]{1,0:T(8,128)(2,1)S(1)} %get-tuple-element.92.first, f32[8,8,128]{2,1,0:T(8,128)S(1)} %all-to-all-done.14.recv, bf16[512,2048]{1,0:T(8,128)(2,1)} %cent.5), custom_call_target="tpu_custom_call" | custom-call | flops 1073741824 | bytes 5275648 | tf_op jit(solution)/shard_map/pallas_call | solution.py:371
  205.5 3.6 %shard_map.69 = (bf16[8,64,512]{2,1,0:T(8,128)(2,1)}, f32[128,1536]{1,0:T(8,128)}, bf16[128,1536]{1,0:T(8,128)(2,1)}, bf16[128,1536]{1,0:T(8,128)(2,1)}, bf16[128,1536]{1,0:T(8,128)(2,1)}) custom-call(bf16[512,1024]{1,0:T(8,128)(2,1)S(1)} %get-tuple-element.96.adjoint, bf16[1024,2048]{1,0:T(8,128)(2,1)S(1)} %copy-done.6), custom_call_target="tpu_custom_call" | custom-call | flops 2147483648 | bytes 5242880 | tf_op jit(solution)/shard_map/pallas_call | solution.py:371
  209.1 4.6 %all-to-all-start.16 = ((bf16[8,64,512]{2,1,0:T(8,128)(2,1)}), bf16[8,64,512]{2,1,0:T(8,128)(2,1)S(1)}, u32[]{:S(2)}, u32[]{:S(2)}) async-start(bf16[8,64,512]{2,1,0:T(8,128)(2,1)} %get-tuple-element.109), calls=%async_computation.16 | async-start | bytes 1048576 | tf_op jit(solution)/shard_map/all_to_all | solution.py:502
  214.2 2.4 collective-permute-start.14
  216.6 1.1 collective-permute-start.15
  217.6 4.5 %shard_map.70 = (bf16[1024,256]{1,0:T(8,128)(2,1)}, bf16[1024,256]{1,0:T(8,128)(2,1)}, bf16[1024,256]{1,0:T(8,128)(2,1)}) custom-call(bf16[1024,512]{1,0:T(8,128)(2,1)} %get-tuple-element.94.turned.turned_hbm, bf16[512,2048]{1,0:T(8,128)(2,1)S(1)} %copy-done.1, bf16[4,1024,256]{2,1,0:T(8,128)(2,1)} %collective-permute-done.9.cross.cross_hbm), custom_call_target="tpu_custom_call" | custom-call | flops 1073741824 | bytes 5242880 | tf_op jit(solution)/shard_map/pallas_call | solution.py:371
  222.1 12.6 %collective-permute-done.13.refs_0_ = bf16[128,1536]{1,0:T(8,128)(2,1)S(1)} collective-permute-done((bf16[128,1536]{1,0:T(8,128)(2,1)}, bf16[128,1536]{1,0:T(8,128)(2,1)S(1)}, u32[]{:S(2)}, u32[]{:S(2)}) %collective-permute-start.13) | collective-permute-done | bytes 393248 | tf_op jit(solution)/shard_map/ppermute | solution.py:388
  234.7 0.6 collective-permute-done.15.refs_2_
  235.3 0.9 shard_map.72
  236.3 7.2 %all-to-all-start.15 = ((bf16[8,16,1536]{2,1,0:T(8,128)(2,1)}), bf16[8,16,1536]{2,1,0:T(8,128)(2,1)S(1)}, u32[]{:S(2)}, u32[]{:S(2)}) async-start(bf16[8,16,1536]{2,1,0:T(8,128)(2,1)} %shard_map.72), calls=%async_computation.15 | async-start | bytes 786432 | tf_op jit(solution)/shard_map/all_to_all | solution.py:526
  243.5 0.6 collective-permute-start.10
  244.1 2.0 collective-permute-start.11
  246.1 1.1 collective-permute-start.12
  247.3 0.8 collective-permute-start.16
  248.1 3.4 %collective-permute-start.17 = (bf16[16,512]{1,0:T(8,128)(2,1)S(1)}, bf16[16,512]{1,0:T(8,128)(2,1)S(1)}, u32[]{:S(2)}, u32[]{:S(2)}) collective-permute-start(bf16[16,512]{1,0:T(8,128)(2,1)S(1)} %get-tuple-element.112), channel_id=1, source_target_pairs={{0,16},{8,24},{16,0},{24,8},{1,17},{9,25},{17,1},{25,9},{2,18},{10... | collective-permute-start | bytes 49160 | tf_op jit(solution)/shard_map/ppermute | solution.py:388
  251.5 17.0 %collective-permute-done.10.refs_0_ = bf16[1024,256]{1,0:T(8,128)(2,1)S(1)} collective-permute-done((bf16[1024,256]{1,0:T(8,128)(2,1)}, bf16[1024,256]{1,0:T(8,128)(2,1)S(1)}, u32[]{:S(2)}, u32[]{:S(2)}) %collective-permute-start.10) | collective-permute-done | bytes 524320 | tf_op jit(solution)/shard_map/ppermute | solution.py:388
  268.5 3.6 %collective-permute-start.18 = (bf16[16,512]{1,0:T(8,128)(2,1)S(1)}, bf16[16,512]{1,0:T(8,128)(2,1)S(1)}, u32[]{:S(2)}, u32[]{:S(2)}) collective-permute-start(bf16[16,512]{1,0:T(8,128)(2,1)S(1)} %get-tuple-element.113), channel_id=1, source_target_pairs={{0,24},{8,0},{16,8},{24,16},{1,25},{9,1},{17,9},{25,17},{2,26},{10... | collective-permute-start | bytes 49160 | tf_op jit(solution)/shard_map/ppermute | solution.py:388
  272.1 4.0 %shard_map.68.first = f32[1024,256]{1,0:T(8,128)} custom-call(bf16[1024,512]{1,0:T(8,128)(2,1)} %get-tuple-element.94.turned.turned_hbm, bf16[512,2048]{1,0:T(8,128)(2,1)} %cent.5, bf16[4,1024,256]{2,1,0:T(8,128)(2,1)} %collective-permute-done.9.cross.cross_hbm), custom_call_target="tpu_custom_call" | custom-call | flops 268435456 | bytes 5242880 | tf_op jit(solution)/shard_map/pallas_call | solution.py:371
  276.0 1.2 copy-done.2
  277.2 1.0 shard_map.71
  278.3 0.7 shard_map.74
  (55 shorter events, 6.1 us)
Async XLA Ops:
  0.6 25.9 %copy-start = (bf16[512,2048]{1,0:T(8,128)(2,1)S(1)}, bf16[512,2048]{1,0:T(8,128)(2,1)}, u32[]{:S(2)}) copy-start(bf16[512,2048]{1,0:T(8,128)(2,1)} %cent.5) | copy-start | bytes 6291460
  0.6 15.2 %collective-permute-start = (bf16[1024,256]{1,0:T(8,128)(2,1)}, bf16[1024,256]{1,0:T(8,128)(2,1)S(1)}, u32[]{:S(2)}, u32[]{:S(2)}) collective-permute-start(bf16[1024,256]{1,0:T(8,128)(2,1)} %refs_0_), channel_id=1, source_target_pairs={{0,2},{2,4},{4,6},{6,0},{1,3},{3,5},{5,7},{7,1},{8,10},{10,12},{12... | collective-permute-start | bytes 1572872 | tf_op jit(solution)/shard_map/ppermute | solution.py:388
  2.3 14.0 %collective-permute-start.2 = (bf16[1024,256]{1,0:T(8,128)(2,1)}, bf16[1024,256]{1,0:T(8,128)(2,1)S(1)}, u32[]{:S(2)}, u32[]{:S(2)}) collective-permute-start(bf16[1024,256]{1,0:T(8,128)(2,1)} %refs_0_), channel_id=1, source_target_pairs={{0,6},{2,0},{4,2},{6,4},{1,7},{3,1},{5,3},{7,5},{8,14},{10,8},{12,... | collective-permute-start | bytes 1572872 | tf_op jit(solution)/shard_map/ppermute | solution.py:388
  4.0 22.6 %collective-permute-start.4 = (bf16[1024,256]{1,0:T(8,128)(2,1)}, bf16[1024,256]{1,0:T(8,128)(2,1)S(1)}, u32[]{:S(2)}, u32[]{:S(2)}) collective-permute-start(bf16[1024,256]{1,0:T(8,128)(2,1)} %refs_0_), channel_id=1, source_target_pairs={{0,1},{1,0},{2,3},{3,2},{4,5},{5,4},{6,7},{7,6},{8,9},{9,8},{10,11... | collective-permute-start | bytes 1572872 | tf_op jit(solution)/shard_map/ppermute | solution.py:388
  15.9 8.5 %collective-permute-start.1 = (bf16[512,256]{1,0:T(8,128)(2,1)S(1)}, bf16[512,256]{1,0:T(8,128)(2,1)S(1)}, u32[]{:S(2)}, u32[]{:S(2)}) collective-permute-start(bf16[512,256]{1,0:T(8,128)(2,1)S(1)} %slice.8), channel_id=1, source_target_pairs={{0,2},{2,4},{4,6},{6,0},{1,3},{3,5},{5,7},{7,1},{8,10},{10,12},{12... | collective-permute-start | bytes 786440 | tf_op jit(solution)/shard_map/ppermute | solution.py:388
  16.3 8.1 %collective-permute-start.3 = (bf16[512,256]{1,0:T(8,128)(2,1)S(1)}, bf16[512,256]{1,0:T(8,128)(2,1)S(1)}, u32[]{:S(2)}, u32[]{:S(2)}) collective-permute-start(bf16[512,256]{1,0:T(8,128)(2,1)S(1)} %slice.9), channel_id=1, source_target_pairs={{0,6},{2,0},{4,2},{6,4},{1,7},{3,1},{5,3},{7,5},{8,14},{10,8},{12,... | collective-permute-start | bytes 786440 | tf_op jit(solution)/shard_map/ppermute | solution.py:388
  19.3 7.2 %collective-permute-start.5 = (bf16[1024,256]{1,0:T(8,128)(2,1)S(1)}, bf16[1024,256]{1,0:T(8,128)(2,1)S(1)}, u32[]{:S(2)}, u32[]{:S(2)}) collective-permute-start(bf16[1024,256]{1,0:T(8,128)(2,1)S(1)} %collective-permute-done.refs_1_), channel_id=1, source_target_pairs={{0,1},{1,0},{2,3},{3,2},{4,5},{5,4},{6,7},{7,6},{8,9},{9,8},{10,11... | collective-permute-start | bytes 1572872 | tf_op jit(solution)/shard_map/ppermute | solution.py:388
  19.3 7.3 %collective-permute-start.8 = (bf16[1024,256]{1,0:T(8,128)(2,1)S(1)}, bf16[1024,256]{1,0:T(8,128)(2,1)S(1)}, u32[]{:S(2)}, u32[]{:S(2)}) collective-permute-start(bf16[1024,256]{1,0:T(8,128)(2,1)S(1)} %collective-permute-done.2.refs_4_), channel_id=1, source_target_pairs={{0,1},{1,0},{2,3},{3,2},{4,5},{5,4},{6,7},{7,6},{8,9},{9,8},{10,11... | collective-permute-start | bytes 1572872 | tf_op jit(solution)/shard_map/ppermute | solution.py:388
  24.4 2.1 collective-permute-start.6
  24.4 2.1 collective-permute-start.7
  24.9 1.2 copy-start.3
  26.2 1.0 copy-start.5
  191.8 8.7 %all-to-all-start.14 = ((f32[8,8,128]{2,1,0:T(8,128)}), f32[8,8,128]{2,1,0:T(8,128)S(1)}, u32[]{:S(2)}, u32[]{:S(2)}) async-start(f32[8,8,128]{2,1,0:T(8,128)} %get-tuple-element.93), calls=%async_computation.14 | async-start | bytes 65536 | tf_op jit(solution)/shard_map/all_to_all | solution.py:412
  200.5 5.0 %copy-start.6 = (bf16[1024,2048]{1,0:T(8,128)(2,1)S(1)}, bf16[1024,2048]{1,0:T(8,128)(2,1)}, u32[]{:S(2)}) copy-start(bf16[1024,2048]{1,0:T(8,128)(2,1)} %get-tuple-element.97.whole) | copy-start | bytes 12582916
  205.4 12.3 %collective-permute-start.9 = (bf16[4,1024,256]{2,1,0:T(8,128)(2,1)}, bf16[4,1024,256]{2,1,0:T(8,128)(2,1)}, u32[]{:S(2)}, u32[]{:S(2)}) collective-permute-start(bf16[4,1024,256]{2,1,0:T(8,128)(2,1)} %get-tuple-element.95), channel_id=1, source_target_pairs={{0,1},{1,0},{2,3},{3,2},{4,5},{5,4},{6,7},{7,6},{8,9},{9,8},{10,11... | collective-permute-start | bytes 6291464 | tf_op jit(solution)/shard_map/ppermute | solution.py:388
  205.5 12.1 %copy-start.1 = (bf16[512,2048]{1,0:T(8,128)(2,1)S(1)}, bf16[512,2048]{1,0:T(8,128)(2,1)}, u32[]{:S(2)}) copy-start(bf16[512,2048]{1,0:T(8,128)(2,1)} %cent.5) | copy-start | bytes 6291460
  209.1 27.2 %all-to-all-start.16 = ((bf16[8,64,512]{2,1,0:T(8,128)(2,1)}), bf16[8,64,512]{2,1,0:T(8,128)(2,1)S(1)}, u32[]{:S(2)}, u32[]{:S(2)}) async-start(bf16[8,64,512]{2,1,0:T(8,128)(2,1)} %get-tuple-element.109), calls=%async_computation.16 | async-start | bytes 1048576 | tf_op jit(solution)/shard_map/all_to_all | solution.py:502
  213.7 21.0 %collective-permute-start.13 = (bf16[128,1536]{1,0:T(8,128)(2,1)}, bf16[128,1536]{1,0:T(8,128)(2,1)S(1)}, u32[]{:S(2)}, u32[]{:S(2)}) collective-permute-start(bf16[128,1536]{1,0:T(8,128)(2,1)} %get-tuple-element.106), channel_id=1, source_target_pairs={{0,8},{8,16},{16,24},{24,0},{1,9},{9,17},{17,25},{25,1},{2,10},{10... | collective-permute-start | bytes 1179656 | tf_op jit(solution)/shard_map/ppermute | solution.py:388
  214.2 20.5 %collective-permute-start.14 = (bf16[128,1536]{1,0:T(8,128)(2,1)}, bf16[128,1536]{1,0:T(8,128)(2,1)S(1)}, u32[]{:S(2)}, u32[]{:S(2)}) collective-permute-start(bf16[128,1536]{1,0:T(8,128)(2,1)} %get-tuple-element.107), channel_id=1, source_target_pairs={{0,16},{8,24},{16,0},{24,8},{1,17},{9,25},{17,1},{25,9},{2,18},{10... | collective-permute-start | bytes 1179656 | tf_op jit(solution)/shard_map/ppermute | solution.py:388
  216.6 18.8 %collective-permute-start.15 = (bf16[128,1536]{1,0:T(8,128)(2,1)}, bf16[128,1536]{1,0:T(8,128)(2,1)S(1)}, u32[]{:S(2)}, u32[]{:S(2)}) collective-permute-start(bf16[128,1536]{1,0:T(8,128)(2,1)} %get-tuple-element.108), channel_id=1, source_target_pairs={{0,24},{8,0},{16,8},{24,16},{1,25},{9,1},{17,9},{25,17},{2,26},{10... | collective-permute-start | bytes 1179656 | tf_op jit(solution)/shard_map/ppermute | solution.py:388
  217.6 17.7 %copy-start.4 = (f32[128,1536]{1,0:T(8,128)S(1)}, f32[128,1536]{1,0:T(8,128)}, u32[]{:S(2)}) copy-start(f32[128,1536]{1,0:T(8,128)} %get-tuple-element.105.first) | copy-start | bytes 2359300
  222.1 21.9 %copy-start.8 = (bf16[1024,256]{1,0:T(8,128)(2,1)S(1)}, bf16[1024,256]{1,0:T(8,128)(2,1)}, u32[]{:S(2)}) copy-start(bf16[1024,256]{1,0:T(8,128)(2,1)} %get-tuple-element.103) | copy-start | bytes 1572868
  222.1 24.0 %copy-start.7 = (bf16[1024,256]{1,0:T(8,128)(2,1)S(1)}, bf16[1024,256]{1,0:T(8,128)(2,1)}, u32[]{:S(2)}) copy-start(bf16[1024,256]{1,0:T(8,128)(2,1)} %get-tuple-element.104) | copy-start | bytes 1572868
  236.3 42.0 %all-to-all-start.15 = ((bf16[8,16,1536]{2,1,0:T(8,128)(2,1)}), bf16[8,16,1536]{2,1,0:T(8,128)(2,1)S(1)}, u32[]{:S(2)}, u32[]{:S(2)}) async-start(bf16[8,16,1536]{2,1,0:T(8,128)(2,1)} %shard_map.72), calls=%async_computation.15 | async-start | bytes 786432 | tf_op jit(solution)/shard_map/all_to_all | solution.py:526
  243.5 25.0 %collective-permute-start.10 = (bf16[1024,256]{1,0:T(8,128)(2,1)}, bf16[1024,256]{1,0:T(8,128)(2,1)S(1)}, u32[]{:S(2)}, u32[]{:S(2)}) collective-permute-start(bf16[1024,256]{1,0:T(8,128)(2,1)} %get-tuple-element.102), channel_id=1, source_target_pairs={{0,2},{2,4},{4,6},{6,0},{1,3},{3,5},{5,7},{7,1},{8,10},{10,12},{12... | collective-permute-start | bytes 1572872 | tf_op jit(solution)/shard_map/ppermute | solution.py:388
  244.1 31.9 %collective-permute-start.11 = (bf16[1024,256]{1,0:T(8,128)(2,1)S(1)}, bf16[1024,256]{1,0:T(8,128)(2,1)S(1)}, u32[]{:S(2)}, u32[]{:S(2)}) collective-permute-start(bf16[1024,256]{1,0:T(8,128)(2,1)S(1)} %copy-done.8), channel_id=1, source_target_pairs={{0,4},{2,6},{4,0},{6,2},{1,5},{3,7},{5,1},{7,3},{8,12},{10,14},{12... | collective-permute-start | bytes 1572872 | tf_op jit(solution)/shard_map/ppermute | solution.py:388
  246.1 29.9 %collective-permute-start.12 = (bf16[1024,256]{1,0:T(8,128)(2,1)S(1)}, bf16[1024,256]{1,0:T(8,128)(2,1)S(1)}, u32[]{:S(2)}, u32[]{:S(2)}) collective-permute-start(bf16[1024,256]{1,0:T(8,128)(2,1)S(1)} %copy-done.7), channel_id=1, source_target_pairs={{0,6},{2,0},{4,2},{6,4},{1,7},{3,1},{5,3},{7,5},{8,14},{10,8},{12,... | collective-permute-start | bytes 1572872 | tf_op jit(solution)/shard_map/ppermute | solution.py:388
  247.3 31.0 %collective-permute-start.16 = (bf16[16,512]{1,0:T(8,128)(2,1)S(1)}, bf16[16,512]{1,0:T(8,128)(2,1)S(1)}, u32[]{:S(2)}, u32[]{:S(2)}) collective-permute-start(bf16[16,512]{1,0:T(8,128)(2,1)S(1)} %get-tuple-element.111), channel_id=1, source_target_pairs={{0,8},{8,16},{16,24},{24,0},{1,9},{9,17},{17,25},{25,1},{2,10},{10... | collective-permute-start | bytes 49160 | tf_op jit(solution)/shard_map/ppermute | solution.py:388
  248.1 30.2 %collective-permute-start.17 = (bf16[16,512]{1,0:T(8,128)(2,1)S(1)}, bf16[16,512]{1,0:T(8,128)(2,1)S(1)}, u32[]{:S(2)}, u32[]{:S(2)}) collective-permute-start(bf16[16,512]{1,0:T(8,128)(2,1)S(1)} %get-tuple-element.112), channel_id=1, source_target_pairs={{0,16},{8,24},{16,0},{24,8},{1,17},{9,25},{17,1},{25,9},{2,18},{10... | collective-permute-start | bytes 49160 | tf_op jit(solution)/shard_map/ppermute | solution.py:388
  268.5 9.8 %collective-permute-start.18 = (bf16[16,512]{1,0:T(8,128)(2,1)S(1)}, bf16[16,512]{1,0:T(8,128)(2,1)S(1)}, u32[]{:S(2)}, u32[]{:S(2)}) collective-permute-start(bf16[16,512]{1,0:T(8,128)(2,1)S(1)} %get-tuple-element.113), channel_id=1, source_target_pairs={{0,24},{8,0},{16,8},{24,16},{1,25},{9,1},{17,9},{25,17},{2,26},{10... | collective-permute-start | bytes 49160 | tf_op jit(solution)/shard_map/ppermute | solution.py:388
  276.0 1.2 copy-start.2
